TPU v7x, 32 devices: a whole 2x2x4 slice. The times are simulated.
32 devices in a mesh: groups: 2 (over x), row: 16 (over z, y, core).
Axes of the slice: x: 2, y: 2, z: 4, core: 2. Of those that a mesh axis runs over, the one named last changes fastest.
Arguments:
- features: bfloat16 [16384, 128], P(('groups', 'row')), parts along dimension 0, may hold values from -6 to 6
- weight: bfloat16 [128, 256], replicated, may hold values from -0.5 to 0.5
- block_cols: int32 [128, 16], P(('groups', 'row')), parts along dimension 0, may hold values from 0 to 63, as said below
- block_counts: int32 [128], P(('groups', 'row')), parts along dimension 0, may hold values from 1 to 16, as said below
- block_vals: bfloat16 [128, 16, 128, 128], P(('groups', 'row')), parts along dimension 0, may hold values from 0 to 0.03125, as said below
- out_grad: bfloat16 [16384, 256], P(('groups', 'row')), parts along dimension 0, may hold values from -6 to 6
Outputs:
- hidden_out: bfloat16 [16384, 256], P(('groups', 'row')), parts along dimension 0
- feat_grad: bfloat16 [16384, 128], P(('groups', 'row')), parts along dimension 0
- weight_grad: float32 [256, 256], P('groups'), parts along dimension 0
There are 2 independent parts, one for each index of `groups`. A program takes and returns all parts, laid end to end along the dimension named above; an argument that names none is the same for every part. Nothing has to cross between parts.
Inputs may be any that keep to these rules, and one draw needn't show every extreme that they name: `block_cols`: within a row panel the first block_counts entries are distinct block columns; entries past the count are valid indices but are not part of A. `block_counts`: some panel holds exactly 16 blocks. `block_vals`: A is symmetric: where panel p stores a block at block column q, panel q stores the transposed block at block column p.
All inputs are finite; a program needn't handle non-finite values.
Results may differ from a plain program's by a relative error of at most 0.005.
Values may be sent and summed in bfloat16 or wider, within the bound.
No kernel may reach another device: no remote copies, remote signals or barrier semaphores. Data moves between devices by JAX's collectives and lax.ppermute only.
A program may use at most 64 MiB of HBM per device.

v0:
```python
import jax
import jax.numpy as jnp
from jax import lax
from jax.sharding import PartitionSpec as P


def body(features, weight, block_cols, block_counts, block_vals, out_grad):
    panel_total, slot_count, block_side, _ = block_vals.shape
    node_rows = features.shape[0]
    in_width = features.shape[1]
    in_use = jnp.arange(slot_count, dtype=jnp.int32)[None, :] < block_counts[:, None]
    blocks = jnp.where(in_use[:, :, None, None], block_vals, jnp.zeros_like(block_vals))
    whole = lax.all_gather(features, "row", axis=0, tiled=True)
    col_blocks = whole.shape[0] // block_side
    picked = whole.reshape(col_blocks, block_side, in_width)[block_cols]
    aggregated = jnp.einsum(
        "pbij,pbjf->pif", blocks, picked, preferred_element_type=jnp.float32
    ).reshape(node_rows, in_width)
    weight_wide = weight.astype(jnp.float32)
    preact = jnp.dot(aggregated, weight_wide, precision=lax.Precision.HIGHEST)
    hidden, pullback = jax.vjp(jax.nn.gelu, preact)
    pre_grad = pullback(out_grad.astype(jnp.float32))[0]
    partial_value = jnp.dot(aggregated.T, pre_grad, precision=lax.Precision.HIGHEST)
    edge_grad = jnp.dot(pre_grad, weight_wide.T, precision=lax.Precision.HIGHEST).astype(
        jnp.bfloat16
    )
    contrib = jnp.einsum(
        "pbij,pif->pbjf",
        blocks,
        edge_grad.reshape(panel_total, block_side, in_width),
        preferred_element_type=jnp.float32,
    )
    contrib = contrib.reshape(panel_total * slot_count, block_side, in_width)
    flat_cols = block_cols.reshape(-1)
    summed = jax.ops.segment_sum(
        contrib, flat_cols, num_segments=lax.axis_size("row") * node_rows // block_side
    )
    feat_term = lax.psum_scatter(
        summed.reshape(lax.axis_size("row") * node_rows, in_width),
        "row",
        scatter_dimension=0,
        tiled=True,
    )
    feat_grad = feat_term.astype(jnp.bfloat16)
    weight_grad = lax.psum(partial_value, "row")
    return (hidden.astype(jnp.bfloat16), feat_grad, weight_grad)


def solution(mesh):
    in_specs = (
        P(("groups", "row"), None),
        P(),
        P(("groups", "row"), None),
        P(("groups", "row")),
        P(("groups", "row"), None, None, None),
        P(("groups", "row"), None),
    )
    out_specs = (P(("groups", "row"), None), P(("groups", "row"), None), P("groups", None))
    return jax.shard_map(body, mesh=mesh, in_specs=in_specs, out_specs=out_specs, check_vma=False)
```

profile of v0, /device:TPU:0, one launch (start us, length us, event | category | flops | bytes accessed | tf_op | source)
XLA Modules:
  0.0 251.5 jit_solution(14611709308456728059)
XLA Ops:
  7.2 0.0 copy-start
  7.2 0.0 all-gather.2.cloned.1.call-start
  7.2 0.7 all-gather.2.cloned.1.call-update
  7.9 0.0 reduce-scatter.2.cloned.1.call-start
  8.0 0.8 reshape.57
  8.7 0.7 compare_select_fusion
  9.4 0.1 reshape.49
  9.5 0.7 iota_compare_fusion
  10.2 44.1 %all-gather.2.cloned.1.call-done = bf16[8192,128]{1,0:T(8,128)(2,1)} async-done(((bf16[512,128]{1,0:T(8,128)(2,1)}), bf16[8192,128]{1,0:T(8,128)(2,1)}) %all-gather.2.cloned.1.call-update) | async-done | bytes 2097168 | tf_op jit(solution)/shard_map/all_gather | solution.py:13
  54.3 0.0 copy-start.1
  54.3 3.9 %gather_fusion = bf16[64,128,128]{2,1,0:T(8,128)(2,1)} fusion(bf16[64,128,128]{2,1,0:T(8,128)(2,1)} %bitcast.23, s32[1024]{0:T(1024)S(1)} %pad_clamp_fusion), kind=kCustom, calls=%fused_computation | custom fusion | bytes 4194560 | tf_op jit(solution)/shard_map/gather | solution.py:15
  58.2 0.0 copy-done.1
  58.2 0.0 copy-start.2
  58.2 2.4 fusion.1
  60.6 0.0 copy-done
  60.6 0.0 copy-done.2
  60.6 1.4 fusion.5
  62.0 0.4 convolution_convert_fusion
  62.3 2.9 %fusion = f32[4,16,128,128]{3,2,1,0:T(8,128)} fusion(bf16[4,128,128,1]{2,1,3,0:T(8,128)(2,1)S(1)} %bitcast.25, bf16[4,16,128,128]{3,2,1,0:T(8,128)(2,1)S(1)} %copy-done.1, pred[4,16]{1,0:T(4,128)(4,1)S(1)} %iota_compare_fusion), kind=kOutput, calls=%fused_computation.3 | convolution fusion | flops 269484032 | bytes 6422592 | tf_op jit(solution)/shard_map/pbij,pif->pbjf/dot_general | solution.py:27
  65.3 2.5 broadcast_in_dim.23
  67.7 13.8 %scatter_fusion = f32[64,128,128]{2,1,0:T(8,128)} fusion(f32[64,128,128]{2,1,0:T(8,128)} %broadcast_in_dim.23, s32[64]{0:T(128)S(1)} %reshape.57, f32[64,128,128]{2,1,0:T(8,128)} %bitcast.22), kind=kCustom, calls=%fused_computation.1 | custom fusion | flops 1048576 | bytes 12583168 | tf_op jit(solution)/shard_map/scatter-add | solution.py:35
  81.5 0.0 reduce-scatter.2.cloned.1.call-update
  81.5 0.0 all-reduce.2.cloned.1.call-start
  81.6 1.3 fusion.15
  82.8 0.0 all-reduce.2.cloned.1.call-update
  82.9 70.2 %reduce-scatter.2.cloned.1.call-done = f32[512,128]{1,0:T(8,128)} async-done(((f32[8192,128]{1,0:T(8,128)}), f32[512,128]{1,0:T(8,128)}) %reduce-scatter.2.cloned.1.call-update) | async-done | bytes 262160 | tf_op jit(solution)/shard_map/reduce_scatter | solution.py:38
  153.1 1.6 convert_element_type.16
  154.7 88.7 %all-reduce.2.cloned.1.call-done = f32[128,256]{1,0:T(8,128)} async-done(((f32[128,256]{1,0:T(8,128)}), f32[128,256]{1,0:T(8,128)}) %all-reduce.2.cloned.1.call-update) | async-done | bytes 131088 | tf_op jit(solution)/shard_map/psum | solution.py:45
  243.4 1.6 copy.15
  (1 shorter events, 0.0 us)
Async XLA Ops:
  7.2 53.4 %copy-start = (bf16[128,256]{1,0:T(8,128)(2,1)S(1)}, bf16[128,256]{1,0:T(8,128)(2,1)}, u32[]{:S(2)}) copy-start(bf16[128,256]{1,0:T(8,128)(2,1)} %param.7) | copy-start | bytes 196612
  7.2 47.1 %all-gather.2.cloned.1.call-start = ((), (), s32[]{:S(2)}) async-start(), calls=%async_computation.1 | async-start | bytes 2228224 | tf_op jit(solution)/shard_map/all_gather | solution.py:13
  7.9 145.1 %reduce-scatter.2.cloned.1.call-start = ((), (), s32[]{:S(2)}) async-start(), calls=%async_computation.2 | async-start | bytes 4456448 | tf_op jit(solution)/shard_map/reduce_scatter | solution.py:38
  54.3 3.9 %copy-start.1 = (bf16[4,16,128,128]{3,2,1,0:T(8,128)(2,1)S(1)}, bf16[4,16,128,128]{3,2,1,0:T(8,128)(2,1)}, u32[]{:S(2)}) copy-start(bf16[4,16,128,128]{3,2,1,0:T(8,128)(2,1)} %param.10) | copy-start | bytes 6291460
  58.2 2.4 copy-start.2
  81.5 161.9 %all-reduce.2.cloned.1.call-start = ((), (), s32[]{:S(2)}) async-start(), calls=%async_computation.3 | async-start | bytes 262144 | tf_op jit(solution)/shard_map/psum | solution.py:45
Sparse Core Ops, SparseCore 0:
  10.2 44.0 all-gather.1
  81.6 71.3 reduce-scatter.1
  157.5 85.8 all-reduce.1
where the time goes:
time: 253 us; the launch traced here: 252 us
  waiting for transfers between devices  204 us (81%)
  other arithmetic  16.8 us (7%)
  between operations  13.8 us (5%)
  local copies, waits for them, and re-layouts  8.74 us (3%)
  matrix products  8.35 us (3%)
    psum x1, waiting for transfers between devices, body(): weight_grad = lax.psum(partial_value, 'row')  88.7 us
    reduce_scatter x1, waiting for transfers between devices, body(): lax.psum_scatter(summed.reshape(lax.axis_size('row') * node_rows, in_widt...  70.2 us
    all_gather x1, waiting for transfers between devices, body(): whole = lax.all_gather(features, 'row', axis=0, tiled=True)  44.1 us
    scatter-add x1, other arithmetic, body(): jax.ops.segment_sum(contrib, flat_cols, num_segments=lax.axis_size('row')...  13.8 us
  transfers between devices with their start and end apart: 3, of which 3 were waited for; matrix products, arithmetic and copies ran while one was open for 2% of the time, Pallas kernels for 0%

commit v1 on v0

v1 whole, which is shorter than its diff:
```python
import jax
import jax.numpy as jnp
from jax import lax
from jax.experimental import pallas as pl
from jax.experimental.pallas import tpu as pltpu
from jax.sharding import PartitionSpec as P

GROUP = 4
GELU_C = 0.7978845608028654
GELU_A = 0.044715


def in_vmem(x):
    return pltpu.with_memory_space_constraint(x, pltpu.VMEM)


def exchange(x, bit, size):
    return lax.ppermute(x, "row", [(i, i ^ bit) for i in range(size)])


def gather_rows(x, size):
    if size != 16:
        return [(None, lax.all_gather(x, "row", axis=0, tiled=True))]
    held = {0: x}
    held[8] = exchange(x, 8, size)
    held[4] = exchange(x, 4, size)
    held[12] = exchange(held[8], 4, size)
    for mask in (0, 4, 8, 12):
        held[mask ^ 2] = exchange(held[mask], 2, size)
    for mask in (0, 2, 4, 6, 8, 10, 12, 14):
        held[mask ^ 1] = exchange(held[mask], 1, size)
    return sorted(held.items())


def row_sum(keep, send, core, size):
    total = keep + exchange(send, 1, size)
    bit = size // 2
    while bit > 1:
        total = total + exchange(total, bit, size)
        bit //= 2
    other = exchange(total, 1, size)
    return jnp.where(
        core == 0, jnp.concatenate([total, other], 0), jnp.concatenate([other, total], 0)
    )


def collect(me, masks, pieces, nodes):
    if nodes is None:
        return pieces[0]
    rows = pieces[0].shape[0]
    for mask, piece in zip(masks, pieces):
        blocks = piece.shape[0]
        start = (me ^ mask) * blocks
        for i in range(blocks):
            nodes[start + i] = piece[i]
    return nodes


def panel_product(cols, counts, vals, nodes, panel):
    used = counts[panel]
    side = vals.shape[2]

    def product(b):
        return jnp.dot(
            vals[panel, b], nodes[cols[panel, b]], preferred_element_type=jnp.float32
        )

    def many(step, total):
        for j in range(GROUP):
            total = total + product(step * GROUP + j)
        return total

    full = used // GROUP
    total = lax.fori_loop(0, full, many, jnp.zeros((side, nodes.shape[2]), jnp.float32))
    return lax.fori_loop(full * GROUP, used, lambda b, t: t + product(b), total)


def split(x):
    high = x.astype(jnp.bfloat16)
    return high, (x - high.astype(jnp.float32)).astype(jnp.bfloat16)


def dot(a, b, dims):
    return lax.dot_general(a, b, (dims, ((), ())), preferred_element_type=jnp.float32)


def forward_kernel(masks, *refs):
    n = len(masks)
    me, cols, counts = refs[:3]
    pieces = refs[3 : 3 + n]
    vals, weight, out_grad = refs[3 + n : 6 + n]
    hidden, edge, keep, send = refs[6 + n : 10 + n]
    wsum = refs[10 + n]
    nodes = collect(me[0], masks, pieces, refs[11 + n] if n > 1 else None)
    panels, _, side, _ = vals.shape
    half = keep.shape[0]
    w = weight[...]
    for panel in range(panels):
        rows = pl.ds(panel * side, side)
        agg = panel_product(cols, counts, vals, nodes, panel)
        agg_h, agg_l = split(agg)
        z = dot(agg_h, w, ((1,), (0,))) + dot(agg_l, w, ((1,), (0,)))
        zz = z * z
        t = jnp.tanh(z * (GELU_C + (GELU_C * GELU_A) * zz))
        half_up = 0.5 + 0.5 * t
        hidden[rows, :] = (z * half_up).astype(jnp.bfloat16)
        slope = half_up + (0.5 * z) * (1.0 - t * t) * (GELU_C + (3.0 * GELU_C * GELU_A) * zz)
        dz = out_grad[rows, :].astype(jnp.float32) * slope
        dz_h, dz_l = split(dz)
        edge[panel] = (dot(dz_h, w, ((1,), (1,))) + dot(dz_l, w, ((1,), (1,)))).astype(jnp.bfloat16)
        part = (
            dot(agg_h, dz_h, ((0,), (0,)))
            + dot(agg_l, dz_h, ((0,), (0,)))
            + dot(agg_h, dz_l, ((0,), (0,)))
        )
        wsum[...] = part if panel == 0 else wsum[...] + part
    core = me[0] % 2
    keep[...] = wsum[pl.ds(pl.multiple_of(core * half, half), half), :]
    send[...] = wsum[pl.ds(pl.multiple_of((1 - core) * half, half), half), :]


def backward_kernel(masks, *refs):
    n = len(masks)
    me, cols, counts = refs[:3]
    pieces = refs[3 : 3 + n]
    vals = refs[3 + n]
    feat = refs[4 + n]
    nodes = collect(me[0], masks, pieces, refs[5 + n] if n > 1 else None)
    panels, _, side, _ = vals.shape
    for panel in range(panels):
        rows = pl.ds(panel * side, side)
        feat[rows, :] = panel_product(cols, counts, vals, nodes, panel).astype(jnp.bfloat16)


PARAMS = pltpu.CompilerParams(vmem_limit_bytes=12 * 2**20)
SMEM = pl.BlockSpec(memory_space=pltpu.SMEM)
VMEM = pl.BlockSpec(memory_space=pltpu.VMEM)


def body(features, weight, block_cols, block_counts, block_vals, out_grad):
    size = lax.axis_size("row")
    panels, _, side, _ = block_vals.shape
    rows, width = features.shape
    hidden_width = weight.shape[1]
    node_blocks = size * panels
    me = lax.axis_index("row").astype(jnp.int32).reshape(1)
    vals = in_vmem(block_vals)

    def gathered(x):
        held = gather_rows(x.reshape(panels, side, width), size)
        scratch = []
        if len(held) > 1:
            scratch = [pltpu.VMEM((node_blocks, side, width), jnp.bfloat16)]
        return tuple(m for m, _ in held), [in_vmem(a) for _, a in held], scratch

    masks, pieces, scratch = gathered(features)
    hidden, edge, keep, send = pl.pallas_call(
        lambda *refs: forward_kernel(masks, *refs),
        name="forward",
        compiler_params=PARAMS,
        out_shape=(
            jax.ShapeDtypeStruct((rows, hidden_width), jnp.bfloat16),
            jax.ShapeDtypeStruct((panels, side, width), jnp.bfloat16),
            jax.ShapeDtypeStruct((width // 2, hidden_width), jnp.float32),
            jax.ShapeDtypeStruct((width // 2, hidden_width), jnp.float32),
        ),
        in_specs=[SMEM] * 3 + [VMEM] * (len(pieces) + 3),
        out_specs=(VMEM,) * 4,
        scratch_shapes=[pltpu.VMEM((width, hidden_width), jnp.float32)] + scratch,
    )(me, block_cols, block_counts, *pieces, vals, in_vmem(weight), in_vmem(out_grad))

    masks, pieces, scratch = gathered(edge)
    feat_grad = pl.pallas_call(
        lambda *refs: backward_kernel(masks, *refs),
        name="backward",
        compiler_params=PARAMS,
        out_shape=jax.ShapeDtypeStruct((rows, width), jnp.bfloat16),
        in_specs=[SMEM] * 3 + [VMEM] * (len(pieces) + 1),
        out_specs=VMEM,
        scratch_shapes=scratch,
    )(me, block_cols, block_counts, *pieces, vals)
    weight_grad = row_sum(keep, send, me[0] % 2, size)
    return hidden, feat_grad, weight_grad


def solution(mesh):
    in_specs = (
        P(("groups", "row"), None),
        P(),
        P(("groups", "row"), None),
        P(("groups", "row")),
        P(("groups", "row"), None, None, None),
        P(("groups", "row"), None),
    )
    out_specs = (P(("groups", "row"), None), P(("groups", "row"), None), P("groups", None))
    return jax.shard_map(body, mesh=mesh, in_specs=in_specs, out_specs=out_specs, check_vma=False)
```

time: 253 us -> 76.1 us (0.30)
  waiting for transfers between devices: 204 us -> 24.8 us
  starting transfers between devices: 0.12 us -> 27.2 us
  other arithmetic: 16.8 us -> 1.65 us
  between operations: 13.8 us -> 0.8 us
  matrix products: 8.35 us -> 0 us
  Pallas kernels: 0 us -> 7.62 us
  local copies, waits for them, and re-layouts: 8.74 us -> 13.4 us
    psum x1 -> x0, waiting for transfers between devices: 88.7 us -> none  [body(): weight_grad = lax.psum(partial_value, 'row')]
    reduce_scatter x1 -> x0, waiting for transfers between devices: 70.2 us -> none  [body(): lax.psum_scatter(summed.reshape(lax.axis_size('row') * node_rows, in_widt...]
    all_gather x1 -> x0, waiting for transfers between devices: 44.1 us -> none  [body(): whole = lax.all_gather(features, 'row', axis=0, tiled=True)]
    ppermute x0 -> x35, starting transfers between devices: none -> 27.2 us  [exchange(): return lax.ppermute(x, 'row', [(i, i ^ bit) for i in range(size)])]
    ppermute x0 -> x35, waiting for transfers between devices: none -> 24.8 us  [exchange(): return lax.ppermute(x, 'row', [(i, i ^ bit) for i in range(size)])]
    scatter-add x1 -> x0, other arithmetic: 13.8 us -> none  [body(): jax.ops.segment_sum(contrib, flat_cols, num_segments=lax.axis_size('row')...]
    unnamed x7 -> x42, local copies, waits for them, and re-layouts: 1.58 us -> 13.4 us
    dot_general x5 -> x0, matrix products: 8.35 us -> none  [the longest x1 2.93 us: body(): jnp.einsum('pbij,pif->pbjf', blocks, edge_grad.reshape(panel_total, block...]
  transfers between devices with their start and end apart: 3 -> 35, of which waited for: 3 -> 10; matrix products, arithmetic and copies ran while one was open for 2% -> 2% of each run, Pallas kernels for 0% -> 0%
where the time goes in v1:
time: 76.1 us; the launch traced here: 75.4 us
  starting transfers between devices  27.2 us (36%)
  waiting for transfers between devices  24.8 us (33%)
  local copies, waits for them, and re-layouts  13.4 us (18%)
  Pallas kernels  7.62 us (10%)
  other arithmetic  1.65 us (2%)
  between operations  0.8 us (1%)
    ppermute x35, starting transfers between devices, exchange(): return lax.ppermute(x, 'row', [(i, i ^ bit) for i in range(size)])  27.2 us
    ppermute x35, waiting for transfers between devices, exchange(): return lax.ppermute(x, 'row', [(i, i ^ bit) for i in range(size)])  24.8 us
    unnamed x42, local copies, waits for them, and re-layouts  13.4 us
    pallas_call x1, Pallas kernels, body(): pl.pallas_call(lambda *refs: forward_kernel(masks, *refs), name='forward'...  4.31 us
    pallas_call x1, Pallas kernels, body(): pl.pallas_call(lambda *refs: backward_kernel(masks, *refs), name='backwar...  3.32 us
    select_n x1, other arithmetic, row_sum(): jnp.where(core == 0, jnp.concatenate([total, other], 0), jnp.concatenate(...  1.61 us
  transfers between devices with their start and end apart: 35, of which 10 were waited for; matrix products, arithmetic and copies ran while one was open for 2% of the time, Pallas kernels for 0%

profile of v1, /device:TPU:0, one launch (start us, length us, event | category | flops | bytes accessed | tf_op | source)
XLA Modules:
  0.0 75.4 jit_solution(14242091755632911910)
XLA Ops:
  0.6 4.1 %collective-permute-start.7 = (bf16[4,128,128]{2,1,0:T(8,128)(2,1)}, bf16[4,128,128]{2,1,0:T(8,128)(2,1)S(1)}, u32[]{:S(2)}, u32[]{:S(2)}) collective-permute-start(bf16[4,128,128]{2,1,0:T(8,128)(2,1)} %bitcast.2), channel_id=1, source_target_pairs={{0,8},{1,9},{2,10},{3,11},{4,12},{5,13},{6,14},{7,15},{8,0},{9,1},... | collective-permute-start | bytes 393224 | tf_op jit(solution)/shard_map/ppermute | solution.py:18
  4.7 1.6 %collective-permute-start.3 = (bf16[4,128,128]{2,1,0:T(8,128)(2,1)}, bf16[4,128,128]{2,1,0:T(8,128)(2,1)S(1)}, u32[]{:S(2)}, u32[]{:S(2)}) collective-permute-start(bf16[4,128,128]{2,1,0:T(8,128)(2,1)} %bitcast.3), channel_id=1, source_target_pairs={{0,4},{1,5},{2,6},{3,7},{4,0},{5,1},{6,2},{7,3},{8,12},{9,13},{10,... | collective-permute-start | bytes 393224 | tf_op jit(solution)/shard_map/ppermute | solution.py:18
  6.3 1.5 %collective-permute-start.1 = (bf16[4,128,128]{2,1,0:T(8,128)(2,1)}, bf16[4,128,128]{2,1,0:T(8,128)(2,1)S(1)}, u32[]{:S(2)}, u32[]{:S(2)}) collective-permute-start(bf16[4,128,128]{2,1,0:T(8,128)(2,1)} %bitcast.4), channel_id=1, source_target_pairs={{0,2},{1,3},{2,0},{3,1},{4,6},{5,7},{6,4},{7,5},{8,10},{9,11},{10,... | collective-permute-start | bytes 393224 | tf_op jit(solution)/shard_map/ppermute | solution.py:18
  7.8 0.0 collective-permute-start
  7.8 3.5 %collective-permute-done.7.refs_11_ = bf16[4,128,128]{2,1,0:T(8,128)(2,1)S(1)} collective-permute-done((bf16[4,128,128]{2,1,0:T(8,128)(2,1)}, bf16[4,128,128]{2,1,0:T(8,128)(2,1)S(1)}, u32[]{:S(2)}, u32[]{:S(2)}) %collective-permute-start.7) | collective-permute-done | bytes 131104 | tf_op jit(solution)/shard_map/ppermute | solution.py:18
  11.4 0.7 collective-permute-start.11
  12.1 1.5 %collective-permute-start.9 = (bf16[4,128,128]{2,1,0:T(8,128)(2,1)S(1)}, bf16[4,128,128]{2,1,0:T(8,128)(2,1)S(1)}, u32[]{:S(2)}, u32[]{:S(2)}) collective-permute-start(bf16[4,128,128]{2,1,0:T(8,128)(2,1)S(1)} %collective-permute-done.7.refs_11_), channel_id=1, source_target_pairs={{0,2},{1,3},{2,0},{3,1},{4,6},{5,7},{6,4},{7,5},{8,10},{9,11},{10,... | collective-permute-start | bytes 393224 | tf_op jit(solution)/shard_map/ppermute | solution.py:18
  13.6 0.0 collective-permute-done.3.refs_7_
  13.6 0.0 collective-permute-start.8
  13.6 0.6 collective-permute-start.5
  14.2 0.2 collective-permute-start.4
  14.3 2.0 %collective-permute-done.11.refs_15_ = bf16[4,128,128]{2,1,0:T(8,128)(2,1)S(1)} collective-permute-done((bf16[4,128,128]{2,1,0:T(8,128)(2,1)S(1)}, bf16[4,128,128]{2,1,0:T(8,128)(2,1)S(1)}, u32[]{:S(2)}, u32[]{:S(2)}) %collective-permute-start.11) | collective-permute-done | bytes 131104 | tf_op jit(solution)/shard_map/ppermute | solution.py:18
  16.3 1.6 %collective-permute-start.13 = (bf16[4,128,128]{2,1,0:T(8,128)(2,1)S(1)}, bf16[4,128,128]{2,1,0:T(8,128)(2,1)S(1)}, u32[]{:S(2)}, u32[]{:S(2)}) collective-permute-start(bf16[4,128,128]{2,1,0:T(8,128)(2,1)S(1)} %collective-permute-done.11.refs_15_), channel_id=1, source_target_pairs={{0,2},{1,3},{2,0},{3,1},{4,6},{5,7},{6,4},{7,5},{8,10},{9,11},{10,... | collective-permute-start | bytes 393224 | tf_op jit(solution)/shard_map/ppermute | solution.py:18
  17.9 0.0 collective-permute-start.2
  17.9 0.0 collective-permute-done.8.refs_12_
  17.9 0.5 collective-permute-start.12
  18.4 2.1 %collective-permute-done.5.refs_9_ = bf16[4,128,128]{2,1,0:T(8,128)(2,1)S(1)} collective-permute-done((bf16[4,128,128]{2,1,0:T(8,128)(2,1)S(1)}, bf16[4,128,128]{2,1,0:T(8,128)(2,1)S(1)}, u32[]{:S(2)}, u32[]{:S(2)}) %collective-permute-start.5) | collective-permute-done | bytes 131104 | tf_op jit(solution)/shard_map/ppermute | solution.py:18
  20.5 0.0 collective-permute-start.10
  20.5 0.0 collective-permute-done.4.refs_8_
  20.5 0.5 collective-permute-start.6
  21.0 1.8 %collective-permute-done.13.refs_17_ = bf16[4,128,128]{2,1,0:T(8,128)(2,1)S(1)} collective-permute-done((bf16[4,128,128]{2,1,0:T(8,128)(2,1)S(1)}, bf16[4,128,128]{2,1,0:T(8,128)(2,1)S(1)}, u32[]{:S(2)}, u32[]{:S(2)}) %collective-permute-start.13) | collective-permute-done | bytes 131104 | tf_op jit(solution)/shard_map/ppermute | solution.py:18
  22.8 0.7 copy-done.4
  23.5 0.0 collective-permute-done.12.refs_16_
  23.5 0.7 copy-done.6
  24.2 0.0 collective-permute-done.10.refs_14_
  24.2 0.7 copy-done.8
  24.8 0.7 copy-done.10
  25.5 0.0 collective-permute-done.14.refs_18_
  25.5 0.7 copy-done.12
  26.1 1.6 %copy-done = bf16[4,16,128,128]{3,2,1,0:T(8,128)(2,1)S(1)} copy-done((bf16[4,16,128,128]{3,2,1,0:T(8,128)(2,1)S(1)}, bf16[4,16,128,128]{3,2,1,0:T(8,128)(2,1)}, u32[]{:S(2)}) %copy-start) | copy-done | bytes 2097176
  27.7 0.9 %copy-done.2 = bf16[512,256]{1,0:T(8,128)(2,1)S(1)} copy-done((bf16[512,256]{1,0:T(8,128)(2,1)S(1)}, bf16[512,256]{1,0:T(8,128)(2,1)}, u32[]{:S(2)}) %copy-start.2) | copy-done | bytes 262168
  28.7 0.9 %copy-done.3 = bf16[512,128]{1,0:T(8,128)(2,1)S(1)} copy-done((bf16[512,128]{1,0:T(8,128)(2,1)S(1)}, bf16[512,128]{1,0:T(8,128)(2,1)}, u32[]{:S(2)}) %copy-start.3) | copy-done | bytes 131096
  29.6 0.9 %copy-done.5 = bf16[4,128,128]{2,1,0:T(8,128)(2,1)S(1)} copy-done((bf16[4,128,128]{2,1,0:T(8,128)(2,1)S(1)}, bf16[4,128,128]{2,1,0:T(8,128)(2,1)}, u32[]{:S(2)}) %copy-start.5) | copy-done | bytes 131096
  30.5 0.9 %copy-done.7 = bf16[4,128,128]{2,1,0:T(8,128)(2,1)S(1)} copy-done((bf16[4,128,128]{2,1,0:T(8,128)(2,1)S(1)}, bf16[4,128,128]{2,1,0:T(8,128)(2,1)}, u32[]{:S(2)}) %copy-start.7) | copy-done | bytes 131096
  31.4 0.9 %copy-done.9 = bf16[4,128,128]{2,1,0:T(8,128)(2,1)S(1)} copy-done((bf16[4,128,128]{2,1,0:T(8,128)(2,1)S(1)}, bf16[4,128,128]{2,1,0:T(8,128)(2,1)}, u32[]{:S(2)}) %copy-start.9) | copy-done | bytes 131096
  32.3 0.9 %copy-done.11 = bf16[4,128,128]{2,1,0:T(8,128)(2,1)S(1)} copy-done((bf16[4,128,128]{2,1,0:T(8,128)(2,1)S(1)}, bf16[4,128,128]{2,1,0:T(8,128)(2,1)}, u32[]{:S(2)}) %copy-start.11) | copy-done | bytes 131096
  33.2 0.9 %copy-done.13 = bf16[4,128,128]{2,1,0:T(8,128)(2,1)S(1)} copy-done((bf16[4,128,128]{2,1,0:T(8,128)(2,1)S(1)}, bf16[4,128,128]{2,1,0:T(8,128)(2,1)}, u32[]{:S(2)}) %copy-start.13) | copy-done | bytes 131096
  34.1 0.8 %copy-done.14 = bf16[128,256]{1,0:T(8,128)(2,1)S(1)} copy-done((bf16[128,256]{1,0:T(8,128)(2,1)S(1)}, bf16[128,256]{1,0:T(8,128)(2,1)}, u32[]{:S(2)}) %copy-start.14) | copy-done | bytes 65560
  34.9 0.7 copy-done.15
  35.6 0.7 copy-done.17
  36.3 4.3 %forward.1 = (bf16[512,256]{1,0:T(8,128)(2,1)}, bf16[4,128,128]{2,1,0:T(8,128)(2,1)S(1)}, f32[64,256]{1,0:T(8,128)S(1)}, f32[64,256]{1,0:T(8,128)S(1)}) custom-call(s32[1]{0:T(128)} %bitcast.refs_0_, s32[4,16]{1,0:T(4,128)S(1)} %copy-done.15, s32[4]{0:T(128)S(1)} %copy-done.17, bf16[4,128,128]{2,1,0:T(8,128)(2,1)S(1)} %bitcast.6, ...), custom_call_target="tpu_custom_call" | custom-call | tf_op jit(solution)/shard_map/forward/pallas_call | solution.py:157
  40.6 0.2 collective-permute-start.30
  40.8 3.6 %collective-permute-start.22 = (bf16[4,128,128]{2,1,0:T(8,128)(2,1)S(1)}, bf16[4,128,128]{2,1,0:T(8,128)(2,1)S(1)}, u32[]{:S(2)}, u32[]{:S(2)}) collective-permute-start(bf16[4,128,128]{2,1,0:T(8,128)(2,1)S(1)} %get-tuple-element.8.refs_3_), channel_id=1, source_target_pairs={{0,8},{1,9},{2,10},{3,11},{4,12},{5,13},{6,14},{7,15},{8,0},{9,1},... | collective-permute-start | bytes 393224 | tf_op jit(solution)/shard_map/ppermute | solution.py:18
  44.4 1.0 %collective-permute-start.31 = (f32[64,256]{1,0:T(8,128)S(1)}, f32[64,256]{1,0:T(8,128)S(1)}, u32[]{:S(2)}, u32[]{:S(2)}) collective-permute-start(f32[64,256]{1,0:T(8,128)S(1)} %add.17), channel_id=1, source_target_pairs={{0,8},{1,9},{2,10},{3,11},{4,12},{5,13},{6,14},{7,15},{8,0},{9,1},... | collective-permute-start | bytes 196616 | tf_op jit(solution)/shard_map/ppermute | solution.py:18
  45.4 0.3 collective-permute-start.18
  45.6 2.1 %collective-permute-start.16 = (bf16[4,128,128]{2,1,0:T(8,128)(2,1)S(1)}, bf16[4,128,128]{2,1,0:T(8,128)(2,1)S(1)}, u32[]{:S(2)}, u32[]{:S(2)}) collective-permute-start(bf16[4,128,128]{2,1,0:T(8,128)(2,1)S(1)} %get-tuple-element.8.refs_3_), channel_id=1, source_target_pairs={{0,2},{1,3},{2,0},{3,1},{4,6},{5,7},{6,4},{7,5},{8,10},{9,11},{10,... | collective-permute-start | bytes 393224 | tf_op jit(solution)/shard_map/ppermute | solution.py:18
  47.8 6.0 %collective-permute-done.31 = f32[64,256]{1,0:T(8,128)S(1)} collective-permute-done((f32[64,256]{1,0:T(8,128)S(1)}, f32[64,256]{1,0:T(8,128)S(1)}, u32[]{:S(2)}, u32[]{:S(2)}) %collective-permute-start.31) | collective-permute-done | bytes 65568 | tf_op jit(solution)/shard_map/ppermute | solution.py:18
  53.8 0.1 collective-permute-start.32
  53.9 0.1 collective-permute-start.15
  53.9 1.9 %collective-permute-start.26 = (bf16[4,128,128]{2,1,0:T(8,128)(2,1)S(1)}, bf16[4,128,128]{2,1,0:T(8,128)(2,1)S(1)}, u32[]{:S(2)}, u32[]{:S(2)}) collective-permute-start(bf16[4,128,128]{2,1,0:T(8,128)(2,1)S(1)} %collective-permute-done.22.refs_11_), channel_id=1, source_target_pairs={{0,4},{1,5},{2,6},{3,7},{4,0},{5,1},{6,2},{7,3},{8,12},{9,13},{10,... | collective-permute-start | bytes 393224 | tf_op jit(solution)/shard_map/ppermute | solution.py:18
  55.9 2.9 %collective-permute-done.32 = f32[64,256]{1,0:T(8,128)S(1)} collective-permute-done((f32[64,256]{1,0:T(8,128)S(1)}, f32[64,256]{1,0:T(8,128)S(1)}, u32[]{:S(2)}, u32[]{:S(2)}) %collective-permute-start.32) | collective-permute-done | bytes 65568 | tf_op jit(solution)/shard_map/ppermute | solution.py:18
  58.8 1.0 %collective-permute-start.33 = (f32[64,256]{1,0:T(8,128)S(1)}, f32[64,256]{1,0:T(8,128)S(1)}, u32[]{:S(2)}, u32[]{:S(2)}) collective-permute-start(f32[64,256]{1,0:T(8,128)S(1)} %add.19), channel_id=1, source_target_pairs={{0,2},{1,3},{2,0},{3,1},{4,6},{5,7},{6,4},{7,5},{8,10},{9,11},{10,... | collective-permute-start | bytes 196616 | tf_op jit(solution)/shard_map/ppermute | solution.py:18
  59.8 1.1 %collective-permute-start.24 = (bf16[4,128,128]{2,1,0:T(8,128)(2,1)S(1)}, bf16[4,128,128]{2,1,0:T(8,128)(2,1)S(1)}, u32[]{:S(2)}, u32[]{:S(2)}) collective-permute-start(bf16[4,128,128]{2,1,0:T(8,128)(2,1)S(1)} %collective-permute-done.22.refs_11_), channel_id=1, source_target_pairs={{0,2},{1,3},{2,0},{3,1},{4,6},{5,7},{6,4},{7,5},{8,10},{9,11},{10,... | collective-permute-start | bytes 393224 | tf_op jit(solution)/shard_map/ppermute | solution.py:18
  60.9 1.0 %collective-permute-start.20 = (bf16[4,128,128]{2,1,0:T(8,128)(2,1)S(1)}, bf16[4,128,128]{2,1,0:T(8,128)(2,1)S(1)}, u32[]{:S(2)}, u32[]{:S(2)}) collective-permute-start(bf16[4,128,128]{2,1,0:T(8,128)(2,1)S(1)} %collective-permute-done.18.refs_7_), channel_id=1, source_target_pairs={{0,2},{1,3},{2,0},{3,1},{4,6},{5,7},{6,4},{7,5},{8,10},{9,11},{10,... | collective-permute-start | bytes 393224 | tf_op jit(solution)/shard_map/ppermute | solution.py:18
  62.0 1.2 %collective-permute-done.33 = f32[64,256]{1,0:T(8,128)S(1)} collective-permute-done((f32[64,256]{1,0:T(8,128)S(1)}, f32[64,256]{1,0:T(8,128)S(1)}, u32[]{:S(2)}, u32[]{:S(2)}) %collective-permute-start.33) | collective-permute-done | bytes 65568 | tf_op jit(solution)/shard_map/ppermute | solution.py:18
  63.2 1.0 %collective-permute-start.28 = (bf16[4,128,128]{2,1,0:T(8,128)(2,1)S(1)}, bf16[4,128,128]{2,1,0:T(8,128)(2,1)S(1)}, u32[]{:S(2)}, u32[]{:S(2)}) collective-permute-start(bf16[4,128,128]{2,1,0:T(8,128)(2,1)S(1)} %collective-permute-done.26.refs_15_), channel_id=1, source_target_pairs={{0,2},{1,3},{2,0},{3,1},{4,6},{5,7},{6,4},{7,5},{8,10},{9,11},{10,... | collective-permute-start | bytes 393224 | tf_op jit(solution)/shard_map/ppermute | solution.py:18
  64.1 1.5 %collective-permute-done.24.refs_13_ = bf16[4,128,128]{2,1,0:T(8,128)(2,1)S(1)} collective-permute-done((bf16[4,128,128]{2,1,0:T(8,128)(2,1)S(1)}, bf16[4,128,128]{2,1,0:T(8,128)(2,1)S(1)}, u32[]{:S(2)}, u32[]{:S(2)}) %collective-permute-start.24) | collective-permute-done | bytes 131104 | tf_op jit(solution)/shard_map/ppermute | solution.py:18
  65.7 0.5 collective-permute-start.17
  66.2 2.3 %collective-permute-done.20.refs_9_ = bf16[4,128,128]{2,1,0:T(8,128)(2,1)S(1)} collective-permute-done((bf16[4,128,128]{2,1,0:T(8,128)(2,1)S(1)}, bf16[4,128,128]{2,1,0:T(8,128)(2,1)S(1)}, u32[]{:S(2)}, u32[]{:S(2)}) %collective-permute-start.20) | collective-permute-done | bytes 131104 | tf_op jit(solution)/shard_map/ppermute | solution.py:18
  68.5 0.5 collective-permute-start.25
  69.0 0.1 collective-permute-start.21
  69.1 1.4 %collective-permute-done.28.refs_17_ = bf16[4,128,128]{2,1,0:T(8,128)(2,1)S(1)} collective-permute-done((bf16[4,128,128]{2,1,0:T(8,128)(2,1)S(1)}, bf16[4,128,128]{2,1,0:T(8,128)(2,1)S(1)}, u32[]{:S(2)}, u32[]{:S(2)}) %collective-permute-start.28) | collective-permute-done | bytes 131104 | tf_op jit(solution)/shard_map/ppermute | solution.py:18
  70.5 1.6 %maximum_select_fusion = f32[128,256]{1,0:T(8,128)} fusion(f32[64,256]{1,0:T(8,128)} %copy-done.20, f32[64,256]{1,0:T(8,128)} %copy-done.19, pred[]{:T(512)S(6)} %eq.5), kind=kLoop, calls=%fused_computation | loop fusion | flops 98304 | bytes 262145 | tf_op jit(solution)/shard_map/jit(_where)/select_n | solution.py:42
  72.1 3.3 %backward.1 = bf16[512,128]{1,0:T(8,128)(2,1)} custom-call(s32[1]{0:T(128)} %bitcast.refs_0_, s32[4,16]{1,0:T(4,128)S(1)} %copy-done.16, s32[4]{0:T(128)S(1)} %copy-done.18, bf16[4,128,128]{2,1,0:T(8,128)(2,1)S(1)} %get-tuple-element.8.refs_3_, bf16[4,128,128]{2,1,0:T(8,128)(2,1)S(1)} %collective-permute-done.15.refs_4_, ...), custom_call_target="tpu_custom_call" | custom-call | tf_op jit(solution)/shard_map/backward/pallas_call | solution.py:173
  (55 shorter events, 0.1 us)
Async XLA Ops:
  0.6 10.7 %collective-permute-start.7 = (bf16[4,128,128]{2,1,0:T(8,128)(2,1)}, bf16[4,128,128]{2,1,0:T(8,128)(2,1)S(1)}, u32[]{:S(2)}, u32[]{:S(2)}) collective-permute-start(bf16[4,128,128]{2,1,0:T(8,128)(2,1)} %bitcast.2), channel_id=1, source_target_pairs={{0,8},{1,9},{2,10},{3,11},{4,12},{5,13},{6,14},{7,15},{8,0},{9,1},... | collective-permute-start | bytes 393224 | tf_op jit(solution)/shard_map/ppermute | solution.py:18
  4.7 8.9 %collective-permute-start.3 = (bf16[4,128,128]{2,1,0:T(8,128)(2,1)}, bf16[4,128,128]{2,1,0:T(8,128)(2,1)S(1)}, u32[]{:S(2)}, u32[]{:S(2)}) collective-permute-start(bf16[4,128,128]{2,1,0:T(8,128)(2,1)} %bitcast.3), channel_id=1, source_target_pairs={{0,4},{1,5},{2,6},{3,7},{4,0},{5,1},{6,2},{7,3},{8,12},{9,13},{10,... | collective-permute-start | bytes 393224 | tf_op jit(solution)/shard_map/ppermute | solution.py:18
  6.3 7.3 %collective-permute-start.1 = (bf16[4,128,128]{2,1,0:T(8,128)(2,1)}, bf16[4,128,128]{2,1,0:T(8,128)(2,1)S(1)}, u32[]{:S(2)}, u32[]{:S(2)}) collective-permute-start(bf16[4,128,128]{2,1,0:T(8,128)(2,1)} %bitcast.4), channel_id=1, source_target_pairs={{0,2},{1,3},{2,0},{3,1},{4,6},{5,7},{6,4},{7,5},{8,10},{9,11},{10,... | collective-permute-start | bytes 393224 | tf_op jit(solution)/shard_map/ppermute | solution.py:18
  7.8 6.4 %collective-permute-start = (bf16[4,128,128]{2,1,0:T(8,128)(2,1)}, bf16[4,128,128]{2,1,0:T(8,128)(2,1)S(1)}, u32[]{:S(2)}, u32[]{:S(2)}) collective-permute-start(bf16[4,128,128]{2,1,0:T(8,128)(2,1)} %bitcast.5), channel_id=1, source_target_pairs={{0,1},{1,0},{2,3},{3,2},{4,5},{5,4},{6,7},{7,6},{8,9},{9,8},{10,11... | collective-permute-start | bytes 393224 | tf_op jit(solution)/shard_map/ppermute | solution.py:18
  11.4 5.0 %collective-permute-start.11 = (bf16[4,128,128]{2,1,0:T(8,128)(2,1)S(1)}, bf16[4,128,128]{2,1,0:T(8,128)(2,1)S(1)}, u32[]{:S(2)}, u32[]{:S(2)}) collective-permute-start(bf16[4,128,128]{2,1,0:T(8,128)(2,1)S(1)} %collective-permute-done.7.refs_11_), channel_id=1, source_target_pairs={{0,4},{1,5},{2,6},{3,7},{4,0},{5,1},{6,2},{7,3},{8,12},{9,13},{10,... | collective-permute-start | bytes 393224 | tf_op jit(solution)/shard_map/ppermute | solution.py:18
  12.1 5.8 %collective-permute-start.9 = (bf16[4,128,128]{2,1,0:T(8,128)(2,1)S(1)}, bf16[4,128,128]{2,1,0:T(8,128)(2,1)S(1)}, u32[]{:S(2)}, u32[]{:S(2)}) collective-permute-start(bf16[4,128,128]{2,1,0:T(8,128)(2,1)S(1)} %collective-permute-done.7.refs_11_), channel_id=1, source_target_pairs={{0,2},{1,3},{2,0},{3,1},{4,6},{5,7},{6,4},{7,5},{8,10},{9,11},{10,... | collective-permute-start | bytes 393224 | tf_op jit(solution)/shard_map/ppermute | solution.py:18
  13.6 4.3 %collective-permute-start.8 = (bf16[4,128,128]{2,1,0:T(8,128)(2,1)S(1)}, bf16[4,128,128]{2,1,0:T(8,128)(2,1)S(1)}, u32[]{:S(2)}, u32[]{:S(2)}) collective-permute-start(bf16[4,128,128]{2,1,0:T(8,128)(2,1)S(1)} %collective-permute-done.7.refs_11_), channel_id=1, source_target_pairs={{0,1},{1,0},{2,3},{3,2},{4,5},{5,4},{6,7},{7,6},{8,9},{9,8},{10,11... | collective-permute-start | bytes 393224 | tf_op jit(solution)/shard_map/ppermute | solution.py:18
  13.6 6.9 %collective-permute-start.5 = (bf16[4,128,128]{2,1,0:T(8,128)(2,1)S(1)}, bf16[4,128,128]{2,1,0:T(8,128)(2,1)S(1)}, u32[]{:S(2)}, u32[]{:S(2)}) collective-permute-start(bf16[4,128,128]{2,1,0:T(8,128)(2,1)S(1)} %collective-permute-done.3.refs_7_), channel_id=1, source_target_pairs={{0,2},{1,3},{2,0},{3,1},{4,6},{5,7},{6,4},{7,5},{8,10},{9,11},{10,... | collective-permute-start | bytes 393224 | tf_op jit(solution)/shard_map/ppermute | solution.py:18
  14.2 6.3 %collective-permute-start.4 = (bf16[4,128,128]{2,1,0:T(8,128)(2,1)S(1)}, bf16[4,128,128]{2,1,0:T(8,128)(2,1)S(1)}, u32[]{:S(2)}, u32[]{:S(2)}) collective-permute-start(bf16[4,128,128]{2,1,0:T(8,128)(2,1)S(1)} %collective-permute-done.3.refs_7_), channel_id=1, source_target_pairs={{0,1},{1,0},{2,3},{3,2},{4,5},{5,4},{6,7},{7,6},{8,9},{9,8},{10,11... | collective-permute-start | bytes 393224 | tf_op jit(solution)/shard_map/ppermute | solution.py:18
  16.3 6.5 %collective-permute-start.13 = (bf16[4,128,128]{2,1,0:T(8,128)(2,1)S(1)}, bf16[4,128,128]{2,1,0:T(8,128)(2,1)S(1)}, u32[]{:S(2)}, u32[]{:S(2)}) collective-permute-start(bf16[4,128,128]{2,1,0:T(8,128)(2,1)S(1)} %collective-permute-done.11.refs_15_), channel_id=1, source_target_pairs={{0,2},{1,3},{2,0},{3,1},{4,6},{5,7},{6,4},{7,5},{8,10},{9,11},{10,... | collective-permute-start | bytes 393224 | tf_op jit(solution)/shard_map/ppermute | solution.py:18
  17.9 4.9 %collective-permute-start.2 = (bf16[4,128,128]{2,1,0:T(8,128)(2,1)S(1)}, bf16[4,128,128]{2,1,0:T(8,128)(2,1)S(1)}, u32[]{:S(2)}, u32[]{:S(2)}) collective-permute-start(bf16[4,128,128]{2,1,0:T(8,128)(2,1)S(1)} %collective-permute-done.1.refs_5_), channel_id=1, source_target_pairs={{0,1},{1,0},{2,3},{3,2},{4,5},{5,4},{6,7},{7,6},{8,9},{9,8},{10,11... | collective-permute-start | bytes 393224 | tf_op jit(solution)/shard_map/ppermute | solution.py:18
  17.9 5.6 %collective-permute-start.12 = (bf16[4,128,128]{2,1,0:T(8,128)(2,1)S(1)}, bf16[4,128,128]{2,1,0:T(8,128)(2,1)S(1)}, u32[]{:S(2)}, u32[]{:S(2)}) collective-permute-start(bf16[4,128,128]{2,1,0:T(8,128)(2,1)S(1)} %collective-permute-done.11.refs_15_), channel_id=1, source_target_pairs={{0,1},{1,0},{2,3},{3,2},{4,5},{5,4},{6,7},{7,6},{8,9},{9,8},{10,11... | collective-permute-start | bytes 393224 | tf_op jit(solution)/shard_map/ppermute | solution.py:18
  20.5 3.6 %collective-permute-start.10 = (bf16[4,128,128]{2,1,0:T(8,128)(2,1)S(1)}, bf16[4,128,128]{2,1,0:T(8,128)(2,1)S(1)}, u32[]{:S(2)}, u32[]{:S(2)}) collective-permute-start(bf16[4,128,128]{2,1,0:T(8,128)(2,1)S(1)} %collective-permute-done.9.refs_13_), channel_id=1, source_target_pairs={{0,1},{1,0},{2,3},{3,2},{4,5},{5,4},{6,7},{7,6},{8,9},{9,8},{10,11... | collective-permute-start | bytes 393224 | tf_op jit(solution)/shard_map/ppermute | solution.py:18
  20.5 4.3 %collective-permute-start.6 = (bf16[4,128,128]{2,1,0:T(8,128)(2,1)S(1)}, bf16[4,128,128]{2,1,0:T(8,128)(2,1)S(1)}, u32[]{:S(2)}, u32[]{:S(2)}) collective-permute-start(bf16[4,128,128]{2,1,0:T(8,128)(2,1)S(1)} %collective-permute-done.5.refs_9_), channel_id=1, source_target_pairs={{0,1},{1,0},{2,3},{3,2},{4,5},{5,4},{6,7},{7,6},{8,9},{9,8},{10,11... | collective-permute-start | bytes 393224 | tf_op jit(solution)/shard_map/ppermute | solution.py:18
  22.8 2.6 %collective-permute-start.14 = (bf16[4,128,128]{2,1,0:T(8,128)(2,1)S(1)}, bf16[4,128,128]{2,1,0:T(8,128)(2,1)S(1)}, u32[]{:S(2)}, u32[]{:S(2)}) collective-permute-start(bf16[4,128,128]{2,1,0:T(8,128)(2,1)S(1)} %collective-permute-done.13.refs_17_), channel_id=1, source_target_pairs={{0,1},{1,0},{2,3},{3,2},{4,5},{5,4},{6,7},{7,6},{8,9},{9,8},{10,11... | collective-permute-start | bytes 393224 | tf_op jit(solution)/shard_map/ppermute | solution.py:18
  22.8 0.7 copy-start.4
  23.5 0.7 copy-start.6
  24.2 0.7 copy-start.8
  24.8 0.7 copy-start.10
  25.5 0.7 copy-start.12
  26.1 1.6 %copy-start = (bf16[4,16,128,128]{3,2,1,0:T(8,128)(2,1)S(1)}, bf16[4,16,128,128]{3,2,1,0:T(8,128)(2,1)}, u32[]{:S(2)}) copy-start(bf16[4,16,128,128]{3,2,1,0:T(8,128)(2,1)} %refs_19_.3) | copy-start | bytes 6291460
  27.7 0.9 %copy-start.2 = (bf16[512,256]{1,0:T(8,128)(2,1)S(1)}, bf16[512,256]{1,0:T(8,128)(2,1)}, u32[]{:S(2)}) copy-start(bf16[512,256]{1,0:T(8,128)(2,1)} %refs_21_.1) | copy-start | bytes 786436
  28.7 0.9 %copy-start.3 = (bf16[512,128]{1,0:T(8,128)(2,1)S(1)}, bf16[512,128]{1,0:T(8,128)(2,1)}, u32[]{:S(2)}) copy-start(bf16[512,128]{1,0:T(8,128)(2,1)} %param.6) | copy-start | bytes 393220
  29.6 0.9 %copy-start.5 = (bf16[4,128,128]{2,1,0:T(8,128)(2,1)S(1)}, bf16[4,128,128]{2,1,0:T(8,128)(2,1)}, u32[]{:S(2)}) copy-start(bf16[4,128,128]{2,1,0:T(8,128)(2,1)} %copy-done.4) | copy-start | bytes 393220
  30.5 0.9 %copy-start.7 = (bf16[4,128,128]{2,1,0:T(8,128)(2,1)S(1)}, bf16[4,128,128]{2,1,0:T(8,128)(2,1)}, u32[]{:S(2)}) copy-start(bf16[4,128,128]{2,1,0:T(8,128)(2,1)} %copy-done.6) | copy-start | bytes 393220
  31.4 0.9 %copy-start.9 = (bf16[4,128,128]{2,1,0:T(8,128)(2,1)S(1)}, bf16[4,128,128]{2,1,0:T(8,128)(2,1)}, u32[]{:S(2)}) copy-start(bf16[4,128,128]{2,1,0:T(8,128)(2,1)} %copy-done.8) | copy-start | bytes 393220
  32.3 0.9 %copy-start.11 = (bf16[4,128,128]{2,1,0:T(8,128)(2,1)S(1)}, bf16[4,128,128]{2,1,0:T(8,128)(2,1)}, u32[]{:S(2)}) copy-start(bf16[4,128,128]{2,1,0:T(8,128)(2,1)} %copy-done.10) | copy-start | bytes 393220
  33.2 0.9 %copy-start.13 = (bf16[4,128,128]{2,1,0:T(8,128)(2,1)S(1)}, bf16[4,128,128]{2,1,0:T(8,128)(2,1)}, u32[]{:S(2)}) copy-start(bf16[4,128,128]{2,1,0:T(8,128)(2,1)} %copy-done.12) | copy-start | bytes 393220
  34.1 0.8 %copy-start.14 = (bf16[128,256]{1,0:T(8,128)(2,1)S(1)}, bf16[128,256]{1,0:T(8,128)(2,1)}, u32[]{:S(2)}) copy-start(bf16[128,256]{1,0:T(8,128)(2,1)} %refs_20_.1) | copy-start | bytes 196612
  34.9 0.7 copy-start.15
  35.6 0.7 copy-start.17
  36.3 35.8 %copy-start.1 = (bf16[4,16,128,128]{3,2,1,0:T(8,128)(2,1)S(1)}, bf16[4,16,128,128]{3,2,1,0:T(8,128)(2,1)}, u32[]{:S(2)}) copy-start(bf16[4,16,128,128]{3,2,1,0:T(8,128)(2,1)} %refs_19_.3) | copy-start | bytes 6291460
  36.3 35.8 %copy-start.16 = (s32[4,16]{1,0:T(4,128)S(1)}, s32[4,16]{1,0:T(4,128)}, u32[]{:S(2)}) copy-start(s32[4,16]{1,0:T(4,128)} %refs_1_.3) | copy-start | bytes 772
  36.3 35.8 %copy-start.18 = (s32[4]{0:T(128)S(1)}, s32[4]{0:T(128)}, u32[]{:S(2)}) copy-start(s32[4]{0:T(128)} %refs_2_.3) | copy-start | bytes 52
  40.6 3.8 %collective-permute-start.30 = (f32[64,256]{1,0:T(8,128)S(1)}, f32[64,256]{1,0:T(8,128)S(1)}, u32[]{:S(2)}, u32[]{:S(2)}) collective-permute-start(f32[64,256]{1,0:T(8,128)S(1)} %get-tuple-element.10), channel_id=1, source_target_pairs={{0,1},{1,0},{2,3},{3,2},{4,5},{5,4},{6,7},{7,6},{8,9},{9,8},{10,11... | collective-permute-start | bytes 196616 | tf_op jit(solution)/shard_map/ppermute | solution.py:18
  40.8 13.2 %collective-permute-start.22 = (bf16[4,128,128]{2,1,0:T(8,128)(2,1)S(1)}, bf16[4,128,128]{2,1,0:T(8,128)(2,1)S(1)}, u32[]{:S(2)}, u32[]{:S(2)}) collective-permute-start(bf16[4,128,128]{2,1,0:T(8,128)(2,1)S(1)} %get-tuple-element.8.refs_3_), channel_id=1, source_target_pairs={{0,8},{1,9},{2,10},{3,11},{4,12},{5,13},{6,14},{7,15},{8,0},{9,1},... | collective-permute-start | bytes 393224 | tf_op jit(solution)/shard_map/ppermute | solution.py:18
  44.4 9.3 %collective-permute-start.31 = (f32[64,256]{1,0:T(8,128)S(1)}, f32[64,256]{1,0:T(8,128)S(1)}, u32[]{:S(2)}, u32[]{:S(2)}) collective-permute-start(f32[64,256]{1,0:T(8,128)S(1)} %add.17), channel_id=1, source_target_pairs={{0,8},{1,9},{2,10},{3,11},{4,12},{5,13},{6,14},{7,15},{8,0},{9,1},... | collective-permute-start | bytes 196616 | tf_op jit(solution)/shard_map/ppermute | solution.py:18
  45.4 14.5 %collective-permute-start.18 = (bf16[4,128,128]{2,1,0:T(8,128)(2,1)S(1)}, bf16[4,128,128]{2,1,0:T(8,128)(2,1)S(1)}, u32[]{:S(2)}, u32[]{:S(2)}) collective-permute-start(bf16[4,128,128]{2,1,0:T(8,128)(2,1)S(1)} %get-tuple-element.8.refs_3_), channel_id=1, source_target_pairs={{0,4},{1,5},{2,6},{3,7},{4,0},{5,1},{6,2},{7,3},{8,12},{9,13},{10,... | collective-permute-start | bytes 393224 | tf_op jit(solution)/shard_map/ppermute | solution.py:18
  45.6 15.3 %collective-permute-start.16 = (bf16[4,128,128]{2,1,0:T(8,128)(2,1)S(1)}, bf16[4,128,128]{2,1,0:T(8,128)(2,1)S(1)}, u32[]{:S(2)}, u32[]{:S(2)}) collective-permute-start(bf16[4,128,128]{2,1,0:T(8,128)(2,1)S(1)} %get-tuple-element.8.refs_3_), channel_id=1, source_target_pairs={{0,2},{1,3},{2,0},{3,1},{4,6},{5,7},{6,4},{7,5},{8,10},{9,11},{10,... | collective-permute-start | bytes 393224 | tf_op jit(solution)/shard_map/ppermute | solution.py:18
  53.8 5.0 %collective-permute-start.32 = (f32[64,256]{1,0:T(8,128)S(1)}, f32[64,256]{1,0:T(8,128)S(1)}, u32[]{:S(2)}, u32[]{:S(2)}) collective-permute-start(f32[64,256]{1,0:T(8,128)S(1)} %add.18), channel_id=1, source_target_pairs={{0,4},{1,5},{2,6},{3,7},{4,0},{5,1},{6,2},{7,3},{8,12},{9,13},{10,... | collective-permute-start | bytes 196616 | tf_op jit(solution)/shard_map/ppermute | solution.py:18
  53.9 7.1 %collective-permute-start.15 = (bf16[4,128,128]{2,1,0:T(8,128)(2,1)S(1)}, bf16[4,128,128]{2,1,0:T(8,128)(2,1)S(1)}, u32[]{:S(2)}, u32[]{:S(2)}) collective-permute-start(bf16[4,128,128]{2,1,0:T(8,128)(2,1)S(1)} %get-tuple-element.8.refs_3_), channel_id=1, source_target_pairs={{0,1},{1,0},{2,3},{3,2},{4,5},{5,4},{6,7},{7,6},{8,9},{9,8},{10,11... | collective-permute-start | bytes 393224 | tf_op jit(solution)/shard_map/ppermute | solution.py:18
  53.9 9.2 %collective-permute-start.26 = (bf16[4,128,128]{2,1,0:T(8,128)(2,1)S(1)}, bf16[4,128,128]{2,1,0:T(8,128)(2,1)S(1)}, u32[]{:S(2)}, u32[]{:S(2)}) collective-permute-start(bf16[4,128,128]{2,1,0:T(8,128)(2,1)S(1)} %collective-permute-done.22.refs_11_), channel_id=1, source_target_pairs={{0,4},{1,5},{2,6},{3,7},{4,0},{5,1},{6,2},{7,3},{8,12},{9,13},{10,... | collective-permute-start | bytes 393224 | tf_op jit(solution)/shard_map/ppermute | solution.py:18
  58.8 4.3 %collective-permute-start.33 = (f32[64,256]{1,0:T(8,128)S(1)}, f32[64,256]{1,0:T(8,128)S(1)}, u32[]{:S(2)}, u32[]{:S(2)}) collective-permute-start(f32[64,256]{1,0:T(8,128)S(1)} %add.19), channel_id=1, source_target_pairs={{0,2},{1,3},{2,0},{3,1},{4,6},{5,7},{6,4},{7,5},{8,10},{9,11},{10,... | collective-permute-start | bytes 196616 | tf_op jit(solution)/shard_map/ppermute | solution.py:18
  59.8 5.8 %collective-permute-start.24 = (bf16[4,128,128]{2,1,0:T(8,128)(2,1)S(1)}, bf16[4,128,128]{2,1,0:T(8,128)(2,1)S(1)}, u32[]{:S(2)}, u32[]{:S(2)}) collective-permute-start(bf16[4,128,128]{2,1,0:T(8,128)(2,1)S(1)} %collective-permute-done.22.refs_11_), channel_id=1, source_target_pairs={{0,2},{1,3},{2,0},{3,1},{4,6},{5,7},{6,4},{7,5},{8,10},{9,11},{10,... | collective-permute-start | bytes 393224 | tf_op jit(solution)/shard_map/ppermute | solution.py:18
  60.9 4.8 %collective-permute-start.23 = (bf16[4,128,128]{2,1,0:T(8,128)(2,1)S(1)}, bf16[4,128,128]{2,1,0:T(8,128)(2,1)S(1)}, u32[]{:S(2)}, u32[]{:S(2)}) collective-permute-start(bf16[4,128,128]{2,1,0:T(8,128)(2,1)S(1)} %collective-permute-done.22.refs_11_), channel_id=1, source_target_pairs={{0,1},{1,0},{2,3},{3,2},{4,5},{5,4},{6,7},{7,6},{8,9},{9,8},{10,11... | collective-permute-start | bytes 393224 | tf_op jit(solution)/shard_map/ppermute | solution.py:18
  60.9 7.5 %collective-permute-start.20 = (bf16[4,128,128]{2,1,0:T(8,128)(2,1)S(1)}, bf16[4,128,128]{2,1,0:T(8,128)(2,1)S(1)}, u32[]{:S(2)}, u32[]{:S(2)}) collective-permute-start(bf16[4,128,128]{2,1,0:T(8,128)(2,1)S(1)} %collective-permute-done.18.refs_7_), channel_id=1, source_target_pairs={{0,2},{1,3},{2,0},{3,1},{4,6},{5,7},{6,4},{7,5},{8,10},{9,11},{10,... | collective-permute-start | bytes 393224 | tf_op jit(solution)/shard_map/ppermute | solution.py:18
  63.1 5.3 %collective-permute-start.19 = (bf16[4,128,128]{2,1,0:T(8,128)(2,1)S(1)}, bf16[4,128,128]{2,1,0:T(8,128)(2,1)S(1)}, u32[]{:S(2)}, u32[]{:S(2)}) collective-permute-start(bf16[4,128,128]{2,1,0:T(8,128)(2,1)S(1)} %collective-permute-done.18.refs_7_), channel_id=1, source_target_pairs={{0,1},{1,0},{2,3},{3,2},{4,5},{5,4},{6,7},{7,6},{8,9},{9,8},{10,11... | collective-permute-start | bytes 393224 | tf_op jit(solution)/shard_map/ppermute | solution.py:18
  63.2 7.3 %collective-permute-start.28 = (bf16[4,128,128]{2,1,0:T(8,128)(2,1)S(1)}, bf16[4,128,128]{2,1,0:T(8,128)(2,1)S(1)}, u32[]{:S(2)}, u32[]{:S(2)}) collective-permute-start(bf16[4,128,128]{2,1,0:T(8,128)(2,1)S(1)} %collective-permute-done.26.refs_15_), channel_id=1, source_target_pairs={{0,2},{1,3},{2,0},{3,1},{4,6},{5,7},{6,4},{7,5},{8,10},{9,11},{10,... | collective-permute-start | bytes 393224 | tf_op jit(solution)/shard_map/ppermute | solution.py:18
  64.1 6.3 %copy-start.19 = (f32[64,256]{1,0:T(8,128)}, f32[64,256]{1,0:T(8,128)S(1)}, u32[]{:S(2)}) copy-start(f32[64,256]{1,0:T(8,128)S(1)} %add.20) | copy-start | bytes 196612
  65.7 3.3 %collective-permute-start.34 = (f32[64,256]{1,0:T(8,128)S(1)}, f32[64,256]{1,0:T(8,128)S(1)}, u32[]{:S(2)}, u32[]{:S(2)}) collective-permute-start(f32[64,256]{1,0:T(8,128)S(1)} %add.20), channel_id=1, source_target_pairs={{0,1},{1,0},{2,3},{3,2},{4,5},{5,4},{6,7},{7,6},{8,9},{9,8},{10,11... | collective-permute-start | bytes 196616 | tf_op jit(solution)/shard_map/ppermute | solution.py:18
  65.7 6.4 %collective-permute-start.17 = (bf16[4,128,128]{2,1,0:T(8,128)(2,1)S(1)}, bf16[4,128,128]{2,1,0:T(8,128)(2,1)}, u32[]{:S(2)}, u32[]{:S(2)}) collective-permute-start(bf16[4,128,128]{2,1,0:T(8,128)(2,1)S(1)} %collective-permute-done.16.refs_5_), channel_id=1, source_target_pairs={{0,1},{1,0},{2,3},{3,2},{4,5},{5,4},{6,7},{7,6},{8,9},{9,8},{10,11... | collective-permute-start | bytes 393224 | tf_op jit(solution)/shard_map/ppermute | solution.py:18
  68.5 3.6 %collective-permute-start.27 = (bf16[4,128,128]{2,1,0:T(8,128)(2,1)S(1)}, bf16[4,128,128]{2,1,0:T(8,128)(2,1)}, u32[]{:S(2)}, u32[]{:S(2)}) collective-permute-start(bf16[4,128,128]{2,1,0:T(8,128)(2,1)S(1)} %collective-permute-done.26.refs_15_), channel_id=1, source_target_pairs={{0,1},{1,0},{2,3},{3,2},{4,5},{5,4},{6,7},{7,6},{8,9},{9,8},{10,11... | collective-permute-start | bytes 393224 | tf_op jit(solution)/shard_map/ppermute | solution.py:18
  68.5 3.6 %collective-permute-start.25 = (bf16[4,128,128]{2,1,0:T(8,128)(2,1)S(1)}, bf16[4,128,128]{2,1,0:T(8,128)(2,1)}, u32[]{:S(2)}, u32[]{:S(2)}) collective-permute-start(bf16[4,128,128]{2,1,0:T(8,128)(2,1)S(1)} %collective-permute-done.24.refs_13_), channel_id=1, source_target_pairs={{0,1},{1,0},{2,3},{3,2},{4,5},{5,4},{6,7},{7,6},{8,9},{9,8},{10,11... | collective-permute-start | bytes 393224 | tf_op jit(solution)/shard_map/ppermute | solution.py:18
  69.0 1.5 %copy-start.20 = (f32[64,256]{1,0:T(8,128)}, f32[64,256]{1,0:T(8,128)S(1)}, u32[]{:S(2)}) copy-start(f32[64,256]{1,0:T(8,128)S(1)} %collective-permute-done.34) | copy-start | bytes 196612
  69.0 3.1 %collective-permute-start.21 = (bf16[4,128,128]{2,1,0:T(8,128)(2,1)S(1)}, bf16[4,128,128]{2,1,0:T(8,128)(2,1)}, u32[]{:S(2)}, u32[]{:S(2)}) collective-permute-start(bf16[4,128,128]{2,1,0:T(8,128)(2,1)S(1)} %collective-permute-done.20.refs_9_), channel_id=1, source_target_pairs={{0,1},{1,0},{2,3},{3,2},{4,5},{5,4},{6,7},{7,6},{8,9},{9,8},{10,11... | collective-permute-start | bytes 393224 | tf_op jit(solution)/shard_map/ppermute | solution.py:18
  70.4 1.7 %collective-permute-start.29 = (bf16[4,128,128]{2,1,0:T(8,128)(2,1)S(1)}, bf16[4,128,128]{2,1,0:T(8,128)(2,1)}, u32[]{:S(2)}, u32[]{:S(2)}) collective-permute-start(bf16[4,128,128]{2,1,0:T(8,128)(2,1)S(1)} %collective-permute-done.28.refs_17_), channel_id=1, source_target_pairs={{0,1},{1,0},{2,3},{3,2},{4,5},{5,4},{6,7},{7,6},{8,9},{9,8},{10,11... | collective-permute-start | bytes 393224 | tf_op jit(solution)/shard_map/ppermute | solution.py:18

commit v2 on v1

--- a/solution.py
+++ b/solution.py
@@ -8,40 +8,76 @@
 GROUP = 4
 GELU_C = 0.7978845608028654
 GELU_A = 0.044715
+PARAMS = pltpu.CompilerParams(vmem_limit_bytes=12 * 2**20)
+SMEM = pl.BlockSpec(memory_space=pltpu.SMEM)
+VMEM = pl.BlockSpec(memory_space=pltpu.VMEM)
 
 
 def in_vmem(x):
     return pltpu.with_memory_space_constraint(x, pltpu.VMEM)
 
 
+def stage(*arrays):
+    n = len(arrays)
+
+    def kernel(*refs):
+        sems = refs[2 * n]
+        copies = [
+            pltpu.make_async_copy(refs[i], refs[n + i], sems.at[i]) for i in range(n)
+        ]
+        for c in copies:
+            c.start()
+        for c in copies:
+            c.wait()
+
+    return pl.pallas_call(
+        kernel,
+        name="stage",
+        compiler_params=PARAMS,
+        out_shape=tuple(pltpu.VMEM(a.shape, a.dtype) for a in arrays),
+        in_specs=[pl.BlockSpec(memory_space=pltpu.HBM)] * n,
+        out_specs=(VMEM,) * n,
+        scratch_shapes=[pltpu.SemaphoreType.DMA((n,))],
+    )(*(pltpu.with_memory_space_constraint(a, pltpu.HBM) for a in arrays))
+
+
 def exchange(x, bit, size):
     return lax.ppermute(x, "row", [(i, i ^ bit) for i in range(size)])
 
 
-def gather_rows(x, size):
+def after(x, *others):
+    return lax.optimization_barrier((x, *others))[0]
+
+
+def gather_rows(x, own, size, staged=None):
     if size != 16:
         return [(None, lax.all_gather(x, "row", axis=0, tiled=True))]
     held = {0: x}
     held[8] = exchange(x, 8, size)
     held[4] = exchange(x, 4, size)
-    held[12] = exchange(held[8], 4, size)
+    far = held[8] if staged is None else after(held[8], staged)
+    held[12] = exchange(far, 4, size)
     for mask in (0, 4, 8, 12):
         held[mask ^ 2] = exchange(held[mask], 2, size)
     for mask in (0, 2, 4, 6, 8, 10, 12, 14):
         held[mask ^ 1] = exchange(held[mask], 1, size)
+    held[0] = own
     return sorted(held.items())
 
 
-def row_sum(keep, send, core, size):
+def row_sum(keep, send, held, size):
+    held = dict(held)
     total = keep + exchange(send, 1, size)
-    bit = size // 2
-    while bit > 1:
-        total = total + exchange(total, bit, size)
-        bit //= 2
-    other = exchange(total, 1, size)
-    return jnp.where(
-        core == 0, jnp.concatenate([total, other], 0), jnp.concatenate([other, total], 0)
-    )
+    if size == 16:
+        total = total + exchange(after(total, held[4]), 2, size)
+        total = total + exchange(total, 4, size)
+        total = total + exchange(after(total, held[8]), 8, size)
+    else:
+        bit = size // 2
+        while bit > 1:
+            total = total + exchange(total, bit, size)
+            bit //= 2
+    return total, exchange(total, 1, size)
 
 
 def collect(me, masks, pieces, nodes):
@@ -86,12 +122,13 @@
 
 def forward_kernel(masks, *refs):
     n = len(masks)
-    me, cols, counts = refs[:3]
-    pieces = refs[3 : 3 + n]
-    vals, weight, out_grad = refs[3 + n : 6 + n]
-    hidden, edge, keep, send = refs[6 + n : 10 + n]
-    wsum = refs[10 + n]
-    nodes = collect(me[0], masks, pieces, refs[11 + n] if n > 1 else None)
+    cols, counts = refs[:2]
+    pieces = refs[2 : 2 + n]
+    vals, weight, out_grad = refs[2 + n : 5 + n]
+    hidden, edge, keep, send = refs[5 + n : 9 + n]
+    wsum = refs[9 + n]
+    me = lax.axis_index("row")
+    nodes = collect(me, masks, pieces, refs[10 + n] if n > 1 else None)
     panels, _, side, _ = vals.shape
     half = keep.shape[0]
     w = weight[...]
@@ -114,27 +151,27 @@
             + dot(agg_h, dz_l, ((0,), (0,)))
         )
         wsum[...] = part if panel == 0 else wsum[...] + part
-    core = me[0] % 2
+    core = me % 2
     keep[...] = wsum[pl.ds(pl.multiple_of(core * half, half), half), :]
     send[...] = wsum[pl.ds(pl.multiple_of((1 - core) * half, half), half), :]
 
 
 def backward_kernel(masks, *refs):
     n = len(masks)
-    me, cols, counts = refs[:3]
-    pieces = refs[3 : 3 + n]
-    vals = refs[3 + n]
-    feat = refs[4 + n]
-    nodes = collect(me[0], masks, pieces, refs[5 + n] if n > 1 else None)
+    cols, counts = refs[:2]
+    pieces = refs[2 : 2 + n]
+    vals, own, other = refs[2 + n : 5 + n]
+    feat, weight_grad = refs[5 + n : 7 + n]
+    me = lax.axis_index("row")
+    half = own.shape[0]
+    core = me % 2
+    weight_grad[pl.ds(pl.multiple_of(core * half, half), half), :] = own[...]
+    weight_grad[pl.ds(pl.multiple_of((1 - core) * half, half), half), :] = other[...]
+    nodes = collect(me, masks, pieces, refs[7 + n] if n > 1 else None)
     panels, _, side, _ = vals.shape
     for panel in range(panels):
         rows = pl.ds(panel * side, side)
         feat[rows, :] = panel_product(cols, counts, vals, nodes, panel).astype(jnp.bfloat16)
-
-
-PARAMS = pltpu.CompilerParams(vmem_limit_bytes=12 * 2**20)
-SMEM = pl.BlockSpec(memory_space=pltpu.SMEM)
-VMEM = pl.BlockSpec(memory_space=pltpu.VMEM)
 
 
 def body(features, weight, block_cols, block_counts, block_vals, out_grad):
@@ -143,17 +180,17 @@
     rows, width = features.shape
     hidden_width = weight.shape[1]
     node_blocks = size * panels
-    me = lax.axis_index("row").astype(jnp.int32).reshape(1)
-    vals = in_vmem(block_vals)
-
-    def gathered(x):
-        held = gather_rows(x.reshape(panels, side, width), size)
+    features_in = features.reshape(panels, side, width)
+    vals, out_grad, weight, own_rows = stage(block_vals, out_grad, weight, features_in)
+
+    def gathered(x, own, staged=None):
+        held = gather_rows(x, own, size, staged)
         scratch = []
         if len(held) > 1:
             scratch = [pltpu.VMEM((node_blocks, side, width), jnp.bfloat16)]
-        return tuple(m for m, _ in held), [in_vmem(a) for _, a in held], scratch
-
-    masks, pieces, scratch = gathered(features)
+        return held, tuple(m for m, _ in held), [in_vmem(a) for _, a in held], scratch
+
+    held, masks, pieces, scratch = gathered(features_in, own_rows, own_rows)
     hidden, edge, keep, send = pl.pallas_call(
         lambda *refs: forward_kernel(masks, *refs),
         name="forward",
@@ -164,22 +201,25 @@
             jax.ShapeDtypeStruct((width // 2, hidden_width), jnp.float32),
             jax.ShapeDtypeStruct((width // 2, hidden_width), jnp.float32),
         ),
-        in_specs=[SMEM] * 3 + [VMEM] * (len(pieces) + 3),
+        in_specs=[SMEM] * 2 + [VMEM] * (len(pieces) + 3),
         out_specs=(VMEM,) * 4,
         scratch_shapes=[pltpu.VMEM((width, hidden_width), jnp.float32)] + scratch,
-    )(me, block_cols, block_counts, *pieces, vals, in_vmem(weight), in_vmem(out_grad))
-
-    masks, pieces, scratch = gathered(edge)
-    feat_grad = pl.pallas_call(
+    )(block_cols, block_counts, *pieces, in_vmem(vals), in_vmem(weight), in_vmem(out_grad))
+
+    held, masks, pieces, scratch = gathered(edge, edge)
+    own, other = row_sum(keep, send, held, size)
+    feat_grad, weight_grad = pl.pallas_call(
         lambda *refs: backward_kernel(masks, *refs),
         name="backward",
         compiler_params=PARAMS,
-        out_shape=jax.ShapeDtypeStruct((rows, width), jnp.bfloat16),
-        in_specs=[SMEM] * 3 + [VMEM] * (len(pieces) + 1),
-        out_specs=VMEM,
+        out_shape=(
+            jax.ShapeDtypeStruct((rows, width), jnp.bfloat16),
+            jax.ShapeDtypeStruct((width, hidden_width), jnp.float32),
+        ),
+        in_specs=[SMEM] * 2 + [VMEM] * (len(pieces) + 3),
+        out_specs=(VMEM, VMEM),
         scratch_shapes=scratch,
-    )(me, block_cols, block_counts, *pieces, vals)
-    weight_grad = row_sum(keep, send, me[0] % 2, size)
+    )(block_cols, block_counts, *pieces, in_vmem(vals), in_vmem(own), in_vmem(other))
     return hidden, feat_grad, weight_grad
 
 

time: 76.1 us -> 59.2 us (0.78); the launches traced: 75.4 us -> 59.7 us
  local copies, waits for them, and re-layouts: 13.4 us -> 0.01 us
  waiting for transfers between devices: 24.8 us -> 20.3 us
  Pallas kernels: 7.62 us -> 10.9 us
  other arithmetic: 1.65 us -> 0.04 us
    unnamed x42 -> x4, local copies, waits for them, and re-layouts: 13.4 us -> 0.01 us
    ppermute x35, waiting for transfers between devices: 24.8 us -> 20.3 us  [exchange(): return lax.ppermute(x, 'row', [(i, i ^ bit) for i in range(size)])]
    pallas_call x0 -> x1, Pallas kernels: none -> 1.67 us  [stage(): pl.pallas_call(kernel, name='stage', compiler_params=PARAMS, out_shape=tu...]
    select_n x1 -> x0, other arithmetic: 1.61 us -> none  [row_sum(): jnp.where(core == 0, jnp.concatenate([total, other], 0), jnp.concatenate(...]
    pallas_call x1, Pallas kernels: 4.31 us -> 5.4 us  [body(): pl.pallas_call(lambda *refs: forward_kernel(masks, *refs), name='forward'...]
  transfers between devices with their start and end apart: 35 -> 35, of which waited for: 10 -> 10; matrix products, arithmetic and copies ran while one was open for 2% -> 0% of each run, Pallas kernels for 0% -> 3%
where the time goes in v2:
time: 59.2 us; the launch traced here: 59.7 us
  starting transfers between devices  27.7 us (47%)
  waiting for transfers between devices  20.3 us (34%)
  Pallas kernels  10.9 us (18%)
  between operations  0.76 us (1%)
    ppermute x35, starting transfers between devices, exchange(): return lax.ppermute(x, 'row', [(i, i ^ bit) for i in range(size)])  27.7 us
    ppermute x35, waiting for transfers between devices, exchange(): return lax.ppermute(x, 'row', [(i, i ^ bit) for i in range(size)])  20.3 us
    pallas_call x1, Pallas kernels, body(): pl.pallas_call(lambda *refs: forward_kernel(masks, *refs), name='forward'...  5.4 us
    pallas_call x1, Pallas kernels, body(): pl.pallas_call(lambda *refs: backward_kernel(masks, *refs), name='backwar...  3.84 us
    pallas_call x1, Pallas kernels, stage(): pl.pallas_call(kernel, name='stage', compiler_params=PARAMS, out_shape=tu...  1.67 us
  transfers between devices with their start and end apart: 35, of which 10 were waited for; matrix products, arithmetic and copies ran while one was open for 0% of the time, Pallas kernels for 3%

profile of v2, /device:TPU:0, one launch (start us, length us, event | category | flops | bytes accessed | tf_op | source)
XLA Modules:
  0.0 59.7 jit_solution(9829466893721838757)
XLA Ops:
  0.7 4.1 %collective-permute-start.7 = (bf16[4,128,128]{2,1,0:T(8,128)(2,1)}, bf16[4,128,128]{2,1,0:T(8,128)(2,1)S(1)}, u32[]{:S(2)}, u32[]{:S(2)}) collective-permute-start(bf16[4,128,128]{2,1,0:T(8,128)(2,1)} %bitcast.1), channel_id=1, source_target_pairs={{0,8},{1,9},{2,10},{3,11},{4,12},{5,13},{6,14},{7,15},{8,0},{9,1},... | collective-permute-start | bytes 393224 | tf_op jit(solution)/shard_map/ppermute | solution.py:45
  4.8 1.6 %collective-permute-start.3 = (bf16[4,128,128]{2,1,0:T(8,128)(2,1)}, bf16[4,128,128]{2,1,0:T(8,128)(2,1)S(1)}, u32[]{:S(2)}, u32[]{:S(2)}) collective-permute-start(bf16[4,128,128]{2,1,0:T(8,128)(2,1)} %bitcast.2), channel_id=1, source_target_pairs={{0,4},{1,5},{2,6},{3,7},{4,0},{5,1},{6,2},{7,3},{8,12},{9,13},{10,... | collective-permute-start | bytes 393224 | tf_op jit(solution)/shard_map/ppermute | solution.py:45
  6.3 1.5 %collective-permute-start.1 = (bf16[4,128,128]{2,1,0:T(8,128)(2,1)}, bf16[4,128,128]{2,1,0:T(8,128)(2,1)S(1)}, u32[]{:S(2)}, u32[]{:S(2)}) collective-permute-start(bf16[4,128,128]{2,1,0:T(8,128)(2,1)} %bitcast.3), channel_id=1, source_target_pairs={{0,2},{1,3},{2,0},{3,1},{4,6},{5,7},{6,4},{7,5},{8,10},{9,11},{10,... | collective-permute-start | bytes 393224 | tf_op jit(solution)/shard_map/ppermute | solution.py:45
  7.9 0.0 collective-permute-start
  7.9 1.7 %stage.1 = (bf16[4,16,128,128]{3,2,1,0:T(8,128)(2,1)S(1)}, bf16[512,256]{1,0:T(8,128)(2,1)S(1)}, bf16[128,256]{1,0:T(8,128)(2,1)S(1)}, bf16[4,128,128]{2,1,0:T(8,128)(2,1)S(1)}) custom-call(bf16[4,16,128,128]{3,2,1,0:T(8,128)(2,1)} %refs_0_.3, bf16[512,256]{1,0:T(8,128)(2,1)} %refs_1_.3, bf16[128,256]{1,0:T(8,128)(2,1)} %refs_2_.1, bf16[4,128,128]{2,1,0:T(8,128)(2,1)} %bitcast.5), custom_call_target="tpu_custom_call" | custom-call | tf_op jit(solution)/shard_map/stage/pallas_call | solution.py:33
  9.5 1.8 %collective-permute-done.7.refs_10_ = bf16[4,128,128]{2,1,0:T(8,128)(2,1)S(1)} collective-permute-done((bf16[4,128,128]{2,1,0:T(8,128)(2,1)}, bf16[4,128,128]{2,1,0:T(8,128)(2,1)S(1)}, u32[]{:S(2)}, u32[]{:S(2)}) %collective-permute-start.7) | collective-permute-done | bytes 131104 | tf_op jit(solution)/shard_map/ppermute | solution.py:45
  11.4 0.7 %collective-permute-start.11 = (bf16[4,128,128]{2,1,0:T(8,128)(2,1)S(1)}, bf16[4,128,128]{2,1,0:T(8,128)(2,1)S(1)}, u32[]{:S(2)}, u32[]{:S(2)}) collective-permute-start(bf16[4,128,128]{2,1,0:T(8,128)(2,1)S(1)} %collective-permute-done.7.refs_10_), channel_id=1, source_target_pairs={{0,4},{1,5},{2,6},{3,7},{4,0},{5,1},{6,2},{7,3},{8,12},{9,13},{10,... | collective-permute-start | bytes 393224 | tf_op jit(solution)/shard_map/ppermute | solution.py:45
  12.1 1.5 %collective-permute-start.9 = (bf16[4,128,128]{2,1,0:T(8,128)(2,1)S(1)}, bf16[4,128,128]{2,1,0:T(8,128)(2,1)S(1)}, u32[]{:S(2)}, u32[]{:S(2)}) collective-permute-start(bf16[4,128,128]{2,1,0:T(8,128)(2,1)S(1)} %collective-permute-done.7.refs_10_), channel_id=1, source_target_pairs={{0,2},{1,3},{2,0},{3,1},{4,6},{5,7},{6,4},{7,5},{8,10},{9,11},{10,... | collective-permute-start | bytes 393224 | tf_op jit(solution)/shard_map/ppermute | solution.py:45
  13.6 0.0 collective-permute-done.3.refs_6_
  13.6 0.0 collective-permute-start.8
  13.6 0.0 collective-permute-done.1.refs_4_
  13.6 0.6 collective-permute-start.5
  14.2 0.0 collective-permute-done.refs_3_
  14.2 0.2 collective-permute-start.4
  14.4 2.0 %collective-permute-done.11.refs_14_ = bf16[4,128,128]{2,1,0:T(8,128)(2,1)S(1)} collective-permute-done((bf16[4,128,128]{2,1,0:T(8,128)(2,1)S(1)}, bf16[4,128,128]{2,1,0:T(8,128)(2,1)S(1)}, u32[]{:S(2)}, u32[]{:S(2)}) %collective-permute-start.11) | collective-permute-done | bytes 131104 | tf_op jit(solution)/shard_map/ppermute | solution.py:45
  16.3 1.6 %collective-permute-start.13 = (bf16[4,128,128]{2,1,0:T(8,128)(2,1)S(1)}, bf16[4,128,128]{2,1,0:T(8,128)(2,1)S(1)}, u32[]{:S(2)}, u32[]{:S(2)}) collective-permute-start(bf16[4,128,128]{2,1,0:T(8,128)(2,1)S(1)} %collective-permute-done.11.refs_14_), channel_id=1, source_target_pairs={{0,2},{1,3},{2,0},{3,1},{4,6},{5,7},{6,4},{7,5},{8,10},{9,11},{10,... | collective-permute-start | bytes 393224 | tf_op jit(solution)/shard_map/ppermute | solution.py:45
  17.9 0.0 collective-permute-done.9.refs_12_
  17.9 0.0 collective-permute-start.2
  17.9 0.0 collective-permute-done.8.refs_11_
  17.9 0.5 collective-permute-start.12
  18.4 2.1 %collective-permute-done.5.refs_8_ = bf16[4,128,128]{2,1,0:T(8,128)(2,1)S(1)} collective-permute-done((bf16[4,128,128]{2,1,0:T(8,128)(2,1)S(1)}, bf16[4,128,128]{2,1,0:T(8,128)(2,1)S(1)}, u32[]{:S(2)}, u32[]{:S(2)}) %collective-permute-start.5) | collective-permute-done | bytes 131104 | tf_op jit(solution)/shard_map/ppermute | solution.py:45
  20.6 0.5 collective-permute-start.6
  21.1 1.8 %collective-permute-done.13.refs_16_ = bf16[4,128,128]{2,1,0:T(8,128)(2,1)S(1)} collective-permute-done((bf16[4,128,128]{2,1,0:T(8,128)(2,1)S(1)}, bf16[4,128,128]{2,1,0:T(8,128)(2,1)S(1)}, u32[]{:S(2)}, u32[]{:S(2)}) %collective-permute-start.13) | collective-permute-done | bytes 131104 | tf_op jit(solution)/shard_map/ppermute | solution.py:45
  22.9 0.0 collective-permute-start.14
  22.9 0.0 collective-permute-done.2.refs_5_
  22.9 0.0 collective-permute-done.10.refs_13_
  22.9 0.0 collective-permute-done.6.refs_9_
  22.9 0.0 collective-permute-done.12.refs_15_
  22.9 1.3 %collective-permute-done.14.refs_17_ = bf16[4,128,128]{2,1,0:T(8,128)(2,1)S(1)} collective-permute-done((bf16[4,128,128]{2,1,0:T(8,128)(2,1)S(1)}, bf16[4,128,128]{2,1,0:T(8,128)(2,1)S(1)}, u32[]{:S(2)}, u32[]{:S(2)}) %collective-permute-start.14) | collective-permute-done | bytes 131104 | tf_op jit(solution)/shard_map/ppermute | solution.py:45
  24.2 5.4 %forward.1 = (bf16[512,256]{1,0:T(8,128)(2,1)}, bf16[4,128,128]{2,1,0:T(8,128)(2,1)S(1)}, f32[64,256]{1,0:T(8,128)S(1)}, f32[64,256]{1,0:T(8,128)S(1)}) custom-call(s32[4,16]{1,0:T(4,128)S(1)} %copy-done, s32[4]{0:T(128)S(1)} %copy-done.1, bf16[4,128,128]{2,1,0:T(8,128)(2,1)S(1)} %get-tuple-element.16.refs_2_, ...), custom_call_target="tpu_custom_call" | custom-call | tf_op jit(solution)/shard_map/forward/pallas_call | solution.py:194
  29.6 0.9 %collective-permute-start.18 = (bf16[4,128,128]{2,1,0:T(8,128)(2,1)S(1)}, bf16[4,128,128]{2,1,0:T(8,128)(2,1)S(1)}, u32[]{:S(2)}, u32[]{:S(2)}) collective-permute-start(bf16[4,128,128]{2,1,0:T(8,128)(2,1)S(1)} %get-tuple-element.22.refs_2_), channel_id=1, source_target_pairs={{0,4},{1,5},{2,6},{3,7},{4,0},{5,1},{6,2},{7,3},{8,12},{9,13},{10,... | collective-permute-start | bytes 393224 | tf_op jit(solution)/shard_map/ppermute | solution.py:45
  30.5 2.3 %collective-permute-start.22 = (bf16[4,128,128]{2,1,0:T(8,128)(2,1)S(1)}, bf16[4,128,128]{2,1,0:T(8,128)(2,1)S(1)}, u32[]{:S(2)}, u32[]{:S(2)}) collective-permute-start(bf16[4,128,128]{2,1,0:T(8,128)(2,1)S(1)} %get-tuple-element.22.refs_2_), channel_id=1, source_target_pairs={{0,8},{1,9},{2,10},{3,11},{4,12},{5,13},{6,14},{7,15},{8,0},{9,1},... | collective-permute-start | bytes 393224 | tf_op jit(solution)/shard_map/ppermute | solution.py:45
  32.8 0.7 %collective-permute-start.16 = (bf16[4,128,128]{2,1,0:T(8,128)(2,1)S(1)}, bf16[4,128,128]{2,1,0:T(8,128)(2,1)S(1)}, u32[]{:S(2)}, u32[]{:S(2)}) collective-permute-start(bf16[4,128,128]{2,1,0:T(8,128)(2,1)S(1)} %get-tuple-element.22.refs_2_), channel_id=1, source_target_pairs={{0,2},{1,3},{2,0},{3,1},{4,6},{5,7},{6,4},{7,5},{8,10},{9,11},{10,... | collective-permute-start | bytes 393224 | tf_op jit(solution)/shard_map/ppermute | solution.py:45
  33.4 0.6 collective-permute-done.30
  34.0 2.1 %collective-permute-done.18.refs_6_ = bf16[4,128,128]{2,1,0:T(8,128)(2,1)S(1)} collective-permute-done((bf16[4,128,128]{2,1,0:T(8,128)(2,1)S(1)}, bf16[4,128,128]{2,1,0:T(8,128)(2,1)S(1)}, u32[]{:S(2)}, u32[]{:S(2)}) %collective-permute-start.18) | collective-permute-done | bytes 131104 | tf_op jit(solution)/shard_map/ppermute | solution.py:45
  36.1 2.4 %collective-permute-start.31 = (f32[64,256]{1,0:T(8,128)S(1)}, f32[64,256]{1,0:T(8,128)S(1)}, u32[]{:S(2)}, u32[]{:S(2)}) collective-permute-start(f32[64,256]{1,0:T(8,128)S(1)} %add.12), channel_id=1, source_target_pairs={{0,2},{1,3},{2,0},{3,1},{4,6},{5,7},{6,4},{7,5},{8,10},{9,11},{10,... | collective-permute-start | bytes 196616 | tf_op jit(solution)/shard_map/ppermute | solution.py:45
  38.5 0.0 collective-permute-start.15
  38.5 0.0 collective-permute-done.22.refs_10_
  38.5 1.3 %collective-permute-start.26 = (bf16[4,128,128]{2,1,0:T(8,128)(2,1)S(1)}, bf16[4,128,128]{2,1,0:T(8,128)(2,1)S(1)}, u32[]{:S(2)}, u32[]{:S(2)}) collective-permute-start(bf16[4,128,128]{2,1,0:T(8,128)(2,1)S(1)} %collective-permute-done.22.refs_10_), channel_id=1, source_target_pairs={{0,4},{1,5},{2,6},{3,7},{4,0},{5,1},{6,2},{7,3},{8,12},{9,13},{10,... | collective-permute-start | bytes 393224 | tf_op jit(solution)/shard_map/ppermute | solution.py:45
  39.8 1.5 %collective-permute-start.24 = (bf16[4,128,128]{2,1,0:T(8,128)(2,1)S(1)}, bf16[4,128,128]{2,1,0:T(8,128)(2,1)S(1)}, u32[]{:S(2)}, u32[]{:S(2)}) collective-permute-start(bf16[4,128,128]{2,1,0:T(8,128)(2,1)S(1)} %collective-permute-done.22.refs_10_), channel_id=1, source_target_pairs={{0,2},{1,3},{2,0},{3,1},{4,6},{5,7},{6,4},{7,5},{8,10},{9,11},{10,... | collective-permute-start | bytes 393224 | tf_op jit(solution)/shard_map/ppermute | solution.py:45
  41.3 0.0 collective-permute-done.31
  41.3 0.2 collective-permute-start.32
  41.5 0.0 collective-permute-done.16.refs_4_
  41.5 0.0 collective-permute-start.23
  41.5 0.0 collective-permute-done.15.refs_3_
  41.5 1.5 %collective-permute-start.20 = (bf16[4,128,128]{2,1,0:T(8,128)(2,1)S(1)}, bf16[4,128,128]{2,1,0:T(8,128)(2,1)S(1)}, u32[]{:S(2)}, u32[]{:S(2)}) collective-permute-start(bf16[4,128,128]{2,1,0:T(8,128)(2,1)S(1)} %collective-permute-done.18.refs_6_), channel_id=1, source_target_pairs={{0,2},{1,3},{2,0},{3,1},{4,6},{5,7},{6,4},{7,5},{8,10},{9,11},{10,... | collective-permute-start | bytes 393224 | tf_op jit(solution)/shard_map/ppermute | solution.py:45
  43.0 2.8 %collective-permute-done.32 = f32[64,256]{1,0:T(8,128)S(1)} collective-permute-done((f32[64,256]{1,0:T(8,128)S(1)}, f32[64,256]{1,0:T(8,128)S(1)}, u32[]{:S(2)}, u32[]{:S(2)}) %collective-permute-start.32) | collective-permute-done | bytes 65568 | tf_op jit(solution)/shard_map/ppermute | solution.py:45
  45.8 0.0 collective-permute-start.19
  45.8 0.0 collective-permute-done.26.refs_14_
  45.8 1.3 %collective-permute-start.28 = (bf16[4,128,128]{2,1,0:T(8,128)(2,1)S(1)}, bf16[4,128,128]{2,1,0:T(8,128)(2,1)S(1)}, u32[]{:S(2)}, u32[]{:S(2)}) collective-permute-start(bf16[4,128,128]{2,1,0:T(8,128)(2,1)S(1)} %collective-permute-done.26.refs_14_), channel_id=1, source_target_pairs={{0,2},{1,3},{2,0},{3,1},{4,6},{5,7},{6,4},{7,5},{8,10},{9,11},{10,... | collective-permute-start | bytes 393224 | tf_op jit(solution)/shard_map/ppermute | solution.py:45
  47.1 0.3 collective-permute-start.17
  47.4 0.0 collective-permute-done.23.refs_11_
  47.4 1.6 %collective-permute-start.33 = (f32[64,256]{1,0:T(8,128)S(1)}, f32[64,256]{1,0:T(8,128)S(1)}, u32[]{:S(2)}, u32[]{:S(2)}) collective-permute-start(f32[64,256]{1,0:T(8,128)S(1)} %add.14), channel_id=1, source_target_pairs={{0,8},{1,9},{2,10},{3,11},{4,12},{5,13},{6,14},{7,15},{8,0},{9,1},... | collective-permute-start | bytes 196616 | tf_op jit(solution)/shard_map/ppermute | solution.py:45
  49.0 0.0 collective-permute-start.27
  49.0 0.5 collective-permute-start.25
  49.5 4.5 %collective-permute-done.33 = f32[64,256]{1,0:T(8,128)S(1)} collective-permute-done((f32[64,256]{1,0:T(8,128)S(1)}, f32[64,256]{1,0:T(8,128)S(1)}, u32[]{:S(2)}, u32[]{:S(2)}) %collective-permute-start.33) | collective-permute-done | bytes 65568 | tf_op jit(solution)/shard_map/ppermute | solution.py:45
  54.0 0.0 collective-permute-start.21
  54.0 0.5 collective-permute-start.29
  54.5 0.1 collective-permute-start.34
  54.6 0.0 collective-permute-done.27.refs_15_
  54.6 1.2 %collective-permute-done.34.refs_20_ = f32[64,256]{1,0:T(8,128)S(1)} collective-permute-done((f32[64,256]{1,0:T(8,128)S(1)}, f32[64,256]{1,0:T(8,128)S(1)}, u32[]{:S(2)}, u32[]{:S(2)}) %collective-permute-start.34) | collective-permute-done | bytes 65568 | tf_op jit(solution)/shard_map/ppermute | solution.py:45
  55.9 0.0 collective-permute-done.21.refs_9_
  55.9 0.0 collective-permute-done.29.refs_17_
  55.9 3.8 %backward.1 = (bf16[512,128]{1,0:T(8,128)(2,1)}, f32[128,256]{1,0:T(8,128)}) custom-call(s32[4,16]{1,0:T(4,128)S(1)} %copy-done, s32[4]{0:T(128)S(1)} %copy-done.1, bf16[4,128,128]{2,1,0:T(8,128)(2,1)S(1)} %get-tuple-element.22.refs_2_, bf16[4,128,128]{2,1,0:T(8,128)(2,1)S(1)} %collective-permute-done.15.refs_3_, ...), custom_call_target="tpu_custom_call" | custom-call | tf_op jit(solution)/shard_map/backward/pallas_call | solution.py:211
  (17 shorter events, 0.1 us)
Async XLA Ops:
  0.6 23.6 %copy-start.1 = (s32[4]{0:T(128)S(1)}, s32[4]{0:T(128)}, u32[]{:S(2)}) copy-start(s32[4]{0:T(128)} %refs_1_.5) | copy-start | bytes 52
  0.6 23.6 %copy-start = (s32[4,16]{1,0:T(4,128)S(1)}, s32[4,16]{1,0:T(4,128)}, u32[]{:S(2)}) copy-start(s32[4,16]{1,0:T(4,128)} %refs_0_.5) | copy-start | bytes 772
  0.7 10.7 %collective-permute-start.7 = (bf16[4,128,128]{2,1,0:T(8,128)(2,1)}, bf16[4,128,128]{2,1,0:T(8,128)(2,1)S(1)}, u32[]{:S(2)}, u32[]{:S(2)}) collective-permute-start(bf16[4,128,128]{2,1,0:T(8,128)(2,1)} %bitcast.1), channel_id=1, source_target_pairs={{0,8},{1,9},{2,10},{3,11},{4,12},{5,13},{6,14},{7,15},{8,0},{9,1},... | collective-permute-start | bytes 393224 | tf_op jit(solution)/shard_map/ppermute | solution.py:45
  4.8 8.9 %collective-permute-start.3 = (bf16[4,128,128]{2,1,0:T(8,128)(2,1)}, bf16[4,128,128]{2,1,0:T(8,128)(2,1)S(1)}, u32[]{:S(2)}, u32[]{:S(2)}) collective-permute-start(bf16[4,128,128]{2,1,0:T(8,128)(2,1)} %bitcast.2), channel_id=1, source_target_pairs={{0,4},{1,5},{2,6},{3,7},{4,0},{5,1},{6,2},{7,3},{8,12},{9,13},{10,... | collective-permute-start | bytes 393224 | tf_op jit(solution)/shard_map/ppermute | solution.py:45
  6.3 7.3 %collective-permute-start.1 = (bf16[4,128,128]{2,1,0:T(8,128)(2,1)}, bf16[4,128,128]{2,1,0:T(8,128)(2,1)S(1)}, u32[]{:S(2)}, u32[]{:S(2)}) collective-permute-start(bf16[4,128,128]{2,1,0:T(8,128)(2,1)} %bitcast.3), channel_id=1, source_target_pairs={{0,2},{1,3},{2,0},{3,1},{4,6},{5,7},{6,4},{7,5},{8,10},{9,11},{10,... | collective-permute-start | bytes 393224 | tf_op jit(solution)/shard_map/ppermute | solution.py:45
  7.9 6.4 %collective-permute-start = (bf16[4,128,128]{2,1,0:T(8,128)(2,1)}, bf16[4,128,128]{2,1,0:T(8,128)(2,1)S(1)}, u32[]{:S(2)}, u32[]{:S(2)}) collective-permute-start(bf16[4,128,128]{2,1,0:T(8,128)(2,1)} %bitcast.4), channel_id=1, source_target_pairs={{0,1},{1,0},{2,3},{3,2},{4,5},{5,4},{6,7},{7,6},{8,9},{9,8},{10,11... | collective-permute-start | bytes 393224 | tf_op jit(solution)/shard_map/ppermute | solution.py:45
  11.4 5.0 %collective-permute-start.11 = (bf16[4,128,128]{2,1,0:T(8,128)(2,1)S(1)}, bf16[4,128,128]{2,1,0:T(8,128)(2,1)S(1)}, u32[]{:S(2)}, u32[]{:S(2)}) collective-permute-start(bf16[4,128,128]{2,1,0:T(8,128)(2,1)S(1)} %collective-permute-done.7.refs_10_), channel_id=1, source_target_pairs={{0,4},{1,5},{2,6},{3,7},{4,0},{5,1},{6,2},{7,3},{8,12},{9,13},{10,... | collective-permute-start | bytes 393224 | tf_op jit(solution)/shard_map/ppermute | solution.py:45
  12.1 5.8 %collective-permute-start.9 = (bf16[4,128,128]{2,1,0:T(8,128)(2,1)S(1)}, bf16[4,128,128]{2,1,0:T(8,128)(2,1)S(1)}, u32[]{:S(2)}, u32[]{:S(2)}) collective-permute-start(bf16[4,128,128]{2,1,0:T(8,128)(2,1)S(1)} %collective-permute-done.7.refs_10_), channel_id=1, source_target_pairs={{0,2},{1,3},{2,0},{3,1},{4,6},{5,7},{6,4},{7,5},{8,10},{9,11},{10,... | collective-permute-start | bytes 393224 | tf_op jit(solution)/shard_map/ppermute | solution.py:45
  13.6 4.3 %collective-permute-start.8 = (bf16[4,128,128]{2,1,0:T(8,128)(2,1)S(1)}, bf16[4,128,128]{2,1,0:T(8,128)(2,1)S(1)}, u32[]{:S(2)}, u32[]{:S(2)}) collective-permute-start(bf16[4,128,128]{2,1,0:T(8,128)(2,1)S(1)} %collective-permute-done.7.refs_10_), channel_id=1, source_target_pairs={{0,1},{1,0},{2,3},{3,2},{4,5},{5,4},{6,7},{7,6},{8,9},{9,8},{10,11... | collective-permute-start | bytes 393224 | tf_op jit(solution)/shard_map/ppermute | solution.py:45
  13.6 6.9 %collective-permute-start.5 = (bf16[4,128,128]{2,1,0:T(8,128)(2,1)S(1)}, bf16[4,128,128]{2,1,0:T(8,128)(2,1)S(1)}, u32[]{:S(2)}, u32[]{:S(2)}) collective-permute-start(bf16[4,128,128]{2,1,0:T(8,128)(2,1)S(1)} %collective-permute-done.3.refs_6_), channel_id=1, source_target_pairs={{0,2},{1,3},{2,0},{3,1},{4,6},{5,7},{6,4},{7,5},{8,10},{9,11},{10,... | collective-permute-start | bytes 393224 | tf_op jit(solution)/shard_map/ppermute | solution.py:45
  14.2 6.3 %collective-permute-start.4 = (bf16[4,128,128]{2,1,0:T(8,128)(2,1)S(1)}, bf16[4,128,128]{2,1,0:T(8,128)(2,1)S(1)}, u32[]{:S(2)}, u32[]{:S(2)}) collective-permute-start(bf16[4,128,128]{2,1,0:T(8,128)(2,1)S(1)} %collective-permute-done.3.refs_6_), channel_id=1, source_target_pairs={{0,1},{1,0},{2,3},{3,2},{4,5},{5,4},{6,7},{7,6},{8,9},{9,8},{10,11... | collective-permute-start | bytes 393224 | tf_op jit(solution)/shard_map/ppermute | solution.py:45
  16.3 6.5 %collective-permute-start.13 = (bf16[4,128,128]{2,1,0:T(8,128)(2,1)S(1)}, bf16[4,128,128]{2,1,0:T(8,128)(2,1)S(1)}, u32[]{:S(2)}, u32[]{:S(2)}) collective-permute-start(bf16[4,128,128]{2,1,0:T(8,128)(2,1)S(1)} %collective-permute-done.11.refs_14_), channel_id=1, source_target_pairs={{0,2},{1,3},{2,0},{3,1},{4,6},{5,7},{6,4},{7,5},{8,10},{9,11},{10,... | collective-permute-start | bytes 393224 | tf_op jit(solution)/shard_map/ppermute | solution.py:45
  17.9 4.9 %collective-permute-start.2 = (bf16[4,128,128]{2,1,0:T(8,128)(2,1)S(1)}, bf16[4,128,128]{2,1,0:T(8,128)(2,1)S(1)}, u32[]{:S(2)}, u32[]{:S(2)}) collective-permute-start(bf16[4,128,128]{2,1,0:T(8,128)(2,1)S(1)} %collective-permute-done.1.refs_4_), channel_id=1, source_target_pairs={{0,1},{1,0},{2,3},{3,2},{4,5},{5,4},{6,7},{7,6},{8,9},{9,8},{10,11... | collective-permute-start | bytes 393224 | tf_op jit(solution)/shard_map/ppermute | solution.py:45
  17.9 5.0 %collective-permute-start.12 = (bf16[4,128,128]{2,1,0:T(8,128)(2,1)S(1)}, bf16[4,128,128]{2,1,0:T(8,128)(2,1)S(1)}, u32[]{:S(2)}, u32[]{:S(2)}) collective-permute-start(bf16[4,128,128]{2,1,0:T(8,128)(2,1)S(1)} %collective-permute-done.11.refs_14_), channel_id=1, source_target_pairs={{0,1},{1,0},{2,3},{3,2},{4,5},{5,4},{6,7},{7,6},{8,9},{9,8},{10,11... | collective-permute-start | bytes 393224 | tf_op jit(solution)/shard_map/ppermute | solution.py:45
  20.5 2.3 %collective-permute-start.10 = (bf16[4,128,128]{2,1,0:T(8,128)(2,1)S(1)}, bf16[4,128,128]{2,1,0:T(8,128)(2,1)S(1)}, u32[]{:S(2)}, u32[]{:S(2)}) collective-permute-start(bf16[4,128,128]{2,1,0:T(8,128)(2,1)S(1)} %collective-permute-done.9.refs_12_), channel_id=1, source_target_pairs={{0,1},{1,0},{2,3},{3,2},{4,5},{5,4},{6,7},{7,6},{8,9},{9,8},{10,11... | collective-permute-start | bytes 393224 | tf_op jit(solution)/shard_map/ppermute | solution.py:45
  20.6 2.3 %collective-permute-start.6 = (bf16[4,128,128]{2,1,0:T(8,128)(2,1)S(1)}, bf16[4,128,128]{2,1,0:T(8,128)(2,1)S(1)}, u32[]{:S(2)}, u32[]{:S(2)}) collective-permute-start(bf16[4,128,128]{2,1,0:T(8,128)(2,1)S(1)} %collective-permute-done.5.refs_8_), channel_id=1, source_target_pairs={{0,1},{1,0},{2,3},{3,2},{4,5},{5,4},{6,7},{7,6},{8,9},{9,8},{10,11... | collective-permute-start | bytes 393224 | tf_op jit(solution)/shard_map/ppermute | solution.py:45
  22.9 1.3 %collective-permute-start.14 = (bf16[4,128,128]{2,1,0:T(8,128)(2,1)S(1)}, bf16[4,128,128]{2,1,0:T(8,128)(2,1)S(1)}, u32[]{:S(2)}, u32[]{:S(2)}) collective-permute-start(bf16[4,128,128]{2,1,0:T(8,128)(2,1)S(1)} %collective-permute-done.13.refs_16_), channel_id=1, source_target_pairs={{0,1},{1,0},{2,3},{3,2},{4,5},{5,4},{6,7},{7,6},{8,9},{9,8},{10,11... | collective-permute-start | bytes 393224 | tf_op jit(solution)/shard_map/ppermute | solution.py:45
  29.6 6.5 %collective-permute-start.18 = (bf16[4,128,128]{2,1,0:T(8,128)(2,1)S(1)}, bf16[4,128,128]{2,1,0:T(8,128)(2,1)S(1)}, u32[]{:S(2)}, u32[]{:S(2)}) collective-permute-start(bf16[4,128,128]{2,1,0:T(8,128)(2,1)S(1)} %get-tuple-element.22.refs_2_), channel_id=1, source_target_pairs={{0,4},{1,5},{2,6},{3,7},{4,0},{5,1},{6,2},{7,3},{8,12},{9,13},{10,... | collective-permute-start | bytes 393224 | tf_op jit(solution)/shard_map/ppermute | solution.py:45
  30.5 8.0 %collective-permute-start.22 = (bf16[4,128,128]{2,1,0:T(8,128)(2,1)S(1)}, bf16[4,128,128]{2,1,0:T(8,128)(2,1)S(1)}, u32[]{:S(2)}, u32[]{:S(2)}) collective-permute-start(bf16[4,128,128]{2,1,0:T(8,128)(2,1)S(1)} %get-tuple-element.22.refs_2_), channel_id=1, source_target_pairs={{0,8},{1,9},{2,10},{3,11},{4,12},{5,13},{6,14},{7,15},{8,0},{9,1},... | collective-permute-start | bytes 393224 | tf_op jit(solution)/shard_map/ppermute | solution.py:45
  32.8 1.3 %collective-permute-start.30 = (f32[64,256]{1,0:T(8,128)S(1)}, f32[64,256]{1,0:T(8,128)S(1)}, u32[]{:S(2)}, u32[]{:S(2)}) collective-permute-start(f32[64,256]{1,0:T(8,128)S(1)} %get-tuple-element.24), channel_id=1, source_target_pairs={{0,1},{1,0},{2,3},{3,2},{4,5},{5,4},{6,7},{7,6},{8,9},{9,8},{10,11... | collective-permute-start | bytes 196616 | tf_op jit(solution)/shard_map/ppermute | solution.py:45
  32.8 8.7 %collective-permute-start.16 = (bf16[4,128,128]{2,1,0:T(8,128)(2,1)S(1)}, bf16[4,128,128]{2,1,0:T(8,128)(2,1)S(1)}, u32[]{:S(2)}, u32[]{:S(2)}) collective-permute-start(bf16[4,128,128]{2,1,0:T(8,128)(2,1)S(1)} %get-tuple-element.22.refs_2_), channel_id=1, source_target_pairs={{0,2},{1,3},{2,0},{3,1},{4,6},{5,7},{6,4},{7,5},{8,10},{9,11},{10,... | collective-permute-start | bytes 393224 | tf_op jit(solution)/shard_map/ppermute | solution.py:45
  36.1 5.2 %collective-permute-start.31 = (f32[64,256]{1,0:T(8,128)S(1)}, f32[64,256]{1,0:T(8,128)S(1)}, u32[]{:S(2)}, u32[]{:S(2)}) collective-permute-start(f32[64,256]{1,0:T(8,128)S(1)} %add.12), channel_id=1, source_target_pairs={{0,2},{1,3},{2,0},{3,1},{4,6},{5,7},{6,4},{7,5},{8,10},{9,11},{10,... | collective-permute-start | bytes 196616 | tf_op jit(solution)/shard_map/ppermute | solution.py:45
  38.5 3.0 %collective-permute-start.15 = (bf16[4,128,128]{2,1,0:T(8,128)(2,1)S(1)}, bf16[4,128,128]{2,1,0:T(8,128)(2,1)S(1)}, u32[]{:S(2)}, u32[]{:S(2)}) collective-permute-start(bf16[4,128,128]{2,1,0:T(8,128)(2,1)S(1)} %get-tuple-element.22.refs_2_), channel_id=1, source_target_pairs={{0,1},{1,0},{2,3},{3,2},{4,5},{5,4},{6,7},{7,6},{8,9},{9,8},{10,11... | collective-permute-start | bytes 393224 | tf_op jit(solution)/shard_map/ppermute | solution.py:45
  38.5 7.3 %collective-permute-start.26 = (bf16[4,128,128]{2,1,0:T(8,128)(2,1)S(1)}, bf16[4,128,128]{2,1,0:T(8,128)(2,1)S(1)}, u32[]{:S(2)}, u32[]{:S(2)}) collective-permute-start(bf16[4,128,128]{2,1,0:T(8,128)(2,1)S(1)} %collective-permute-done.22.refs_10_), channel_id=1, source_target_pairs={{0,4},{1,5},{2,6},{3,7},{4,0},{5,1},{6,2},{7,3},{8,12},{9,13},{10,... | collective-permute-start | bytes 393224 | tf_op jit(solution)/shard_map/ppermute | solution.py:45
  39.8 7.4 %collective-permute-start.24 = (bf16[4,128,128]{2,1,0:T(8,128)(2,1)S(1)}, bf16[4,128,128]{2,1,0:T(8,128)(2,1)S(1)}, u32[]{:S(2)}, u32[]{:S(2)}) collective-permute-start(bf16[4,128,128]{2,1,0:T(8,128)(2,1)S(1)} %collective-permute-done.22.refs_10_), channel_id=1, source_target_pairs={{0,2},{1,3},{2,0},{3,1},{4,6},{5,7},{6,4},{7,5},{8,10},{9,11},{10,... | collective-permute-start | bytes 393224 | tf_op jit(solution)/shard_map/ppermute | solution.py:45
  41.3 4.5 %collective-permute-start.32 = (f32[64,256]{1,0:T(8,128)S(1)}, f32[64,256]{1,0:T(8,128)S(1)}, u32[]{:S(2)}, u32[]{:S(2)}) collective-permute-start(f32[64,256]{1,0:T(8,128)S(1)} %add.13), channel_id=1, source_target_pairs={{0,4},{1,5},{2,6},{3,7},{4,0},{5,1},{6,2},{7,3},{8,12},{9,13},{10,... | collective-permute-start | bytes 196616 | tf_op jit(solution)/shard_map/ppermute | solution.py:45
  41.5 5.9 %collective-permute-start.23 = (bf16[4,128,128]{2,1,0:T(8,128)(2,1)S(1)}, bf16[4,128,128]{2,1,0:T(8,128)(2,1)S(1)}, u32[]{:S(2)}, u32[]{:S(2)}) collective-permute-start(bf16[4,128,128]{2,1,0:T(8,128)(2,1)S(1)} %collective-permute-done.22.refs_10_), channel_id=1, source_target_pairs={{0,1},{1,0},{2,3},{3,2},{4,5},{5,4},{6,7},{7,6},{8,9},{9,8},{10,11... | collective-permute-start | bytes 393224 | tf_op jit(solution)/shard_map/ppermute | solution.py:45
  41.5 7.5 %collective-permute-start.20 = (bf16[4,128,128]{2,1,0:T(8,128)(2,1)S(1)}, bf16[4,128,128]{2,1,0:T(8,128)(2,1)S(1)}, u32[]{:S(2)}, u32[]{:S(2)}) collective-permute-start(bf16[4,128,128]{2,1,0:T(8,128)(2,1)S(1)} %collective-permute-done.18.refs_6_), channel_id=1, source_target_pairs={{0,2},{1,3},{2,0},{3,1},{4,6},{5,7},{6,4},{7,5},{8,10},{9,11},{10,... | collective-permute-start | bytes 393224 | tf_op jit(solution)/shard_map/ppermute | solution.py:45
  45.8 3.2 %collective-permute-start.19 = (bf16[4,128,128]{2,1,0:T(8,128)(2,1)S(1)}, bf16[4,128,128]{2,1,0:T(8,128)(2,1)S(1)}, u32[]{:S(2)}, u32[]{:S(2)}) collective-permute-start(bf16[4,128,128]{2,1,0:T(8,128)(2,1)S(1)} %collective-permute-done.18.refs_6_), channel_id=1, source_target_pairs={{0,1},{1,0},{2,3},{3,2},{4,5},{5,4},{6,7},{7,6},{8,9},{9,8},{10,11... | collective-permute-start | bytes 393224 | tf_op jit(solution)/shard_map/ppermute | solution.py:45
  45.8 8.2 %collective-permute-start.28 = (bf16[4,128,128]{2,1,0:T(8,128)(2,1)S(1)}, bf16[4,128,128]{2,1,0:T(8,128)(2,1)S(1)}, u32[]{:S(2)}, u32[]{:S(2)}) collective-permute-start(bf16[4,128,128]{2,1,0:T(8,128)(2,1)S(1)} %collective-permute-done.26.refs_14_), channel_id=1, source_target_pairs={{0,2},{1,3},{2,0},{3,1},{4,6},{5,7},{6,4},{7,5},{8,10},{9,11},{10,... | collective-permute-start | bytes 393224 | tf_op jit(solution)/shard_map/ppermute | solution.py:45
  47.1 7.4 %collective-permute-start.17 = (bf16[4,128,128]{2,1,0:T(8,128)(2,1)S(1)}, bf16[4,128,128]{2,1,0:T(8,128)(2,1)S(1)}, u32[]{:S(2)}, u32[]{:S(2)}) collective-permute-start(bf16[4,128,128]{2,1,0:T(8,128)(2,1)S(1)} %collective-permute-done.16.refs_4_), channel_id=1, source_target_pairs={{0,1},{1,0},{2,3},{3,2},{4,5},{5,4},{6,7},{7,6},{8,9},{9,8},{10,11... | collective-permute-start | bytes 393224 | tf_op jit(solution)/shard_map/ppermute | solution.py:45
  47.4 6.6 %collective-permute-start.33 = (f32[64,256]{1,0:T(8,128)S(1)}, f32[64,256]{1,0:T(8,128)S(1)}, u32[]{:S(2)}, u32[]{:S(2)}) collective-permute-start(f32[64,256]{1,0:T(8,128)S(1)} %add.14), channel_id=1, source_target_pairs={{0,8},{1,9},{2,10},{3,11},{4,12},{5,13},{6,14},{7,15},{8,0},{9,1},... | collective-permute-start | bytes 196616 | tf_op jit(solution)/shard_map/ppermute | solution.py:45
  49.0 5.6 %collective-permute-start.27 = (bf16[4,128,128]{2,1,0:T(8,128)(2,1)S(1)}, bf16[4,128,128]{2,1,0:T(8,128)(2,1)S(1)}, u32[]{:S(2)}, u32[]{:S(2)}) collective-permute-start(bf16[4,128,128]{2,1,0:T(8,128)(2,1)S(1)} %collective-permute-done.26.refs_14_), channel_id=1, source_target_pairs={{0,1},{1,0},{2,3},{3,2},{4,5},{5,4},{6,7},{7,6},{8,9},{9,8},{10,11... | collective-permute-start | bytes 393224 | tf_op jit(solution)/shard_map/ppermute | solution.py:45
  49.0 5.6 %collective-permute-start.25 = (bf16[4,128,128]{2,1,0:T(8,128)(2,1)S(1)}, bf16[4,128,128]{2,1,0:T(8,128)(2,1)S(1)}, u32[]{:S(2)}, u32[]{:S(2)}) collective-permute-start(bf16[4,128,128]{2,1,0:T(8,128)(2,1)S(1)} %collective-permute-done.24.refs_12_), channel_id=1, source_target_pairs={{0,1},{1,0},{2,3},{3,2},{4,5},{5,4},{6,7},{7,6},{8,9},{9,8},{10,11... | collective-permute-start | bytes 393224 | tf_op jit(solution)/shard_map/ppermute | solution.py:45
  54.0 1.9 %collective-permute-start.21 = (bf16[4,128,128]{2,1,0:T(8,128)(2,1)S(1)}, bf16[4,128,128]{2,1,0:T(8,128)(2,1)S(1)}, u32[]{:S(2)}, u32[]{:S(2)}) collective-permute-start(bf16[4,128,128]{2,1,0:T(8,128)(2,1)S(1)} %collective-permute-done.20.refs_8_), channel_id=1, source_target_pairs={{0,1},{1,0},{2,3},{3,2},{4,5},{5,4},{6,7},{7,6},{8,9},{9,8},{10,11... | collective-permute-start | bytes 393224 | tf_op jit(solution)/shard_map/ppermute | solution.py:45
  54.0 1.8 %collective-permute-start.29 = (bf16[4,128,128]{2,1,0:T(8,128)(2,1)S(1)}, bf16[4,128,128]{2,1,0:T(8,128)(2,1)S(1)}, u32[]{:S(2)}, u32[]{:S(2)}) collective-permute-start(bf16[4,128,128]{2,1,0:T(8,128)(2,1)S(1)} %collective-permute-done.28.refs_16_), channel_id=1, source_target_pairs={{0,1},{1,0},{2,3},{3,2},{4,5},{5,4},{6,7},{7,6},{8,9},{9,8},{10,11... | collective-permute-start | bytes 393224 | tf_op jit(solution)/shard_map/ppermute | solution.py:45
  54.5 1.3 %collective-permute-start.34 = (f32[64,256]{1,0:T(8,128)S(1)}, f32[64,256]{1,0:T(8,128)S(1)}, u32[]{:S(2)}, u32[]{:S(2)}) collective-permute-start(f32[64,256]{1,0:T(8,128)S(1)} %add.15.refs_19_), channel_id=1, source_target_pairs={{0,1},{1,0},{2,3},{3,2},{4,5},{5,4},{6,7},{7,6},{8,9},{9,8},{10,11... | collective-permute-start | bytes 196616 | tf_op jit(solution)/shard_map/ppermute | solution.py:45

commit v3 on v2

--- a/solution.py
+++ b/solution.py
@@ -5,7 +5,7 @@
 from jax.experimental.pallas import tpu as pltpu
 from jax.sharding import PartitionSpec as P
 
-GROUP = 4
+GROUP = 2
 GELU_C = 0.7978845608028654
 GELU_A = 0.044715
 PARAMS = pltpu.CompilerParams(vmem_limit_bytes=12 * 2**20)
@@ -57,8 +57,10 @@
     held[4] = exchange(x, 4, size)
     far = held[8] if staged is None else after(held[8], staged)
     held[12] = exchange(far, 4, size)
-    for mask in (0, 4, 8, 12):
-        held[mask ^ 2] = exchange(held[mask], 2, size)
+    held[2] = exchange(x, 2, size)
+    held[6] = exchange(held[2], 4, size)
+    held[10] = exchange(held[8], 2, size)
+    held[14] = exchange(held[12], 2, size)
     for mask in (0, 2, 4, 6, 8, 10, 12, 14):
         held[mask ^ 1] = exchange(held[mask], 1, size)
     held[0] = own
@@ -69,9 +71,9 @@
     held = dict(held)
     total = keep + exchange(send, 1, size)
     if size == 16:
-        total = total + exchange(after(total, held[4]), 2, size)
-        total = total + exchange(total, 4, size)
-        total = total + exchange(after(total, held[8]), 8, size)
+        total = total + exchange(total, 8, size)
+        total = total + exchange(after(total, held[8]), 4, size)
+        total = total + exchange(after(total, held[12]), 2, size)
     else:
         bit = size // 2
         while bit > 1:
@@ -94,22 +96,18 @@
 
 def panel_product(cols, counts, vals, nodes, panel):
     used = counts[panel]
-    side = vals.shape[2]
-
-    def product(b):
-        return jnp.dot(
-            vals[panel, b], nodes[cols[panel, b]], preferred_element_type=jnp.float32
+    slots, side = vals.shape[1:3]
+    none = jnp.zeros((side, side), vals.dtype)
+    total = None
+    for b in range(0, slots, GROUP):
+        group = range(b, b + GROUP)
+        part = jnp.dot(
+            jnp.concatenate([jnp.where(i < used, vals[panel, i], none) for i in group], 1),
+            jnp.concatenate([nodes[cols[panel, i]] for i in group], 0),
+            preferred_element_type=jnp.float32,
         )
-
-    def many(step, total):
-        for j in range(GROUP):
-            total = total + product(step * GROUP + j)
-        return total
-
-    full = used // GROUP
-    total = lax.fori_loop(0, full, many, jnp.zeros((side, nodes.shape[2]), jnp.float32))
-    return lax.fori_loop(full * GROUP, used, lambda b, t: t + product(b), total)
-
+        total = part if total is None else total + part
+    return total
 
 def split(x):
     high = x.astype(jnp.bfloat16)
@@ -132,11 +130,12 @@
     panels, _, side, _ = vals.shape
     half = keep.shape[0]
     w = weight[...]
+    ww = jnp.concatenate([w, w], 0)
     for panel in range(panels):
         rows = pl.ds(panel * side, side)
         agg = panel_product(cols, counts, vals, nodes, panel)
         agg_h, agg_l = split(agg)
-        z = dot(agg_h, w, ((1,), (0,))) + dot(agg_l, w, ((1,), (0,)))
+        z = dot(jnp.concatenate([agg_h, agg_l], 1), ww, ((1,), (0,)))
         zz = z * z
         t = jnp.tanh(z * (GELU_C + (GELU_C * GELU_A) * zz))
         half_up = 0.5 + 0.5 * t
@@ -145,10 +144,10 @@
         dz = out_grad[rows, :].astype(jnp.float32) * slope
         dz_h, dz_l = split(dz)
         edge[panel] = (dot(dz_h, w, ((1,), (1,))) + dot(dz_l, w, ((1,), (1,)))).astype(jnp.bfloat16)
-        part = (
-            dot(agg_h, dz_h, ((0,), (0,)))
-            + dot(agg_l, dz_h, ((0,), (0,)))
-            + dot(agg_h, dz_l, ((0,), (0,)))
+        part = dot(
+            jnp.concatenate([agg_h, agg_l, agg_h], 0),
+            jnp.concatenate([dz_h, dz_h, dz_l], 0),
+            ((0,), (0,)),
         )
         wsum[...] = part if panel == 0 else wsum[...] + part
     core = me % 2
@@ -196,10 +195,10 @@
         name="forward",
         compiler_params=PARAMS,
         out_shape=(
-            jax.ShapeDtypeStruct((rows, hidden_width), jnp.bfloat16),
-            jax.ShapeDtypeStruct((panels, side, width), jnp.bfloat16),
-            jax.ShapeDtypeStruct((width // 2, hidden_width), jnp.float32),
-            jax.ShapeDtypeStruct((width // 2, hidden_width), jnp.float32),
+            pltpu.VMEM((rows, hidden_width), jnp.bfloat16),
+            pltpu.VMEM((panels, side, width), jnp.bfloat16),
+            pltpu.VMEM((width // 2, hidden_width), jnp.float32),
+            pltpu.VMEM((width // 2, hidden_width), jnp.float32),
         ),
         in_specs=[SMEM] * 2 + [VMEM] * (len(pieces) + 3),
         out_specs=(VMEM,) * 4,

time: 59.2 us -> 54 us (0.912); the launches traced: 59.7 us -> 53.9 us
  Pallas kernels: 10.9 us -> 6.83 us
  waiting for transfers between devices: 20.3 us -> 18.3 us
  local copies, waits for them, and re-layouts: 0.01 us -> 0.71 us
  starting transfers between devices: 27.7 us -> 27.1 us
    pallas_call x1, Pallas kernels: 5.4 us -> 3.04 us  [body(): pl.pallas_call(lambda *refs: forward_kernel(masks, *refs), name='forward'...]
    ppermute x35, waiting for transfers between devices: 20.3 us -> 18.3 us  [exchange(): return lax.ppermute(x, 'row', [(i, i ^ bit) for i in range(size)])]
    pallas_call x1, Pallas kernels: 3.84 us -> 2.12 us  [body(): pl.pallas_call(lambda *refs: backward_kernel(masks, *refs), name='backwar...]
    unnamed x4 -> x5, local copies, waits for them, and re-layouts: 0.01 us -> 0.71 us
  transfers between devices with their start and end apart: 35 -> 35, of which waited for: 10 -> 11; matrix products, arithmetic and copies ran while one was open for 0% -> 1% of each run, Pallas kernels for 3% -> 3%
where the time goes in v3:
time: 54 us; the launch traced here: 53.9 us
  starting transfers between devices  27.1 us (50%)
  waiting for transfers between devices  18.3 us (34%)
  Pallas kernels  6.83 us (13%)
  between operations  0.8 us (1%)
  local copies, waits for them, and re-layouts  0.71 us (1%)
    ppermute x35, starting transfers between devices, exchange(): return lax.ppermute(x, 'row', [(i, i ^ bit) for i in range(size)])  27.1 us
    ppermute x35, waiting for transfers between devices, exchange(): return lax.ppermute(x, 'row', [(i, i ^ bit) for i in range(size)])  18.3 us
    pallas_call x1, Pallas kernels, body(): pl.pallas_call(lambda *refs: forward_kernel(masks, *refs), name='forward'...  3.04 us
    pallas_call x1, Pallas kernels, body(): pl.pallas_call(lambda *refs: backward_kernel(masks, *refs), name='backwar...  2.12 us
    pallas_call x1, Pallas kernels, stage(): pl.pallas_call(kernel, name='stage', compiler_params=PARAMS, out_shape=tu...  1.67 us
  transfers between devices with their start and end apart: 35, of which 11 were waited for; matrix products, arithmetic and copies ran while one was open for 1% of the time, Pallas kernels for 3%

profile of v3, /device:TPU:0, one launch (start us, length us, event | category | flops | bytes accessed | tf_op | source)
XLA Modules:
  0.0 53.9 jit_solution(177188521845273479)
XLA Ops:
  0.7 4.1 %collective-permute-start.7 = (bf16[4,128,128]{2,1,0:T(8,128)(2,1)}, bf16[4,128,128]{2,1,0:T(8,128)(2,1)S(1)}, u32[]{:S(2)}, u32[]{:S(2)}) collective-permute-start(bf16[4,128,128]{2,1,0:T(8,128)(2,1)} %bitcast.1), channel_id=1, source_target_pairs={{0,8},{1,9},{2,10},{3,11},{4,12},{5,13},{6,14},{7,15},{8,0},{9,1},... | collective-permute-start | bytes 393224 | tf_op jit(solution)/shard_map/ppermute | solution.py:45
  4.8 1.6 %collective-permute-start.3 = (bf16[4,128,128]{2,1,0:T(8,128)(2,1)}, bf16[4,128,128]{2,1,0:T(8,128)(2,1)S(1)}, u32[]{:S(2)}, u32[]{:S(2)}) collective-permute-start(bf16[4,128,128]{2,1,0:T(8,128)(2,1)} %bitcast.2), channel_id=1, source_target_pairs={{0,4},{1,5},{2,6},{3,7},{4,0},{5,1},{6,2},{7,3},{8,12},{9,13},{10,... | collective-permute-start | bytes 393224 | tf_op jit(solution)/shard_map/ppermute | solution.py:45
  6.3 1.5 %collective-permute-start.1 = (bf16[4,128,128]{2,1,0:T(8,128)(2,1)}, bf16[4,128,128]{2,1,0:T(8,128)(2,1)S(1)}, u32[]{:S(2)}, u32[]{:S(2)}) collective-permute-start(bf16[4,128,128]{2,1,0:T(8,128)(2,1)} %bitcast.3), channel_id=1, source_target_pairs={{0,2},{1,3},{2,0},{3,1},{4,6},{5,7},{6,4},{7,5},{8,10},{9,11},{10,... | collective-permute-start | bytes 393224 | tf_op jit(solution)/shard_map/ppermute | solution.py:45
  7.9 0.0 collective-permute-start
  7.9 1.7 %stage.1 = (bf16[4,16,128,128]{3,2,1,0:T(8,128)(2,1)S(1)}, bf16[512,256]{1,0:T(8,128)(2,1)S(1)}, bf16[128,256]{1,0:T(8,128)(2,1)S(1)}, bf16[4,128,128]{2,1,0:T(8,128)(2,1)S(1)}) custom-call(bf16[4,16,128,128]{3,2,1,0:T(8,128)(2,1)} %refs_0_.3, bf16[512,256]{1,0:T(8,128)(2,1)} %refs_1_.3, bf16[128,256]{1,0:T(8,128)(2,1)} %refs_2_.1, bf16[4,128,128]{2,1,0:T(8,128)(2,1)} %bitcast.5), custom_call_target="tpu_custom_call" | custom-call | tf_op jit(solution)/shard_map/stage/pallas_call | solution.py:33
  9.5 1.8 %collective-permute-done.7.refs_10_ = bf16[4,128,128]{2,1,0:T(8,128)(2,1)S(1)} collective-permute-done((bf16[4,128,128]{2,1,0:T(8,128)(2,1)}, bf16[4,128,128]{2,1,0:T(8,128)(2,1)S(1)}, u32[]{:S(2)}, u32[]{:S(2)}) %collective-permute-start.7) | collective-permute-done | bytes 131104 | tf_op jit(solution)/shard_map/ppermute | solution.py:45
  11.4 0.7 %collective-permute-start.11 = (bf16[4,128,128]{2,1,0:T(8,128)(2,1)S(1)}, bf16[4,128,128]{2,1,0:T(8,128)(2,1)S(1)}, u32[]{:S(2)}, u32[]{:S(2)}) collective-permute-start(bf16[4,128,128]{2,1,0:T(8,128)(2,1)S(1)} %collective-permute-done.7.refs_10_), channel_id=1, source_target_pairs={{0,4},{1,5},{2,6},{3,7},{4,0},{5,1},{6,2},{7,3},{8,12},{9,13},{10,... | collective-permute-start | bytes 393224 | tf_op jit(solution)/shard_map/ppermute | solution.py:45
  12.1 1.5 %collective-permute-start.9 = (bf16[4,128,128]{2,1,0:T(8,128)(2,1)S(1)}, bf16[4,128,128]{2,1,0:T(8,128)(2,1)S(1)}, u32[]{:S(2)}, u32[]{:S(2)}) collective-permute-start(bf16[4,128,128]{2,1,0:T(8,128)(2,1)S(1)} %collective-permute-done.7.refs_10_), channel_id=1, source_target_pairs={{0,2},{1,3},{2,0},{3,1},{4,6},{5,7},{6,4},{7,5},{8,10},{9,11},{10,... | collective-permute-start | bytes 393224 | tf_op jit(solution)/shard_map/ppermute | solution.py:45
  13.6 0.0 collective-permute-done.3.refs_6_
  13.6 0.0 collective-permute-start.8
  13.6 0.0 collective-permute-done.1.refs_4_
  13.6 0.5 collective-permute-start.4
  14.1 1.4 %collective-permute-start.5 = (bf16[4,128,128]{2,1,0:T(8,128)(2,1)S(1)}, bf16[4,128,128]{2,1,0:T(8,128)(2,1)S(1)}, u32[]{:S(2)}, u32[]{:S(2)}) collective-permute-start(bf16[4,128,128]{2,1,0:T(8,128)(2,1)S(1)} %collective-permute-done.1.refs_4_), channel_id=1, source_target_pairs={{0,4},{1,5},{2,6},{3,7},{4,0},{5,1},{6,2},{7,3},{8,12},{9,13},{10,... | collective-permute-start | bytes 393224 | tf_op jit(solution)/shard_map/ppermute | solution.py:45
  15.5 0.8 %collective-permute-done.11.refs_14_ = bf16[4,128,128]{2,1,0:T(8,128)(2,1)S(1)} collective-permute-done((bf16[4,128,128]{2,1,0:T(8,128)(2,1)S(1)}, bf16[4,128,128]{2,1,0:T(8,128)(2,1)S(1)}, u32[]{:S(2)}, u32[]{:S(2)}) %collective-permute-start.11) | collective-permute-done | bytes 131104 | tf_op jit(solution)/shard_map/ppermute | solution.py:45
  16.3 2.2 %collective-permute-start.13 = (bf16[4,128,128]{2,1,0:T(8,128)(2,1)S(1)}, bf16[4,128,128]{2,1,0:T(8,128)(2,1)S(1)}, u32[]{:S(2)}, u32[]{:S(2)}) collective-permute-start(bf16[4,128,128]{2,1,0:T(8,128)(2,1)S(1)} %collective-permute-done.11.refs_14_), channel_id=1, source_target_pairs={{0,2},{1,3},{2,0},{3,1},{4,6},{5,7},{6,4},{7,5},{8,10},{9,11},{10,... | collective-permute-start | bytes 393224 | tf_op jit(solution)/shard_map/ppermute | solution.py:45
  18.5 0.0 collective-permute-done.9.refs_12_
  18.5 0.0 collective-permute-start.2
  18.6 0.5 collective-permute-start.12
  19.1 0.0 collective-permute-done.4.refs_7_
  19.1 0.1 collective-permute-start.10
  19.1 0.5 collective-permute-done.5.refs_8_
  19.6 0.0 collective-permute-start.6
  19.6 1.9 %collective-permute-done.13.refs_16_ = bf16[4,128,128]{2,1,0:T(8,128)(2,1)S(1)} collective-permute-done((bf16[4,128,128]{2,1,0:T(8,128)(2,1)S(1)}, bf16[4,128,128]{2,1,0:T(8,128)(2,1)S(1)}, u32[]{:S(2)}, u32[]{:S(2)}) %collective-permute-start.13) | collective-permute-done | bytes 131104 | tf_op jit(solution)/shard_map/ppermute | solution.py:45
  21.5 0.0 collective-permute-start.14
  21.5 0.0 collective-permute-done.2.refs_5_
  21.5 0.0 collective-permute-done.10.refs_13_
  21.5 0.0 collective-permute-done.12.refs_15_
  21.5 1.3 %collective-permute-done.14.refs_17_ = bf16[4,128,128]{2,1,0:T(8,128)(2,1)S(1)} collective-permute-done((bf16[4,128,128]{2,1,0:T(8,128)(2,1)S(1)}, bf16[4,128,128]{2,1,0:T(8,128)(2,1)S(1)}, u32[]{:S(2)}, u32[]{:S(2)}) %collective-permute-start.14) | collective-permute-done | bytes 131104 | tf_op jit(solution)/shard_map/ppermute | solution.py:45
  22.8 3.0 %forward.1 = (bf16[512,256]{1,0:T(8,128)(2,1)S(1)}, bf16[4,128,128]{2,1,0:T(8,128)(2,1)S(1)}, f32[64,256]{1,0:T(8,128)S(1)}, f32[64,256]{1,0:T(8,128)S(1)}) custom-call(s32[4,16]{1,0:T(4,128)S(1)} %copy-done, s32[4]{0:T(128)S(1)} %copy-done.1, bf16[4,128,128]{2,1,0:T(8,128)(2,1)S(1)} %get-tuple-element.16.refs_2_, ...), custom_call_target="tpu_custom_call" | custom-call | tf_op jit(solution)/shard_map/forward/pallas_call | solution.py:193
  25.9 2.6 %collective-permute-start.22 = (bf16[4,128,128]{2,1,0:T(8,128)(2,1)S(1)}, bf16[4,128,128]{2,1,0:T(8,128)(2,1)S(1)}, u32[]{:S(2)}, u32[]{:S(2)}) collective-permute-start(bf16[4,128,128]{2,1,0:T(8,128)(2,1)S(1)} %get-tuple-element.22.refs_2_), channel_id=1, source_target_pairs={{0,8},{1,9},{2,10},{3,11},{4,12},{5,13},{6,14},{7,15},{8,0},{9,1},... | collective-permute-start | bytes 393224 | tf_op jit(solution)/shard_map/ppermute | solution.py:45
  28.5 0.0 collective-permute-start.30
  28.5 2.2 %collective-permute-start.18 = (bf16[4,128,128]{2,1,0:T(8,128)(2,1)S(1)}, bf16[4,128,128]{2,1,0:T(8,128)(2,1)S(1)}, u32[]{:S(2)}, u32[]{:S(2)}) collective-permute-start(bf16[4,128,128]{2,1,0:T(8,128)(2,1)S(1)} %get-tuple-element.22.refs_2_), channel_id=1, source_target_pairs={{0,4},{1,5},{2,6},{3,7},{4,0},{5,1},{6,2},{7,3},{8,12},{9,13},{10,... | collective-permute-start | bytes 393224 | tf_op jit(solution)/shard_map/ppermute | solution.py:45
  30.7 2.0 %collective-permute-start.16 = (bf16[4,128,128]{2,1,0:T(8,128)(2,1)S(1)}, bf16[4,128,128]{2,1,0:T(8,128)(2,1)S(1)}, u32[]{:S(2)}, u32[]{:S(2)}) collective-permute-start(bf16[4,128,128]{2,1,0:T(8,128)(2,1)S(1)} %get-tuple-element.22.refs_2_), channel_id=1, source_target_pairs={{0,2},{1,3},{2,0},{3,1},{4,6},{5,7},{6,4},{7,5},{8,10},{9,11},{10,... | collective-permute-start | bytes 393224 | tf_op jit(solution)/shard_map/ppermute | solution.py:45
  32.7 0.3 collective-permute-start.31
  33.0 2.3 %collective-permute-done.22.refs_10_ = bf16[4,128,128]{2,1,0:T(8,128)(2,1)S(1)} collective-permute-done((bf16[4,128,128]{2,1,0:T(8,128)(2,1)S(1)}, bf16[4,128,128]{2,1,0:T(8,128)(2,1)S(1)}, u32[]{:S(2)}, u32[]{:S(2)}) %collective-permute-start.22) | collective-permute-done | bytes 131104 | tf_op jit(solution)/shard_map/ppermute | solution.py:45
  35.3 0.6 %collective-permute-start.26 = (bf16[4,128,128]{2,1,0:T(8,128)(2,1)S(1)}, bf16[4,128,128]{2,1,0:T(8,128)(2,1)S(1)}, u32[]{:S(2)}, u32[]{:S(2)}) collective-permute-start(bf16[4,128,128]{2,1,0:T(8,128)(2,1)S(1)} %collective-permute-done.22.refs_10_), channel_id=1, source_target_pairs={{0,4},{1,5},{2,6},{3,7},{4,0},{5,1},{6,2},{7,3},{8,12},{9,13},{10,... | collective-permute-start | bytes 393224 | tf_op jit(solution)/shard_map/ppermute | solution.py:45
  36.0 3.2 %collective-permute-done.31 = f32[64,256]{1,0:T(8,128)S(1)} collective-permute-done((f32[64,256]{1,0:T(8,128)S(1)}, f32[64,256]{1,0:T(8,128)S(1)}, u32[]{:S(2)}, u32[]{:S(2)}) %collective-permute-start.31) | collective-permute-done | bytes 65568 | tf_op jit(solution)/shard_map/ppermute | solution.py:45
  39.1 0.1 collective-permute-start.32
  39.2 0.0 collective-permute-done.18.refs_6_
  39.2 1.6 %collective-permute-start.24 = (bf16[4,128,128]{2,1,0:T(8,128)(2,1)S(1)}, bf16[4,128,128]{2,1,0:T(8,128)(2,1)S(1)}, u32[]{:S(2)}, u32[]{:S(2)}) collective-permute-start(bf16[4,128,128]{2,1,0:T(8,128)(2,1)S(1)} %collective-permute-done.22.refs_10_), channel_id=1, source_target_pairs={{0,2},{1,3},{2,0},{3,1},{4,6},{5,7},{6,4},{7,5},{8,10},{9,11},{10,... | collective-permute-start | bytes 393224 | tf_op jit(solution)/shard_map/ppermute | solution.py:45
  40.8 0.0 collective-permute-done.16.refs_4_
  40.8 0.0 collective-permute-start.23
  40.8 0.0 collective-permute-done.15.refs_3_
  40.8 0.5 collective-permute-start.19
  41.4 2.1 %collective-permute-done.32 = f32[64,256]{1,0:T(8,128)S(1)} collective-permute-done((f32[64,256]{1,0:T(8,128)S(1)}, f32[64,256]{1,0:T(8,128)S(1)}, u32[]{:S(2)}, u32[]{:S(2)}) %collective-permute-start.32) | collective-permute-done | bytes 65568 | tf_op jit(solution)/shard_map/ppermute | solution.py:45
  43.5 0.0 collective-permute-start.20
  43.5 1.6 %collective-permute-start.28 = (bf16[4,128,128]{2,1,0:T(8,128)(2,1)S(1)}, bf16[4,128,128]{2,1,0:T(8,128)(2,1)S(1)}, u32[]{:S(2)}, u32[]{:S(2)}) collective-permute-start(bf16[4,128,128]{2,1,0:T(8,128)(2,1)S(1)} %collective-permute-done.26.refs_14_), channel_id=1, source_target_pairs={{0,2},{1,3},{2,0},{3,1},{4,6},{5,7},{6,4},{7,5},{8,10},{9,11},{10,... | collective-permute-start | bytes 393224 | tf_op jit(solution)/shard_map/ppermute | solution.py:45
  45.1 0.0 collective-permute-done.24.refs_12_
  45.1 0.1 collective-permute-start.17
  45.2 0.6 %collective-permute-start.33 = (f32[64,256]{1,0:T(8,128)S(1)}, f32[64,256]{1,0:T(8,128)S(1)}, u32[]{:S(2)}, u32[]{:S(2)}) collective-permute-start(f32[64,256]{1,0:T(8,128)S(1)} %add.14), channel_id=1, source_target_pairs={{0,2},{1,3},{2,0},{3,1},{4,6},{5,7},{6,4},{7,5},{8,10},{9,11},{10,... | collective-permute-start | bytes 196616 | tf_op jit(solution)/shard_map/ppermute | solution.py:45
  45.8 0.0 collective-permute-done.19.refs_7_
  45.8 0.2 collective-permute-start.27
  46.0 2.4 %collective-permute-done.20.refs_8_ = bf16[4,128,128]{2,1,0:T(8,128)(2,1)S(1)} collective-permute-done((bf16[4,128,128]{2,1,0:T(8,128)(2,1)S(1)}, bf16[4,128,128]{2,1,0:T(8,128)(2,1)S(1)}, u32[]{:S(2)}, u32[]{:S(2)}) %collective-permute-start.20) | collective-permute-done | bytes 131104 | tf_op jit(solution)/shard_map/ppermute | solution.py:45
  48.4 1.4 %collective-permute-done.33 = f32[64,256]{1,0:T(8,128)S(1)} collective-permute-done((f32[64,256]{1,0:T(8,128)S(1)}, f32[64,256]{1,0:T(8,128)S(1)}, u32[]{:S(2)}, u32[]{:S(2)}) %collective-permute-start.33) | collective-permute-done | bytes 65568 | tf_op jit(solution)/shard_map/ppermute | solution.py:45
  49.8 0.0 collective-permute-start.21
  49.9 0.0 collective-permute-done.28.refs_16_
  49.9 0.5 collective-permute-start.29
  50.4 0.1 collective-permute-start.34
  50.5 0.7 %copy.9 = bf16[512,256]{1,0:T(8,128)(2,1)} copy(bf16[512,256]{1,0:T(8,128)(2,1)S(1)} %get-tuple-element.29) | data formatting | bytes 524288
  51.2 0.5 collective-permute-done.34.refs_20_
  51.7 0.0 collective-permute-done.27.refs_15_
  51.7 0.0 collective-permute-done.25.refs_13_
  51.7 0.0 collective-permute-done.21.refs_9_
  51.7 2.1 %backward.1 = (bf16[512,128]{1,0:T(8,128)(2,1)}, f32[128,256]{1,0:T(8,128)}) custom-call(s32[4,16]{1,0:T(4,128)S(1)} %copy-done, s32[4]{0:T(128)S(1)} %copy-done.1, bf16[4,128,128]{2,1,0:T(8,128)(2,1)S(1)} %get-tuple-element.22.refs_2_, bf16[4,128,128]{2,1,0:T(8,128)(2,1)S(1)} %collective-permute-done.15.refs_3_, ...), custom_call_target="tpu_custom_call" | custom-call | tf_op jit(solution)/shard_map/backward/pallas_call | solution.py:210
  (18 shorter events, 0.1 us)
Async XLA Ops:
  0.6 22.2 %copy-start.1 = (s32[4]{0:T(128)S(1)}, s32[4]{0:T(128)}, u32[]{:S(2)}) copy-start(s32[4]{0:T(128)} %refs_1_.5) | copy-start | bytes 52
  0.6 22.2 %copy-start = (s32[4,16]{1,0:T(4,128)S(1)}, s32[4,16]{1,0:T(4,128)}, u32[]{:S(2)}) copy-start(s32[4,16]{1,0:T(4,128)} %refs_0_.5) | copy-start | bytes 772
  0.7 10.7 %collective-permute-start.7 = (bf16[4,128,128]{2,1,0:T(8,128)(2,1)}, bf16[4,128,128]{2,1,0:T(8,128)(2,1)S(1)}, u32[]{:S(2)}, u32[]{:S(2)}) collective-permute-start(bf16[4,128,128]{2,1,0:T(8,128)(2,1)} %bitcast.1), channel_id=1, source_target_pairs={{0,8},{1,9},{2,10},{3,11},{4,12},{5,13},{6,14},{7,15},{8,0},{9,1},... | collective-permute-start | bytes 393224 | tf_op jit(solution)/shard_map/ppermute | solution.py:45
  4.8 8.9 %collective-permute-start.3 = (bf16[4,128,128]{2,1,0:T(8,128)(2,1)}, bf16[4,128,128]{2,1,0:T(8,128)(2,1)S(1)}, u32[]{:S(2)}, u32[]{:S(2)}) collective-permute-start(bf16[4,128,128]{2,1,0:T(8,128)(2,1)} %bitcast.2), channel_id=1, source_target_pairs={{0,4},{1,5},{2,6},{3,7},{4,0},{5,1},{6,2},{7,3},{8,12},{9,13},{10,... | collective-permute-start | bytes 393224 | tf_op jit(solution)/shard_map/ppermute | solution.py:45
  6.3 7.3 %collective-permute-start.1 = (bf16[4,128,128]{2,1,0:T(8,128)(2,1)}, bf16[4,128,128]{2,1,0:T(8,128)(2,1)S(1)}, u32[]{:S(2)}, u32[]{:S(2)}) collective-permute-start(bf16[4,128,128]{2,1,0:T(8,128)(2,1)} %bitcast.3), channel_id=1, source_target_pairs={{0,2},{1,3},{2,0},{3,1},{4,6},{5,7},{6,4},{7,5},{8,10},{9,11},{10,... | collective-permute-start | bytes 393224 | tf_op jit(solution)/shard_map/ppermute | solution.py:45
  7.9 6.3 %collective-permute-start = (bf16[4,128,128]{2,1,0:T(8,128)(2,1)}, bf16[4,128,128]{2,1,0:T(8,128)(2,1)S(1)}, u32[]{:S(2)}, u32[]{:S(2)}) collective-permute-start(bf16[4,128,128]{2,1,0:T(8,128)(2,1)} %bitcast.4), channel_id=1, source_target_pairs={{0,1},{1,0},{2,3},{3,2},{4,5},{5,4},{6,7},{7,6},{8,9},{9,8},{10,11... | collective-permute-start | bytes 393224 | tf_op jit(solution)/shard_map/ppermute | solution.py:45
  11.4 5.0 %collective-permute-start.11 = (bf16[4,128,128]{2,1,0:T(8,128)(2,1)S(1)}, bf16[4,128,128]{2,1,0:T(8,128)(2,1)S(1)}, u32[]{:S(2)}, u32[]{:S(2)}) collective-permute-start(bf16[4,128,128]{2,1,0:T(8,128)(2,1)S(1)} %collective-permute-done.7.refs_10_), channel_id=1, source_target_pairs={{0,4},{1,5},{2,6},{3,7},{4,0},{5,1},{6,2},{7,3},{8,12},{9,13},{10,... | collective-permute-start | bytes 393224 | tf_op jit(solution)/shard_map/ppermute | solution.py:45
  12.1 6.4 %collective-permute-start.9 = (bf16[4,128,128]{2,1,0:T(8,128)(2,1)S(1)}, bf16[4,128,128]{2,1,0:T(8,128)(2,1)S(1)}, u32[]{:S(2)}, u32[]{:S(2)}) collective-permute-start(bf16[4,128,128]{2,1,0:T(8,128)(2,1)S(1)} %collective-permute-done.7.refs_10_), channel_id=1, source_target_pairs={{0,2},{1,3},{2,0},{3,1},{4,6},{5,7},{6,4},{7,5},{8,10},{9,11},{10,... | collective-permute-start | bytes 393224 | tf_op jit(solution)/shard_map/ppermute | solution.py:45
  13.6 4.9 %collective-permute-start.8 = (bf16[4,128,128]{2,1,0:T(8,128)(2,1)S(1)}, bf16[4,128,128]{2,1,0:T(8,128)(2,1)S(1)}, u32[]{:S(2)}, u32[]{:S(2)}) collective-permute-start(bf16[4,128,128]{2,1,0:T(8,128)(2,1)S(1)} %collective-permute-done.7.refs_10_), channel_id=1, source_target_pairs={{0,1},{1,0},{2,3},{3,2},{4,5},{5,4},{6,7},{7,6},{8,9},{9,8},{10,11... | collective-permute-start | bytes 393224 | tf_op jit(solution)/shard_map/ppermute | solution.py:45
  13.6 5.4 %collective-permute-start.4 = (bf16[4,128,128]{2,1,0:T(8,128)(2,1)S(1)}, bf16[4,128,128]{2,1,0:T(8,128)(2,1)S(1)}, u32[]{:S(2)}, u32[]{:S(2)}) collective-permute-start(bf16[4,128,128]{2,1,0:T(8,128)(2,1)S(1)} %collective-permute-done.3.refs_6_), channel_id=1, source_target_pairs={{0,1},{1,0},{2,3},{3,2},{4,5},{5,4},{6,7},{7,6},{8,9},{9,8},{10,11... | collective-permute-start | bytes 393224 | tf_op jit(solution)/shard_map/ppermute | solution.py:45
  14.1 5.5 %collective-permute-start.5 = (bf16[4,128,128]{2,1,0:T(8,128)(2,1)S(1)}, bf16[4,128,128]{2,1,0:T(8,128)(2,1)S(1)}, u32[]{:S(2)}, u32[]{:S(2)}) collective-permute-start(bf16[4,128,128]{2,1,0:T(8,128)(2,1)S(1)} %collective-permute-done.1.refs_4_), channel_id=1, source_target_pairs={{0,4},{1,5},{2,6},{3,7},{4,0},{5,1},{6,2},{7,3},{8,12},{9,13},{10,... | collective-permute-start | bytes 393224 | tf_op jit(solution)/shard_map/ppermute | solution.py:45
  16.3 5.1 %collective-permute-start.13 = (bf16[4,128,128]{2,1,0:T(8,128)(2,1)S(1)}, bf16[4,128,128]{2,1,0:T(8,128)(2,1)S(1)}, u32[]{:S(2)}, u32[]{:S(2)}) collective-permute-start(bf16[4,128,128]{2,1,0:T(8,128)(2,1)S(1)} %collective-permute-done.11.refs_14_), channel_id=1, source_target_pairs={{0,2},{1,3},{2,0},{3,1},{4,6},{5,7},{6,4},{7,5},{8,10},{9,11},{10,... | collective-permute-start | bytes 393224 | tf_op jit(solution)/shard_map/ppermute | solution.py:45
  18.5 2.9 %collective-permute-start.2 = (bf16[4,128,128]{2,1,0:T(8,128)(2,1)S(1)}, bf16[4,128,128]{2,1,0:T(8,128)(2,1)S(1)}, u32[]{:S(2)}, u32[]{:S(2)}) collective-permute-start(bf16[4,128,128]{2,1,0:T(8,128)(2,1)S(1)} %collective-permute-done.1.refs_4_), channel_id=1, source_target_pairs={{0,1},{1,0},{2,3},{3,2},{4,5},{5,4},{6,7},{7,6},{8,9},{9,8},{10,11... | collective-permute-start | bytes 393224 | tf_op jit(solution)/shard_map/ppermute | solution.py:45
  18.6 3.0 %collective-permute-start.12 = (bf16[4,128,128]{2,1,0:T(8,128)(2,1)S(1)}, bf16[4,128,128]{2,1,0:T(8,128)(2,1)S(1)}, u32[]{:S(2)}, u32[]{:S(2)}) collective-permute-start(bf16[4,128,128]{2,1,0:T(8,128)(2,1)S(1)} %collective-permute-done.11.refs_14_), channel_id=1, source_target_pairs={{0,1},{1,0},{2,3},{3,2},{4,5},{5,4},{6,7},{7,6},{8,9},{9,8},{10,11... | collective-permute-start | bytes 393224 | tf_op jit(solution)/shard_map/ppermute | solution.py:45
  19.1 2.4 %collective-permute-start.10 = (bf16[4,128,128]{2,1,0:T(8,128)(2,1)S(1)}, bf16[4,128,128]{2,1,0:T(8,128)(2,1)S(1)}, u32[]{:S(2)}, u32[]{:S(2)}) collective-permute-start(bf16[4,128,128]{2,1,0:T(8,128)(2,1)S(1)} %collective-permute-done.9.refs_12_), channel_id=1, source_target_pairs={{0,1},{1,0},{2,3},{3,2},{4,5},{5,4},{6,7},{7,6},{8,9},{9,8},{10,11... | collective-permute-start | bytes 393224 | tf_op jit(solution)/shard_map/ppermute | solution.py:45
  19.6 1.9 %collective-permute-start.6 = (bf16[4,128,128]{2,1,0:T(8,128)(2,1)S(1)}, bf16[4,128,128]{2,1,0:T(8,128)(2,1)S(1)}, u32[]{:S(2)}, u32[]{:S(2)}) collective-permute-start(bf16[4,128,128]{2,1,0:T(8,128)(2,1)S(1)} %collective-permute-done.5.refs_8_), channel_id=1, source_target_pairs={{0,1},{1,0},{2,3},{3,2},{4,5},{5,4},{6,7},{7,6},{8,9},{9,8},{10,11... | collective-permute-start | bytes 393224 | tf_op jit(solution)/shard_map/ppermute | solution.py:45
  21.5 1.3 %collective-permute-start.14 = (bf16[4,128,128]{2,1,0:T(8,128)(2,1)S(1)}, bf16[4,128,128]{2,1,0:T(8,128)(2,1)S(1)}, u32[]{:S(2)}, u32[]{:S(2)}) collective-permute-start(bf16[4,128,128]{2,1,0:T(8,128)(2,1)S(1)} %collective-permute-done.13.refs_16_), channel_id=1, source_target_pairs={{0,1},{1,0},{2,3},{3,2},{4,5},{5,4},{6,7},{7,6},{8,9},{9,8},{10,11... | collective-permute-start | bytes 393224 | tf_op jit(solution)/shard_map/ppermute | solution.py:45
  25.9 9.4 %collective-permute-start.22 = (bf16[4,128,128]{2,1,0:T(8,128)(2,1)S(1)}, bf16[4,128,128]{2,1,0:T(8,128)(2,1)S(1)}, u32[]{:S(2)}, u32[]{:S(2)}) collective-permute-start(bf16[4,128,128]{2,1,0:T(8,128)(2,1)S(1)} %get-tuple-element.22.refs_2_), channel_id=1, source_target_pairs={{0,8},{1,9},{2,10},{3,11},{4,12},{5,13},{6,14},{7,15},{8,0},{9,1},... | collective-permute-start | bytes 393224 | tf_op jit(solution)/shard_map/ppermute | solution.py:45
  28.5 4.2 %collective-permute-start.30 = (f32[64,256]{1,0:T(8,128)S(1)}, f32[64,256]{1,0:T(8,128)S(1)}, u32[]{:S(2)}, u32[]{:S(2)}) collective-permute-start(f32[64,256]{1,0:T(8,128)S(1)} %get-tuple-element.24), channel_id=1, source_target_pairs={{0,1},{1,0},{2,3},{3,2},{4,5},{5,4},{6,7},{7,6},{8,9},{9,8},{10,11... | collective-permute-start | bytes 196616 | tf_op jit(solution)/shard_map/ppermute | solution.py:45
  28.5 10.7 %collective-permute-start.18 = (bf16[4,128,128]{2,1,0:T(8,128)(2,1)S(1)}, bf16[4,128,128]{2,1,0:T(8,128)(2,1)S(1)}, u32[]{:S(2)}, u32[]{:S(2)}) collective-permute-start(bf16[4,128,128]{2,1,0:T(8,128)(2,1)S(1)} %get-tuple-element.22.refs_2_), channel_id=1, source_target_pairs={{0,4},{1,5},{2,6},{3,7},{4,0},{5,1},{6,2},{7,3},{8,12},{9,13},{10,... | collective-permute-start | bytes 393224 | tf_op jit(solution)/shard_map/ppermute | solution.py:45
  30.7 10.2 %collective-permute-start.16 = (bf16[4,128,128]{2,1,0:T(8,128)(2,1)S(1)}, bf16[4,128,128]{2,1,0:T(8,128)(2,1)S(1)}, u32[]{:S(2)}, u32[]{:S(2)}) collective-permute-start(bf16[4,128,128]{2,1,0:T(8,128)(2,1)S(1)} %get-tuple-element.22.refs_2_), channel_id=1, source_target_pairs={{0,2},{1,3},{2,0},{3,1},{4,6},{5,7},{6,4},{7,5},{8,10},{9,11},{10,... | collective-permute-start | bytes 393224 | tf_op jit(solution)/shard_map/ppermute | solution.py:45
  32.7 6.4 %collective-permute-start.31 = (f32[64,256]{1,0:T(8,128)S(1)}, f32[64,256]{1,0:T(8,128)S(1)}, u32[]{:S(2)}, u32[]{:S(2)}) collective-permute-start(f32[64,256]{1,0:T(8,128)S(1)} %add.12), channel_id=1, source_target_pairs={{0,8},{1,9},{2,10},{3,11},{4,12},{5,13},{6,14},{7,15},{8,0},{9,1},... | collective-permute-start | bytes 196616 | tf_op jit(solution)/shard_map/ppermute | solution.py:45
  33.0 7.8 %collective-permute-start.15 = (bf16[4,128,128]{2,1,0:T(8,128)(2,1)S(1)}, bf16[4,128,128]{2,1,0:T(8,128)(2,1)S(1)}, u32[]{:S(2)}, u32[]{:S(2)}) collective-permute-start(bf16[4,128,128]{2,1,0:T(8,128)(2,1)S(1)} %get-tuple-element.22.refs_2_), channel_id=1, source_target_pairs={{0,1},{1,0},{2,3},{3,2},{4,5},{5,4},{6,7},{7,6},{8,9},{9,8},{10,11... | collective-permute-start | bytes 393224 | tf_op jit(solution)/shard_map/ppermute | solution.py:45
  35.3 8.2 %collective-permute-start.26 = (bf16[4,128,128]{2,1,0:T(8,128)(2,1)S(1)}, bf16[4,128,128]{2,1,0:T(8,128)(2,1)S(1)}, u32[]{:S(2)}, u32[]{:S(2)}) collective-permute-start(bf16[4,128,128]{2,1,0:T(8,128)(2,1)S(1)} %collective-permute-done.22.refs_10_), channel_id=1, source_target_pairs={{0,4},{1,5},{2,6},{3,7},{4,0},{5,1},{6,2},{7,3},{8,12},{9,13},{10,... | collective-permute-start | bytes 393224 | tf_op jit(solution)/shard_map/ppermute | solution.py:45
  39.1 4.3 %collective-permute-start.32 = (f32[64,256]{1,0:T(8,128)S(1)}, f32[64,256]{1,0:T(8,128)S(1)}, u32[]{:S(2)}, u32[]{:S(2)}) collective-permute-start(f32[64,256]{1,0:T(8,128)S(1)} %add.13), channel_id=1, source_target_pairs={{0,4},{1,5},{2,6},{3,7},{4,0},{5,1},{6,2},{7,3},{8,12},{9,13},{10,... | collective-permute-start | bytes 196616 | tf_op jit(solution)/shard_map/ppermute | solution.py:45
  39.2 5.9 %collective-permute-start.24 = (bf16[4,128,128]{2,1,0:T(8,128)(2,1)S(1)}, bf16[4,128,128]{2,1,0:T(8,128)(2,1)S(1)}, u32[]{:S(2)}, u32[]{:S(2)}) collective-permute-start(bf16[4,128,128]{2,1,0:T(8,128)(2,1)S(1)} %collective-permute-done.22.refs_10_), channel_id=1, source_target_pairs={{0,2},{1,3},{2,0},{3,1},{4,6},{5,7},{6,4},{7,5},{8,10},{9,11},{10,... | collective-permute-start | bytes 393224 | tf_op jit(solution)/shard_map/ppermute | solution.py:45
  40.8 4.4 %collective-permute-start.23 = (bf16[4,128,128]{2,1,0:T(8,128)(2,1)S(1)}, bf16[4,128,128]{2,1,0:T(8,128)(2,1)S(1)}, u32[]{:S(2)}, u32[]{:S(2)}) collective-permute-start(bf16[4,128,128]{2,1,0:T(8,128)(2,1)S(1)} %collective-permute-done.22.refs_10_), channel_id=1, source_target_pairs={{0,1},{1,0},{2,3},{3,2},{4,5},{5,4},{6,7},{7,6},{8,9},{9,8},{10,11... | collective-permute-start | bytes 393224 | tf_op jit(solution)/shard_map/ppermute | solution.py:45
  40.8 5.0 %collective-permute-start.19 = (bf16[4,128,128]{2,1,0:T(8,128)(2,1)S(1)}, bf16[4,128,128]{2,1,0:T(8,128)(2,1)S(1)}, u32[]{:S(2)}, u32[]{:S(2)}) collective-permute-start(bf16[4,128,128]{2,1,0:T(8,128)(2,1)S(1)} %collective-permute-done.18.refs_6_), channel_id=1, source_target_pairs={{0,1},{1,0},{2,3},{3,2},{4,5},{5,4},{6,7},{7,6},{8,9},{9,8},{10,11... | collective-permute-start | bytes 393224 | tf_op jit(solution)/shard_map/ppermute | solution.py:45
  43.5 5.0 %collective-permute-start.20 = (bf16[4,128,128]{2,1,0:T(8,128)(2,1)S(1)}, bf16[4,128,128]{2,1,0:T(8,128)(2,1)S(1)}, u32[]{:S(2)}, u32[]{:S(2)}) collective-permute-start(bf16[4,128,128]{2,1,0:T(8,128)(2,1)S(1)} %collective-permute-done.16.refs_4_), channel_id=1, source_target_pairs={{0,4},{1,5},{2,6},{3,7},{4,0},{5,1},{6,2},{7,3},{8,12},{9,13},{10,... | collective-permute-start | bytes 393224 | tf_op jit(solution)/shard_map/ppermute | solution.py:45
  43.5 6.4 %collective-permute-start.28 = (bf16[4,128,128]{2,1,0:T(8,128)(2,1)S(1)}, bf16[4,128,128]{2,1,0:T(8,128)(2,1)S(1)}, u32[]{:S(2)}, u32[]{:S(2)}) collective-permute-start(bf16[4,128,128]{2,1,0:T(8,128)(2,1)S(1)} %collective-permute-done.26.refs_14_), channel_id=1, source_target_pairs={{0,2},{1,3},{2,0},{3,1},{4,6},{5,7},{6,4},{7,5},{8,10},{9,11},{10,... | collective-permute-start | bytes 393224 | tf_op jit(solution)/shard_map/ppermute | solution.py:45
  45.1 5.3 %collective-permute-start.17 = (bf16[4,128,128]{2,1,0:T(8,128)(2,1)S(1)}, bf16[4,128,128]{2,1,0:T(8,128)(2,1)S(1)}, u32[]{:S(2)}, u32[]{:S(2)}) collective-permute-start(bf16[4,128,128]{2,1,0:T(8,128)(2,1)S(1)} %collective-permute-done.16.refs_4_), channel_id=1, source_target_pairs={{0,1},{1,0},{2,3},{3,2},{4,5},{5,4},{6,7},{7,6},{8,9},{9,8},{10,11... | collective-permute-start | bytes 393224 | tf_op jit(solution)/shard_map/ppermute | solution.py:45
  45.2 4.6 %collective-permute-start.33 = (f32[64,256]{1,0:T(8,128)S(1)}, f32[64,256]{1,0:T(8,128)S(1)}, u32[]{:S(2)}, u32[]{:S(2)}) collective-permute-start(f32[64,256]{1,0:T(8,128)S(1)} %add.14), channel_id=1, source_target_pairs={{0,2},{1,3},{2,0},{3,1},{4,6},{5,7},{6,4},{7,5},{8,10},{9,11},{10,... | collective-permute-start | bytes 196616 | tf_op jit(solution)/shard_map/ppermute | solution.py:45
  45.8 5.9 %collective-permute-start.27 = (bf16[4,128,128]{2,1,0:T(8,128)(2,1)S(1)}, bf16[4,128,128]{2,1,0:T(8,128)(2,1)S(1)}, u32[]{:S(2)}, u32[]{:S(2)}) collective-permute-start(bf16[4,128,128]{2,1,0:T(8,128)(2,1)S(1)} %collective-permute-done.26.refs_14_), channel_id=1, source_target_pairs={{0,1},{1,0},{2,3},{3,2},{4,5},{5,4},{6,7},{7,6},{8,9},{9,8},{10,11... | collective-permute-start | bytes 393224 | tf_op jit(solution)/shard_map/ppermute | solution.py:45
  48.4 3.3 %collective-permute-start.25 = (bf16[4,128,128]{2,1,0:T(8,128)(2,1)S(1)}, bf16[4,128,128]{2,1,0:T(8,128)(2,1)S(1)}, u32[]{:S(2)}, u32[]{:S(2)}) collective-permute-start(bf16[4,128,128]{2,1,0:T(8,128)(2,1)S(1)} %collective-permute-done.24.refs_12_), channel_id=1, source_target_pairs={{0,1},{1,0},{2,3},{3,2},{4,5},{5,4},{6,7},{7,6},{8,9},{9,8},{10,11... | collective-permute-start | bytes 393224 | tf_op jit(solution)/shard_map/ppermute | solution.py:45
  49.8 1.9 %collective-permute-start.21 = (bf16[4,128,128]{2,1,0:T(8,128)(2,1)S(1)}, bf16[4,128,128]{2,1,0:T(8,128)(2,1)S(1)}, u32[]{:S(2)}, u32[]{:S(2)}) collective-permute-start(bf16[4,128,128]{2,1,0:T(8,128)(2,1)S(1)} %collective-permute-done.20.refs_8_), channel_id=1, source_target_pairs={{0,1},{1,0},{2,3},{3,2},{4,5},{5,4},{6,7},{7,6},{8,9},{9,8},{10,11... | collective-permute-start | bytes 393224 | tf_op jit(solution)/shard_map/ppermute | solution.py:45
  49.9 1.9 %collective-permute-start.29 = (bf16[4,128,128]{2,1,0:T(8,128)(2,1)S(1)}, bf16[4,128,128]{2,1,0:T(8,128)(2,1)S(1)}, u32[]{:S(2)}, u32[]{:S(2)}) collective-permute-start(bf16[4,128,128]{2,1,0:T(8,128)(2,1)S(1)} %collective-permute-done.28.refs_16_), channel_id=1, source_target_pairs={{0,1},{1,0},{2,3},{3,2},{4,5},{5,4},{6,7},{7,6},{8,9},{9,8},{10,11... | collective-permute-start | bytes 393224 | tf_op jit(solution)/shard_map/ppermute | solution.py:45
  50.4 1.3 %collective-permute-start.34 = (f32[64,256]{1,0:T(8,128)S(1)}, f32[64,256]{1,0:T(8,128)S(1)}, u32[]{:S(2)}, u32[]{:S(2)}) collective-permute-start(f32[64,256]{1,0:T(8,128)S(1)} %add.15.refs_19_), channel_id=1, source_target_pairs={{0,1},{1,0},{2,3},{3,2},{4,5},{5,4},{6,7},{7,6},{8,9},{9,8},{10,11... | collective-permute-start | bytes 196616 | tf_op jit(solution)/shard_map/ppermute | solution.py:45

commit v4 on v3

--- a/solution.py
+++ b/solution.py
@@ -11,34 +11,78 @@
 PARAMS = pltpu.CompilerParams(vmem_limit_bytes=12 * 2**20)
 SMEM = pl.BlockSpec(memory_space=pltpu.SMEM)
 VMEM = pl.BlockSpec(memory_space=pltpu.VMEM)
+HBM = pl.BlockSpec(memory_space=pltpu.HBM)
 
 
 def in_vmem(x):
     return pltpu.with_memory_space_constraint(x, pltpu.VMEM)
 
 
-def stage(*arrays):
-    n = len(arrays)
-
-    def kernel(*refs):
-        sems = refs[2 * n]
-        copies = [
-            pltpu.make_async_copy(refs[i], refs[n + i], sems.at[i]) for i in range(n)
-        ]
-        for c in copies:
-            c.start()
-        for c in copies:
-            c.wait()
-
+def in_hbm(x):
+    return pltpu.with_memory_space_constraint(x, pltpu.HBM)
+
+
+def in_smem(x):
+    return pltpu.with_memory_space_constraint(x, pltpu.SMEM)
+
+
+def run(copies):
+    for c in copies:
+        c.start()
+    for c in copies:
+        c.wait()
+
+
+def stage_kernel(cols, counts, vals, *refs):
+    n = (len(refs) - 3) // 2
+    plain, refs = refs[:n], refs[n:]
+    cols_out, vals_out = refs[:2]
+    plain_out = refs[2 : 2 + n]
+    counts_in, sems = refs[2 + n :]
+    pairs = [(counts, counts_in), (cols, cols_out), (vals, vals_out), *zip(plain, plain_out)]
+    run([pltpu.make_async_copy(i, o, sems.at[k]) for k, (i, o) in enumerate(pairs)])
+    panels, slots = vals_out.shape[:2]
+    for panel in range(panels):
+        for slot in range(slots):
+
+            @pl.when(slot >= counts_in[panel])
+            def _():
+                vals_out[panel, slot] = jnp.zeros(vals_out.shape[2:], vals_out.dtype)
+
+
+def stage(cols, counts, vals, *plain):
+    n = len(plain)
     return pl.pallas_call(
-        kernel,
+        stage_kernel,
         name="stage",
         compiler_params=PARAMS,
-        out_shape=tuple(pltpu.VMEM(a.shape, a.dtype) for a in arrays),
-        in_specs=[pl.BlockSpec(memory_space=pltpu.HBM)] * n,
-        out_specs=(VMEM,) * n,
-        scratch_shapes=[pltpu.SemaphoreType.DMA((n,))],
-    )(*(pltpu.with_memory_space_constraint(a, pltpu.HBM) for a in arrays))
+        out_shape=(
+            pltpu.SMEM(cols.shape, cols.dtype),
+            *(pltpu.VMEM(a.shape, a.dtype) for a in (vals, *plain)),
+        ),
+        in_specs=[HBM] * (3 + n),
+        out_specs=(SMEM,) + (VMEM,) * (1 + n),
+        scratch_shapes=[
+            pltpu.SMEM(counts.shape, counts.dtype),
+            pltpu.SemaphoreType.DMA((3 + n,)),
+        ],
+    )(*(in_hbm(a) for a in (cols, counts, vals, *plain)))
+
+
+def unstage_kernel(x, out, sem):
+    run([pltpu.make_async_copy(x, out, sem)])
+
+
+def unstage(x):
+    return pl.pallas_call(
+        unstage_kernel,
+        name="unstage",
+        compiler_params=PARAMS,
+        out_shape=jax.ShapeDtypeStruct(x.shape, x.dtype),
+        in_specs=[VMEM],
+        out_specs=HBM,
+        scratch_shapes=[pltpu.SemaphoreType.DMA],
+    )(in_vmem(x))
 
 
 def exchange(x, bit, size):
@@ -94,21 +138,19 @@
     return nodes
 
 
-def panel_product(cols, counts, vals, nodes, panel):
-    used = counts[panel]
-    slots, side = vals.shape[1:3]
-    none = jnp.zeros((side, side), vals.dtype)
+def panel_product(cols, vals, nodes, panel):
     total = None
-    for b in range(0, slots, GROUP):
+    for b in range(0, vals.shape[1], GROUP):
         group = range(b, b + GROUP)
         part = jnp.dot(
-            jnp.concatenate([jnp.where(i < used, vals[panel, i], none) for i in group], 1),
+            jnp.concatenate([vals[panel, i] for i in group], 1),
             jnp.concatenate([nodes[cols[panel, i]] for i in group], 0),
             preferred_element_type=jnp.float32,
         )
         total = part if total is None else total + part
     return total
 
+
 def split(x):
     high = x.astype(jnp.bfloat16)
     return high, (x - high.astype(jnp.float32)).astype(jnp.bfloat16)
@@ -120,20 +162,20 @@
 
 def forward_kernel(masks, *refs):
     n = len(masks)
-    cols, counts = refs[:2]
-    pieces = refs[2 : 2 + n]
-    vals, weight, out_grad = refs[2 + n : 5 + n]
-    hidden, edge, keep, send = refs[5 + n : 9 + n]
-    wsum = refs[9 + n]
+    cols = refs[0]
+    pieces = refs[1 : 1 + n]
+    vals, weight, out_grad = refs[1 + n : 4 + n]
+    hidden, edge, keep, send = refs[4 + n : 8 + n]
+    wsum = refs[8 + n]
     me = lax.axis_index("row")
-    nodes = collect(me, masks, pieces, refs[10 + n] if n > 1 else None)
+    nodes = collect(me, masks, pieces, refs[9 + n] if n > 1 else None)
     panels, _, side, _ = vals.shape
     half = keep.shape[0]
     w = weight[...]
     ww = jnp.concatenate([w, w], 0)
     for panel in range(panels):
         rows = pl.ds(panel * side, side)
-        agg = panel_product(cols, counts, vals, nodes, panel)
+        agg = panel_product(cols, vals, nodes, panel)
         agg_h, agg_l = split(agg)
         z = dot(jnp.concatenate([agg_h, agg_l], 1), ww, ((1,), (0,)))
         zz = z * z
@@ -157,20 +199,29 @@
 
 def backward_kernel(masks, *refs):
     n = len(masks)
-    cols, counts = refs[:2]
-    pieces = refs[2 : 2 + n]
-    vals, own, other = refs[2 + n : 5 + n]
-    feat, weight_grad = refs[5 + n : 7 + n]
+    cols = refs[0]
+    pieces = refs[1 : 1 + n]
+    vals, own, other = refs[1 + n : 4 + n]
+    feat, weight_grad, rows, sems = refs[4 + n : 8 + n]
     me = lax.axis_index("row")
+    panels, _, side, _ = vals.shape
     half = own.shape[0]
+    copies = []
+
+    def send(source, target):
+        copies.append(pltpu.make_async_copy(source, target, sems.at[len(copies)]))
+        copies[-1].start()
+
     core = me % 2
-    weight_grad[pl.ds(pl.multiple_of(core * half, half), half), :] = own[...]
-    weight_grad[pl.ds(pl.multiple_of((1 - core) * half, half), half), :] = other[...]
-    nodes = collect(me, masks, pieces, refs[7 + n] if n > 1 else None)
-    panels, _, side, _ = vals.shape
+    send(own, weight_grad.at[pl.ds(pl.multiple_of(core * half, half), half)])
+    send(other, weight_grad.at[pl.ds(pl.multiple_of((1 - core) * half, half), half)])
+    nodes = collect(me, masks, pieces, refs[8 + n] if n > 1 else None)
     for panel in range(panels):
-        rows = pl.ds(panel * side, side)
-        feat[rows, :] = panel_product(cols, counts, vals, nodes, panel).astype(jnp.bfloat16)
+        here = pl.ds(panel * side, side)
+        rows[here, :] = panel_product(cols, vals, nodes, panel).astype(jnp.bfloat16)
+        send(rows.at[here], feat.at[here])
+    for c in copies:
+        c.wait()
 
 
 def body(features, weight, block_cols, block_counts, block_vals, out_grad):
@@ -180,7 +231,10 @@
     hidden_width = weight.shape[1]
     node_blocks = size * panels
     features_in = features.reshape(panels, side, width)
-    vals, out_grad, weight, own_rows = stage(block_vals, out_grad, weight, features_in)
+    cols, vals, out_grad, weight, own_rows = stage(
+        block_cols, block_counts, block_vals, out_grad, weight, features_in
+    )
+    cols, vals = in_smem(cols), in_vmem(vals)
 
     def gathered(x, own, staged=None):
         held = gather_rows(x, own, size, staged)
@@ -200,12 +254,13 @@
             pltpu.VMEM((width // 2, hidden_width), jnp.float32),
             pltpu.VMEM((width // 2, hidden_width), jnp.float32),
         ),
-        in_specs=[SMEM] * 2 + [VMEM] * (len(pieces) + 3),
+        in_specs=[SMEM] + [VMEM] * (len(pieces) + 3),
         out_specs=(VMEM,) * 4,
         scratch_shapes=[pltpu.VMEM((width, hidden_width), jnp.float32)] + scratch,
-    )(block_cols, block_counts, *pieces, in_vmem(vals), in_vmem(weight), in_vmem(out_grad))
-
-    held, masks, pieces, scratch = gathered(edge, edge)
+    )(cols, *pieces, vals, in_vmem(weight), in_vmem(out_grad))
+
+    hidden = unstage(hidden)
+    held, masks, pieces, scratch = gathered(edge, edge, hidden)
     own, other = row_sum(keep, send, held, size)
     feat_grad, weight_grad = pl.pallas_call(
         lambda *refs: backward_kernel(masks, *refs),
@@ -215,10 +270,14 @@
             jax.ShapeDtypeStruct((rows, width), jnp.bfloat16),
             jax.ShapeDtypeStruct((width, hidden_width), jnp.float32),
         ),
-        in_specs=[SMEM] * 2 + [VMEM] * (len(pieces) + 3),
-        out_specs=(VMEM, VMEM),
-        scratch_shapes=scratch,
-    )(block_cols, block_counts, *pieces, in_vmem(vals), in_vmem(own), in_vmem(other))
+        in_specs=[SMEM] + [VMEM] * (len(pieces) + 3),
+        out_specs=(HBM, HBM),
+        scratch_shapes=[
+            pltpu.VMEM((rows, width), jnp.bfloat16),
+            pltpu.SemaphoreType.DMA((panels + 2,)),
+        ]
+        + scratch,
+    )(cols, *pieces, vals, in_vmem(own), in_vmem(other))
     return hidden, feat_grad, weight_grad
 
 

time: 54 us -> 52.8 us (0.978)
  local copies, waits for them, and re-layouts: 0.71 us -> 0 us
    pallas_call x1 -> x2, Pallas kernels: 1.67 us -> 2.86 us  [the longest x1 2.15 us: stage(): pl.pallas_call(stage_kernel, name='stage', compiler_params=PARAMS, out_sh...]
    unnamed x5 -> x0, local copies, waits for them, and re-layouts: 0.71 us -> none
    pallas_call x1, Pallas kernels: 3.04 us -> 2.44 us  [body(): pl.pallas_call(lambda *refs: forward_kernel(masks, *refs), name='forward'...]
    pallas_call x1, Pallas kernels: 2.12 us -> 1.52 us  [body(): pl.pallas_call(lambda *refs: backward_kernel(masks, *refs), name='backwar...]
  transfers between devices with their start and end apart: 35 -> 35, of which waited for: 11 -> 11; matrix products, arithmetic and copies ran while one was open for 1% -> 0% of each run, Pallas kernels for 3% -> 5%
where the time goes in v4:
time: 52.8 us; the launch traced here: 52.6 us
  starting transfers between devices  27.1 us (51%)
  waiting for transfers between devices  17.9 us (34%)
  Pallas kernels  6.81 us (13%)
  between operations  0.79 us (1%)
    ppermute x35, starting transfers between devices, exchange(): return lax.ppermute(x, 'row', [(i, i ^ bit) for i in range(size)])  27.1 us
    ppermute x35, waiting for transfers between devices, exchange(): return lax.ppermute(x, 'row', [(i, i ^ bit) for i in range(size)])  17.9 us
    pallas_call x1, Pallas kernels, body(): pl.pallas_call(lambda *refs: forward_kernel(masks, *refs), name='forward'...  2.44 us
    pallas_call x1, Pallas kernels, stage(): pl.pallas_call(stage_kernel, name='stage', compiler_params=PARAMS, out_sh...  2.15 us
    pallas_call x1, Pallas kernels, body(): pl.pallas_call(lambda *refs: backward_kernel(masks, *refs), name='backwar...  1.52 us
  transfers between devices with their start and end apart: 35, of which 11 were waited for; matrix products, arithmetic and copies ran while one was open for 0% of the time, Pallas kernels for 5%

profile of v4, /device:TPU:0, one launch (start us, length us, event | category | flops | bytes accessed | tf_op | source)
XLA Modules:
  0.0 52.6 jit_solution(8512363875900008381)
XLA Ops:
  0.6 4.1 %collective-permute-start.7 = (bf16[4,128,128]{2,1,0:T(8,128)(2,1)}, bf16[4,128,128]{2,1,0:T(8,128)(2,1)S(1)}, u32[]{:S(2)}, u32[]{:S(2)}) collective-permute-start(bf16[4,128,128]{2,1,0:T(8,128)(2,1)} %bitcast.1), channel_id=1, source_target_pairs={{0,8},{1,9},{2,10},{3,11},{4,12},{5,13},{6,14},{7,15},{8,0},{9,1},... | collective-permute-start | bytes 393224 | tf_op jit(solution)/shard_map/ppermute | solution.py:89
  4.7 1.6 %collective-permute-start.3 = (bf16[4,128,128]{2,1,0:T(8,128)(2,1)}, bf16[4,128,128]{2,1,0:T(8,128)(2,1)S(1)}, u32[]{:S(2)}, u32[]{:S(2)}) collective-permute-start(bf16[4,128,128]{2,1,0:T(8,128)(2,1)} %bitcast.2), channel_id=1, source_target_pairs={{0,4},{1,5},{2,6},{3,7},{4,0},{5,1},{6,2},{7,3},{8,12},{9,13},{10,... | collective-permute-start | bytes 393224 | tf_op jit(solution)/shard_map/ppermute | solution.py:89
  6.3 1.5 %collective-permute-start.1 = (bf16[4,128,128]{2,1,0:T(8,128)(2,1)}, bf16[4,128,128]{2,1,0:T(8,128)(2,1)S(1)}, u32[]{:S(2)}, u32[]{:S(2)}) collective-permute-start(bf16[4,128,128]{2,1,0:T(8,128)(2,1)} %bitcast.3), channel_id=1, source_target_pairs={{0,2},{1,3},{2,0},{3,1},{4,6},{5,7},{6,4},{7,5},{8,10},{9,11},{10,... | collective-permute-start | bytes 393224 | tf_op jit(solution)/shard_map/ppermute | solution.py:89
  7.8 0.0 collective-permute-start
  7.8 2.2 %stage.1 = (s32[4,16]{1,0:T(4,128)S(4)}, bf16[4,16,128,128]{3,2,1,0:T(8,128)(2,1)S(1)}, bf16[512,256]{1,0:T(8,128)(2,1)S(1)}, bf16[128,256]{1,0:T(8,128)(2,1)S(1)}, bf16[4,128,128]{2,1,0:T(8,128)(2,1)S(1)}) custom-call(s32[4,16]{1,0:T(4,128)} %cols.1, s32[4]{0:T(128)} %counts.1, bf16[4,16,128,128]{3,2,1,0:T(8,128)(2,1)} %vals.1, bf16[512,256]{1,0:T(8,128)(2,1)} %refs_0_.1, ...), custom_call_target="tpu_custom_call" | custom-call | tf_op jit(solution)/shard_map/stage/pallas_call | solution.py:55
  10.0 1.4 %collective-permute-done.7.refs_9_ = bf16[4,128,128]{2,1,0:T(8,128)(2,1)S(1)} collective-permute-done((bf16[4,128,128]{2,1,0:T(8,128)(2,1)}, bf16[4,128,128]{2,1,0:T(8,128)(2,1)S(1)}, u32[]{:S(2)}, u32[]{:S(2)}) %collective-permute-start.7) | collective-permute-done | bytes 131104 | tf_op jit(solution)/shard_map/ppermute | solution.py:89
  11.4 0.7 %collective-permute-start.11 = (bf16[4,128,128]{2,1,0:T(8,128)(2,1)S(1)}, bf16[4,128,128]{2,1,0:T(8,128)(2,1)S(1)}, u32[]{:S(2)}, u32[]{:S(2)}) collective-permute-start(bf16[4,128,128]{2,1,0:T(8,128)(2,1)S(1)} %collective-permute-done.7.refs_9_), channel_id=1, source_target_pairs={{0,4},{1,5},{2,6},{3,7},{4,0},{5,1},{6,2},{7,3},{8,12},{9,13},{10,... | collective-permute-start | bytes 393224 | tf_op jit(solution)/shard_map/ppermute | solution.py:89
  12.1 1.5 %collective-permute-start.9 = (bf16[4,128,128]{2,1,0:T(8,128)(2,1)S(1)}, bf16[4,128,128]{2,1,0:T(8,128)(2,1)S(1)}, u32[]{:S(2)}, u32[]{:S(2)}) collective-permute-start(bf16[4,128,128]{2,1,0:T(8,128)(2,1)S(1)} %collective-permute-done.7.refs_9_), channel_id=1, source_target_pairs={{0,2},{1,3},{2,0},{3,1},{4,6},{5,7},{6,4},{7,5},{8,10},{9,11},{10,... | collective-permute-start | bytes 393224 | tf_op jit(solution)/shard_map/ppermute | solution.py:89
  13.6 0.0 collective-permute-done.3.refs_5_
  13.6 0.0 collective-permute-start.8
  13.6 0.0 collective-permute-done.1.refs_3_
  13.6 0.5 collective-permute-start.4
  14.1 0.0 collective-permute-done.refs_2_
  14.1 1.4 %collective-permute-start.5 = (bf16[4,128,128]{2,1,0:T(8,128)(2,1)S(1)}, bf16[4,128,128]{2,1,0:T(8,128)(2,1)S(1)}, u32[]{:S(2)}, u32[]{:S(2)}) collective-permute-start(bf16[4,128,128]{2,1,0:T(8,128)(2,1)S(1)} %collective-permute-done.1.refs_3_), channel_id=1, source_target_pairs={{0,4},{1,5},{2,6},{3,7},{4,0},{5,1},{6,2},{7,3},{8,12},{9,13},{10,... | collective-permute-start | bytes 393224 | tf_op jit(solution)/shard_map/ppermute | solution.py:89
  15.5 0.8 %collective-permute-done.11.refs_13_ = bf16[4,128,128]{2,1,0:T(8,128)(2,1)S(1)} collective-permute-done((bf16[4,128,128]{2,1,0:T(8,128)(2,1)S(1)}, bf16[4,128,128]{2,1,0:T(8,128)(2,1)S(1)}, u32[]{:S(2)}, u32[]{:S(2)}) %collective-permute-start.11) | collective-permute-done | bytes 131104 | tf_op jit(solution)/shard_map/ppermute | solution.py:89
  16.3 2.2 %collective-permute-start.13 = (bf16[4,128,128]{2,1,0:T(8,128)(2,1)S(1)}, bf16[4,128,128]{2,1,0:T(8,128)(2,1)S(1)}, u32[]{:S(2)}, u32[]{:S(2)}) collective-permute-start(bf16[4,128,128]{2,1,0:T(8,128)(2,1)S(1)} %collective-permute-done.11.refs_13_), channel_id=1, source_target_pairs={{0,2},{1,3},{2,0},{3,1},{4,6},{5,7},{6,4},{7,5},{8,10},{9,11},{10,... | collective-permute-start | bytes 393224 | tf_op jit(solution)/shard_map/ppermute | solution.py:89
  18.5 0.0 collective-permute-done.9.refs_11_
  18.5 0.0 collective-permute-start.2
  18.5 0.0 collective-permute-done.8.refs_10_
  18.5 0.5 collective-permute-start.12
  19.0 0.0 collective-permute-done.4.refs_6_
  19.0 0.1 collective-permute-start.10
  19.1 0.5 collective-permute-done.5.refs_7_
  19.6 0.0 collective-permute-start.6
  19.6 1.9 %collective-permute-done.13.refs_15_ = bf16[4,128,128]{2,1,0:T(8,128)(2,1)S(1)} collective-permute-done((bf16[4,128,128]{2,1,0:T(8,128)(2,1)S(1)}, bf16[4,128,128]{2,1,0:T(8,128)(2,1)S(1)}, u32[]{:S(2)}, u32[]{:S(2)}) %collective-permute-start.13) | collective-permute-done | bytes 131104 | tf_op jit(solution)/shard_map/ppermute | solution.py:89
  21.5 0.0 collective-permute-start.14
  21.5 0.0 collective-permute-done.2.refs_4_
  21.5 0.0 collective-permute-done.10.refs_12_
  21.5 0.0 collective-permute-done.6.refs_8_
  21.5 0.0 collective-permute-done.12.refs_14_
  21.5 1.3 %collective-permute-done.14.refs_16_ = bf16[4,128,128]{2,1,0:T(8,128)(2,1)S(1)} collective-permute-done((bf16[4,128,128]{2,1,0:T(8,128)(2,1)S(1)}, bf16[4,128,128]{2,1,0:T(8,128)(2,1)S(1)}, u32[]{:S(2)}, u32[]{:S(2)}) %collective-permute-start.14) | collective-permute-done | bytes 131104 | tf_op jit(solution)/shard_map/ppermute | solution.py:89
  22.8 2.4 %forward.1 = (bf16[512,256]{1,0:T(8,128)(2,1)S(1)}, bf16[4,128,128]{2,1,0:T(8,128)(2,1)S(1)}, f32[64,256]{1,0:T(8,128)S(1)}, f32[64,256]{1,0:T(8,128)S(1)}) custom-call(s32[4,16]{1,0:T(4,128)S(4)} %get-tuple-element.18.refs_0_, bf16[4,128,128]{2,1,0:T(8,128)(2,1)S(1)} %get-tuple-element.19.refs_1_, bf16[4,128,128]{2,1,0:T(8,128)(2,1)S(1)} %collective-permute-done.refs_2_, ...), custom_call_target="tpu_custom_call" | custom-call | tf_op jit(solution)/shard_map/forward/pallas_call | solution.py:247
  25.3 2.6 %collective-permute-start.22 = (bf16[4,128,128]{2,1,0:T(8,128)(2,1)S(1)}, bf16[4,128,128]{2,1,0:T(8,128)(2,1)S(1)}, u32[]{:S(2)}, u32[]{:S(2)}) collective-permute-start(bf16[4,128,128]{2,1,0:T(8,128)(2,1)S(1)} %get-tuple-element.25.refs_1_), channel_id=1, source_target_pairs={{0,8},{1,9},{2,10},{3,11},{4,12},{5,13},{6,14},{7,15},{8,0},{9,1},... | collective-permute-start | bytes 393224 | tf_op jit(solution)/shard_map/ppermute | solution.py:89
  27.9 2.2 %collective-permute-start.18 = (bf16[4,128,128]{2,1,0:T(8,128)(2,1)S(1)}, bf16[4,128,128]{2,1,0:T(8,128)(2,1)S(1)}, u32[]{:S(2)}, u32[]{:S(2)}) collective-permute-start(bf16[4,128,128]{2,1,0:T(8,128)(2,1)S(1)} %get-tuple-element.25.refs_1_), channel_id=1, source_target_pairs={{0,4},{1,5},{2,6},{3,7},{4,0},{5,1},{6,2},{7,3},{8,12},{9,13},{10,... | collective-permute-start | bytes 393224 | tf_op jit(solution)/shard_map/ppermute | solution.py:89
  30.0 2.0 %collective-permute-start.16 = (bf16[4,128,128]{2,1,0:T(8,128)(2,1)S(1)}, bf16[4,128,128]{2,1,0:T(8,128)(2,1)S(1)}, u32[]{:S(2)}, u32[]{:S(2)}) collective-permute-start(bf16[4,128,128]{2,1,0:T(8,128)(2,1)S(1)} %get-tuple-element.25.refs_1_), channel_id=1, source_target_pairs={{0,2},{1,3},{2,0},{3,1},{4,6},{5,7},{6,4},{7,5},{8,10},{9,11},{10,... | collective-permute-start | bytes 393224 | tf_op jit(solution)/shard_map/ppermute | solution.py:89
  32.1 0.3 collective-permute-start.31
  32.4 0.0 collective-permute-start.15
  32.4 0.7 %unstage.1 = bf16[512,256]{1,0:T(8,128)(2,1)} custom-call(bf16[512,256]{1,0:T(8,128)(2,1)S(1)} %get-tuple-element.24.x), custom_call_target="tpu_custom_call" | custom-call | tf_op jit(solution)/shard_map/unstage/pallas_call | solution.py:77
  33.1 1.6 %collective-permute-done.22.refs_9_ = bf16[4,128,128]{2,1,0:T(8,128)(2,1)S(1)} collective-permute-done((bf16[4,128,128]{2,1,0:T(8,128)(2,1)S(1)}, bf16[4,128,128]{2,1,0:T(8,128)(2,1)S(1)}, u32[]{:S(2)}, u32[]{:S(2)}) %collective-permute-start.22) | collective-permute-done | bytes 131104 | tf_op jit(solution)/shard_map/ppermute | solution.py:89
  34.7 0.6 %collective-permute-start.26 = (bf16[4,128,128]{2,1,0:T(8,128)(2,1)S(1)}, bf16[4,128,128]{2,1,0:T(8,128)(2,1)S(1)}, u32[]{:S(2)}, u32[]{:S(2)}) collective-permute-start(bf16[4,128,128]{2,1,0:T(8,128)(2,1)S(1)} %collective-permute-done.22.refs_9_), channel_id=1, source_target_pairs={{0,4},{1,5},{2,6},{3,7},{4,0},{5,1},{6,2},{7,3},{8,12},{9,13},{10,... | collective-permute-start | bytes 393224 | tf_op jit(solution)/shard_map/ppermute | solution.py:89
  35.3 3.2 %collective-permute-done.31 = f32[64,256]{1,0:T(8,128)S(1)} collective-permute-done((f32[64,256]{1,0:T(8,128)S(1)}, f32[64,256]{1,0:T(8,128)S(1)}, u32[]{:S(2)}, u32[]{:S(2)}) %collective-permute-start.31) | collective-permute-done | bytes 65568 | tf_op jit(solution)/shard_map/ppermute | solution.py:89
  38.5 0.1 collective-permute-start.32
  38.6 0.0 collective-permute-done.18.refs_5_
  38.6 1.6 %collective-permute-start.24 = (bf16[4,128,128]{2,1,0:T(8,128)(2,1)S(1)}, bf16[4,128,128]{2,1,0:T(8,128)(2,1)S(1)}, u32[]{:S(2)}, u32[]{:S(2)}) collective-permute-start(bf16[4,128,128]{2,1,0:T(8,128)(2,1)S(1)} %collective-permute-done.22.refs_9_), channel_id=1, source_target_pairs={{0,2},{1,3},{2,0},{3,1},{4,6},{5,7},{6,4},{7,5},{8,10},{9,11},{10,... | collective-permute-start | bytes 393224 | tf_op jit(solution)/shard_map/ppermute | solution.py:89
  40.2 0.0 collective-permute-done.16.refs_3_
  40.2 0.5 collective-permute-start.19
  40.7 2.1 %collective-permute-done.32 = f32[64,256]{1,0:T(8,128)S(1)} collective-permute-done((f32[64,256]{1,0:T(8,128)S(1)}, f32[64,256]{1,0:T(8,128)S(1)}, u32[]{:S(2)}, u32[]{:S(2)}) %collective-permute-start.32) | collective-permute-done | bytes 65568 | tf_op jit(solution)/shard_map/ppermute | solution.py:89
  42.8 0.0 collective-permute-start.20
  42.8 0.0 collective-permute-done.26.refs_13_
  42.8 1.6 %collective-permute-start.28 = (bf16[4,128,128]{2,1,0:T(8,128)(2,1)S(1)}, bf16[4,128,128]{2,1,0:T(8,128)(2,1)S(1)}, u32[]{:S(2)}, u32[]{:S(2)}) collective-permute-start(bf16[4,128,128]{2,1,0:T(8,128)(2,1)S(1)} %collective-permute-done.26.refs_13_), channel_id=1, source_target_pairs={{0,2},{1,3},{2,0},{3,1},{4,6},{5,7},{6,4},{7,5},{8,10},{9,11},{10,... | collective-permute-start | bytes 393224 | tf_op jit(solution)/shard_map/ppermute | solution.py:89
  44.5 0.0 collective-permute-done.24.refs_11_
  44.5 0.1 collective-permute-start.17
  44.6 0.6 %collective-permute-start.33 = (f32[64,256]{1,0:T(8,128)S(1)}, f32[64,256]{1,0:T(8,128)S(1)}, u32[]{:S(2)}, u32[]{:S(2)}) collective-permute-start(f32[64,256]{1,0:T(8,128)S(1)} %add.14), channel_id=1, source_target_pairs={{0,2},{1,3},{2,0},{3,1},{4,6},{5,7},{6,4},{7,5},{8,10},{9,11},{10,... | collective-permute-start | bytes 196616 | tf_op jit(solution)/shard_map/ppermute | solution.py:89
  45.2 0.2 collective-permute-start.27
  45.4 2.4 %collective-permute-done.20.refs_7_ = bf16[4,128,128]{2,1,0:T(8,128)(2,1)S(1)} collective-permute-done((bf16[4,128,128]{2,1,0:T(8,128)(2,1)S(1)}, bf16[4,128,128]{2,1,0:T(8,128)(2,1)S(1)}, u32[]{:S(2)}, u32[]{:S(2)}) %collective-permute-start.20) | collective-permute-done | bytes 131104 | tf_op jit(solution)/shard_map/ppermute | solution.py:89
  47.8 1.4 %collective-permute-done.33 = f32[64,256]{1,0:T(8,128)S(1)} collective-permute-done((f32[64,256]{1,0:T(8,128)S(1)}, f32[64,256]{1,0:T(8,128)S(1)}, u32[]{:S(2)}, u32[]{:S(2)}) %collective-permute-start.33) | collective-permute-done | bytes 65568 | tf_op jit(solution)/shard_map/ppermute | solution.py:89
  49.2 0.0 collective-permute-start.21
  49.2 0.0 collective-permute-done.28.refs_15_
  49.2 0.5 collective-permute-start.29
  49.7 0.0 collective-permute-done.17.refs_4_
  49.8 0.1 collective-permute-start.34
  49.8 1.2 %collective-permute-done.34.refs_19_ = f32[64,256]{1,0:T(8,128)S(1)} collective-permute-done((f32[64,256]{1,0:T(8,128)S(1)}, f32[64,256]{1,0:T(8,128)S(1)}, u32[]{:S(2)}, u32[]{:S(2)}) %collective-permute-start.34) | collective-permute-done | bytes 65568 | tf_op jit(solution)/shard_map/ppermute | solution.py:89
  51.1 0.0 collective-permute-done.29.refs_16_
  51.1 1.5 %backward.1 = (bf16[512,128]{1,0:T(8,128)(2,1)}, f32[128,256]{1,0:T(8,128)}) custom-call(s32[4,16]{1,0:T(4,128)S(4)} %get-tuple-element.18.refs_0_, bf16[4,128,128]{2,1,0:T(8,128)(2,1)S(1)} %get-tuple-element.25.refs_1_, bf16[4,128,128]{2,1,0:T(8,128)(2,1)S(1)} %collective-permute-done.15.refs_2_, bf16[4,128,128]{2,1,0:T(8,128)(2,1)S(1)} %collective-permute-done.16.refs_3_, ...), custom_call_target="tpu_custom_call" | custom-call | tf_op jit(solution)/shard_map/backward/pallas_call | solution.py:265
  (14 shorter events, 0.1 us)
Async XLA Ops:
  0.6 10.7 %collective-permute-start.7 = (bf16[4,128,128]{2,1,0:T(8,128)(2,1)}, bf16[4,128,128]{2,1,0:T(8,128)(2,1)S(1)}, u32[]{:S(2)}, u32[]{:S(2)}) collective-permute-start(bf16[4,128,128]{2,1,0:T(8,128)(2,1)} %bitcast.1), channel_id=1, source_target_pairs={{0,8},{1,9},{2,10},{3,11},{4,12},{5,13},{6,14},{7,15},{8,0},{9,1},... | collective-permute-start | bytes 393224 | tf_op jit(solution)/shard_map/ppermute | solution.py:89
  4.7 8.9 %collective-permute-start.3 = (bf16[4,128,128]{2,1,0:T(8,128)(2,1)}, bf16[4,128,128]{2,1,0:T(8,128)(2,1)S(1)}, u32[]{:S(2)}, u32[]{:S(2)}) collective-permute-start(bf16[4,128,128]{2,1,0:T(8,128)(2,1)} %bitcast.2), channel_id=1, source_target_pairs={{0,4},{1,5},{2,6},{3,7},{4,0},{5,1},{6,2},{7,3},{8,12},{9,13},{10,... | collective-permute-start | bytes 393224 | tf_op jit(solution)/shard_map/ppermute | solution.py:89
  6.3 7.3 %collective-permute-start.1 = (bf16[4,128,128]{2,1,0:T(8,128)(2,1)}, bf16[4,128,128]{2,1,0:T(8,128)(2,1)S(1)}, u32[]{:S(2)}, u32[]{:S(2)}) collective-permute-start(bf16[4,128,128]{2,1,0:T(8,128)(2,1)} %bitcast.3), channel_id=1, source_target_pairs={{0,2},{1,3},{2,0},{3,1},{4,6},{5,7},{6,4},{7,5},{8,10},{9,11},{10,... | collective-permute-start | bytes 393224 | tf_op jit(solution)/shard_map/ppermute | solution.py:89
  7.8 6.3 %collective-permute-start = (bf16[4,128,128]{2,1,0:T(8,128)(2,1)}, bf16[4,128,128]{2,1,0:T(8,128)(2,1)S(1)}, u32[]{:S(2)}, u32[]{:S(2)}) collective-permute-start(bf16[4,128,128]{2,1,0:T(8,128)(2,1)} %bitcast.4), channel_id=1, source_target_pairs={{0,1},{1,0},{2,3},{3,2},{4,5},{5,4},{6,7},{7,6},{8,9},{9,8},{10,11... | collective-permute-start | bytes 393224 | tf_op jit(solution)/shard_map/ppermute | solution.py:89
  11.4 5.0 %collective-permute-start.11 = (bf16[4,128,128]{2,1,0:T(8,128)(2,1)S(1)}, bf16[4,128,128]{2,1,0:T(8,128)(2,1)S(1)}, u32[]{:S(2)}, u32[]{:S(2)}) collective-permute-start(bf16[4,128,128]{2,1,0:T(8,128)(2,1)S(1)} %collective-permute-done.7.refs_9_), channel_id=1, source_target_pairs={{0,4},{1,5},{2,6},{3,7},{4,0},{5,1},{6,2},{7,3},{8,12},{9,13},{10,... | collective-permute-start | bytes 393224 | tf_op jit(solution)/shard_map/ppermute | solution.py:89
  12.1 6.4 %collective-permute-start.9 = (bf16[4,128,128]{2,1,0:T(8,128)(2,1)S(1)}, bf16[4,128,128]{2,1,0:T(8,128)(2,1)S(1)}, u32[]{:S(2)}, u32[]{:S(2)}) collective-permute-start(bf16[4,128,128]{2,1,0:T(8,128)(2,1)S(1)} %collective-permute-done.7.refs_9_), channel_id=1, source_target_pairs={{0,2},{1,3},{2,0},{3,1},{4,6},{5,7},{6,4},{7,5},{8,10},{9,11},{10,... | collective-permute-start | bytes 393224 | tf_op jit(solution)/shard_map/ppermute | solution.py:89
  13.6 4.9 %collective-permute-start.8 = (bf16[4,128,128]{2,1,0:T(8,128)(2,1)S(1)}, bf16[4,128,128]{2,1,0:T(8,128)(2,1)S(1)}, u32[]{:S(2)}, u32[]{:S(2)}) collective-permute-start(bf16[4,128,128]{2,1,0:T(8,128)(2,1)S(1)} %collective-permute-done.7.refs_9_), channel_id=1, source_target_pairs={{0,1},{1,0},{2,3},{3,2},{4,5},{5,4},{6,7},{7,6},{8,9},{9,8},{10,11... | collective-permute-start | bytes 393224 | tf_op jit(solution)/shard_map/ppermute | solution.py:89
  13.6 5.4 %collective-permute-start.4 = (bf16[4,128,128]{2,1,0:T(8,128)(2,1)S(1)}, bf16[4,128,128]{2,1,0:T(8,128)(2,1)S(1)}, u32[]{:S(2)}, u32[]{:S(2)}) collective-permute-start(bf16[4,128,128]{2,1,0:T(8,128)(2,1)S(1)} %collective-permute-done.3.refs_5_), channel_id=1, source_target_pairs={{0,1},{1,0},{2,3},{3,2},{4,5},{5,4},{6,7},{7,6},{8,9},{9,8},{10,11... | collective-permute-start | bytes 393224 | tf_op jit(solution)/shard_map/ppermute | solution.py:89
  14.1 5.5 %collective-permute-start.5 = (bf16[4,128,128]{2,1,0:T(8,128)(2,1)S(1)}, bf16[4,128,128]{2,1,0:T(8,128)(2,1)S(1)}, u32[]{:S(2)}, u32[]{:S(2)}) collective-permute-start(bf16[4,128,128]{2,1,0:T(8,128)(2,1)S(1)} %collective-permute-done.1.refs_3_), channel_id=1, source_target_pairs={{0,4},{1,5},{2,6},{3,7},{4,0},{5,1},{6,2},{7,3},{8,12},{9,13},{10,... | collective-permute-start | bytes 393224 | tf_op jit(solution)/shard_map/ppermute | solution.py:89
  16.3 5.1 %collective-permute-start.13 = (bf16[4,128,128]{2,1,0:T(8,128)(2,1)S(1)}, bf16[4,128,128]{2,1,0:T(8,128)(2,1)S(1)}, u32[]{:S(2)}, u32[]{:S(2)}) collective-permute-start(bf16[4,128,128]{2,1,0:T(8,128)(2,1)S(1)} %collective-permute-done.11.refs_13_), channel_id=1, source_target_pairs={{0,2},{1,3},{2,0},{3,1},{4,6},{5,7},{6,4},{7,5},{8,10},{9,11},{10,... | collective-permute-start | bytes 393224 | tf_op jit(solution)/shard_map/ppermute | solution.py:89
  18.5 2.9 %collective-permute-start.2 = (bf16[4,128,128]{2,1,0:T(8,128)(2,1)S(1)}, bf16[4,128,128]{2,1,0:T(8,128)(2,1)S(1)}, u32[]{:S(2)}, u32[]{:S(2)}) collective-permute-start(bf16[4,128,128]{2,1,0:T(8,128)(2,1)S(1)} %collective-permute-done.1.refs_3_), channel_id=1, source_target_pairs={{0,1},{1,0},{2,3},{3,2},{4,5},{5,4},{6,7},{7,6},{8,9},{9,8},{10,11... | collective-permute-start | bytes 393224 | tf_op jit(solution)/shard_map/ppermute | solution.py:89
  18.5 3.0 %collective-permute-start.12 = (bf16[4,128,128]{2,1,0:T(8,128)(2,1)S(1)}, bf16[4,128,128]{2,1,0:T(8,128)(2,1)S(1)}, u32[]{:S(2)}, u32[]{:S(2)}) collective-permute-start(bf16[4,128,128]{2,1,0:T(8,128)(2,1)S(1)} %collective-permute-done.11.refs_13_), channel_id=1, source_target_pairs={{0,1},{1,0},{2,3},{3,2},{4,5},{5,4},{6,7},{7,6},{8,9},{9,8},{10,11... | collective-permute-start | bytes 393224 | tf_op jit(solution)/shard_map/ppermute | solution.py:89
  19.0 2.4 %collective-permute-start.10 = (bf16[4,128,128]{2,1,0:T(8,128)(2,1)S(1)}, bf16[4,128,128]{2,1,0:T(8,128)(2,1)S(1)}, u32[]{:S(2)}, u32[]{:S(2)}) collective-permute-start(bf16[4,128,128]{2,1,0:T(8,128)(2,1)S(1)} %collective-permute-done.9.refs_11_), channel_id=1, source_target_pairs={{0,1},{1,0},{2,3},{3,2},{4,5},{5,4},{6,7},{7,6},{8,9},{9,8},{10,11... | collective-permute-start | bytes 393224 | tf_op jit(solution)/shard_map/ppermute | solution.py:89
  19.6 1.9 %collective-permute-start.6 = (bf16[4,128,128]{2,1,0:T(8,128)(2,1)S(1)}, bf16[4,128,128]{2,1,0:T(8,128)(2,1)S(1)}, u32[]{:S(2)}, u32[]{:S(2)}) collective-permute-start(bf16[4,128,128]{2,1,0:T(8,128)(2,1)S(1)} %collective-permute-done.5.refs_7_), channel_id=1, source_target_pairs={{0,1},{1,0},{2,3},{3,2},{4,5},{5,4},{6,7},{7,6},{8,9},{9,8},{10,11... | collective-permute-start | bytes 393224 | tf_op jit(solution)/shard_map/ppermute | solution.py:89
  21.5 1.3 %collective-permute-start.14 = (bf16[4,128,128]{2,1,0:T(8,128)(2,1)S(1)}, bf16[4,128,128]{2,1,0:T(8,128)(2,1)S(1)}, u32[]{:S(2)}, u32[]{:S(2)}) collective-permute-start(bf16[4,128,128]{2,1,0:T(8,128)(2,1)S(1)} %collective-permute-done.13.refs_15_), channel_id=1, source_target_pairs={{0,1},{1,0},{2,3},{3,2},{4,5},{5,4},{6,7},{7,6},{8,9},{9,8},{10,11... | collective-permute-start | bytes 393224 | tf_op jit(solution)/shard_map/ppermute | solution.py:89
  25.3 9.4 %collective-permute-start.22 = (bf16[4,128,128]{2,1,0:T(8,128)(2,1)S(1)}, bf16[4,128,128]{2,1,0:T(8,128)(2,1)S(1)}, u32[]{:S(2)}, u32[]{:S(2)}) collective-permute-start(bf16[4,128,128]{2,1,0:T(8,128)(2,1)S(1)} %get-tuple-element.25.refs_1_), channel_id=1, source_target_pairs={{0,8},{1,9},{2,10},{3,11},{4,12},{5,13},{6,14},{7,15},{8,0},{9,1},... | collective-permute-start | bytes 393224 | tf_op jit(solution)/shard_map/ppermute | solution.py:89
  27.9 4.2 %collective-permute-start.30 = (f32[64,256]{1,0:T(8,128)S(1)}, f32[64,256]{1,0:T(8,128)S(1)}, u32[]{:S(2)}, u32[]{:S(2)}) collective-permute-start(f32[64,256]{1,0:T(8,128)S(1)} %get-tuple-element.28), channel_id=1, source_target_pairs={{0,1},{1,0},{2,3},{3,2},{4,5},{5,4},{6,7},{7,6},{8,9},{9,8},{10,11... | collective-permute-start | bytes 196616 | tf_op jit(solution)/shard_map/ppermute | solution.py:89
  27.9 10.7 %collective-permute-start.18 = (bf16[4,128,128]{2,1,0:T(8,128)(2,1)S(1)}, bf16[4,128,128]{2,1,0:T(8,128)(2,1)S(1)}, u32[]{:S(2)}, u32[]{:S(2)}) collective-permute-start(bf16[4,128,128]{2,1,0:T(8,128)(2,1)S(1)} %get-tuple-element.25.refs_1_), channel_id=1, source_target_pairs={{0,4},{1,5},{2,6},{3,7},{4,0},{5,1},{6,2},{7,3},{8,12},{9,13},{10,... | collective-permute-start | bytes 393224 | tf_op jit(solution)/shard_map/ppermute | solution.py:89
  30.0 10.2 %collective-permute-start.16 = (bf16[4,128,128]{2,1,0:T(8,128)(2,1)S(1)}, bf16[4,128,128]{2,1,0:T(8,128)(2,1)S(1)}, u32[]{:S(2)}, u32[]{:S(2)}) collective-permute-start(bf16[4,128,128]{2,1,0:T(8,128)(2,1)S(1)} %get-tuple-element.25.refs_1_), channel_id=1, source_target_pairs={{0,2},{1,3},{2,0},{3,1},{4,6},{5,7},{6,4},{7,5},{8,10},{9,11},{10,... | collective-permute-start | bytes 393224 | tf_op jit(solution)/shard_map/ppermute | solution.py:89
  32.1 6.4 %collective-permute-start.31 = (f32[64,256]{1,0:T(8,128)S(1)}, f32[64,256]{1,0:T(8,128)S(1)}, u32[]{:S(2)}, u32[]{:S(2)}) collective-permute-start(f32[64,256]{1,0:T(8,128)S(1)} %add.12), channel_id=1, source_target_pairs={{0,8},{1,9},{2,10},{3,11},{4,12},{5,13},{6,14},{7,15},{8,0},{9,1},... | collective-permute-start | bytes 196616 | tf_op jit(solution)/shard_map/ppermute | solution.py:89
  32.4 7.8 %collective-permute-start.15 = (bf16[4,128,128]{2,1,0:T(8,128)(2,1)S(1)}, bf16[4,128,128]{2,1,0:T(8,128)(2,1)S(1)}, u32[]{:S(2)}, u32[]{:S(2)}) collective-permute-start(bf16[4,128,128]{2,1,0:T(8,128)(2,1)S(1)} %get-tuple-element.25.refs_1_), channel_id=1, source_target_pairs={{0,1},{1,0},{2,3},{3,2},{4,5},{5,4},{6,7},{7,6},{8,9},{9,8},{10,11... | collective-permute-start | bytes 393224 | tf_op jit(solution)/shard_map/ppermute | solution.py:89
  34.7 8.2 %collective-permute-start.26 = (bf16[4,128,128]{2,1,0:T(8,128)(2,1)S(1)}, bf16[4,128,128]{2,1,0:T(8,128)(2,1)S(1)}, u32[]{:S(2)}, u32[]{:S(2)}) collective-permute-start(bf16[4,128,128]{2,1,0:T(8,128)(2,1)S(1)} %collective-permute-done.22.refs_9_), channel_id=1, source_target_pairs={{0,4},{1,5},{2,6},{3,7},{4,0},{5,1},{6,2},{7,3},{8,12},{9,13},{10,... | collective-permute-start | bytes 393224 | tf_op jit(solution)/shard_map/ppermute | solution.py:89
  38.5 4.3 %collective-permute-start.32 = (f32[64,256]{1,0:T(8,128)S(1)}, f32[64,256]{1,0:T(8,128)S(1)}, u32[]{:S(2)}, u32[]{:S(2)}) collective-permute-start(f32[64,256]{1,0:T(8,128)S(1)} %add.13), channel_id=1, source_target_pairs={{0,4},{1,5},{2,6},{3,7},{4,0},{5,1},{6,2},{7,3},{8,12},{9,13},{10,... | collective-permute-start | bytes 196616 | tf_op jit(solution)/shard_map/ppermute | solution.py:89
  38.6 5.9 %collective-permute-start.24 = (bf16[4,128,128]{2,1,0:T(8,128)(2,1)S(1)}, bf16[4,128,128]{2,1,0:T(8,128)(2,1)S(1)}, u32[]{:S(2)}, u32[]{:S(2)}) collective-permute-start(bf16[4,128,128]{2,1,0:T(8,128)(2,1)S(1)} %collective-permute-done.22.refs_9_), channel_id=1, source_target_pairs={{0,2},{1,3},{2,0},{3,1},{4,6},{5,7},{6,4},{7,5},{8,10},{9,11},{10,... | collective-permute-start | bytes 393224 | tf_op jit(solution)/shard_map/ppermute | solution.py:89
  40.2 4.4 %collective-permute-start.23 = (bf16[4,128,128]{2,1,0:T(8,128)(2,1)S(1)}, bf16[4,128,128]{2,1,0:T(8,128)(2,1)S(1)}, u32[]{:S(2)}, u32[]{:S(2)}) collective-permute-start(bf16[4,128,128]{2,1,0:T(8,128)(2,1)S(1)} %collective-permute-done.22.refs_9_), channel_id=1, source_target_pairs={{0,1},{1,0},{2,3},{3,2},{4,5},{5,4},{6,7},{7,6},{8,9},{9,8},{10,11... | collective-permute-start | bytes 393224 | tf_op jit(solution)/shard_map/ppermute | solution.py:89
  40.2 5.0 %collective-permute-start.19 = (bf16[4,128,128]{2,1,0:T(8,128)(2,1)S(1)}, bf16[4,128,128]{2,1,0:T(8,128)(2,1)S(1)}, u32[]{:S(2)}, u32[]{:S(2)}) collective-permute-start(bf16[4,128,128]{2,1,0:T(8,128)(2,1)S(1)} %collective-permute-done.18.refs_5_), channel_id=1, source_target_pairs={{0,1},{1,0},{2,3},{3,2},{4,5},{5,4},{6,7},{7,6},{8,9},{9,8},{10,11... | collective-permute-start | bytes 393224 | tf_op jit(solution)/shard_map/ppermute | solution.py:89
  42.8 5.0 %collective-permute-start.20 = (bf16[4,128,128]{2,1,0:T(8,128)(2,1)S(1)}, bf16[4,128,128]{2,1,0:T(8,128)(2,1)S(1)}, u32[]{:S(2)}, u32[]{:S(2)}) collective-permute-start(bf16[4,128,128]{2,1,0:T(8,128)(2,1)S(1)} %collective-permute-done.16.refs_3_), channel_id=1, source_target_pairs={{0,4},{1,5},{2,6},{3,7},{4,0},{5,1},{6,2},{7,3},{8,12},{9,13},{10,... | collective-permute-start | bytes 393224 | tf_op jit(solution)/shard_map/ppermute | solution.py:89
  42.8 6.4 %collective-permute-start.28 = (bf16[4,128,128]{2,1,0:T(8,128)(2,1)S(1)}, bf16[4,128,128]{2,1,0:T(8,128)(2,1)S(1)}, u32[]{:S(2)}, u32[]{:S(2)}) collective-permute-start(bf16[4,128,128]{2,1,0:T(8,128)(2,1)S(1)} %collective-permute-done.26.refs_13_), channel_id=1, source_target_pairs={{0,2},{1,3},{2,0},{3,1},{4,6},{5,7},{6,4},{7,5},{8,10},{9,11},{10,... | collective-permute-start | bytes 393224 | tf_op jit(solution)/shard_map/ppermute | solution.py:89
  44.5 5.3 %collective-permute-start.17 = (bf16[4,128,128]{2,1,0:T(8,128)(2,1)S(1)}, bf16[4,128,128]{2,1,0:T(8,128)(2,1)S(1)}, u32[]{:S(2)}, u32[]{:S(2)}) collective-permute-start(bf16[4,128,128]{2,1,0:T(8,128)(2,1)S(1)} %collective-permute-done.16.refs_3_), channel_id=1, source_target_pairs={{0,1},{1,0},{2,3},{3,2},{4,5},{5,4},{6,7},{7,6},{8,9},{9,8},{10,11... | collective-permute-start | bytes 393224 | tf_op jit(solution)/shard_map/ppermute | solution.py:89
  44.6 4.6 %collective-permute-start.33 = (f32[64,256]{1,0:T(8,128)S(1)}, f32[64,256]{1,0:T(8,128)S(1)}, u32[]{:S(2)}, u32[]{:S(2)}) collective-permute-start(f32[64,256]{1,0:T(8,128)S(1)} %add.14), channel_id=1, source_target_pairs={{0,2},{1,3},{2,0},{3,1},{4,6},{5,7},{6,4},{7,5},{8,10},{9,11},{10,... | collective-permute-start | bytes 196616 | tf_op jit(solution)/shard_map/ppermute | solution.py:89
  45.2 5.9 %collective-permute-start.27 = (bf16[4,128,128]{2,1,0:T(8,128)(2,1)S(1)}, bf16[4,128,128]{2,1,0:T(8,128)(2,1)S(1)}, u32[]{:S(2)}, u32[]{:S(2)}) collective-permute-start(bf16[4,128,128]{2,1,0:T(8,128)(2,1)S(1)} %collective-permute-done.26.refs_13_), channel_id=1, source_target_pairs={{0,1},{1,0},{2,3},{3,2},{4,5},{5,4},{6,7},{7,6},{8,9},{9,8},{10,11... | collective-permute-start | bytes 393224 | tf_op jit(solution)/shard_map/ppermute | solution.py:89
  47.8 3.3 %collective-permute-start.25 = (bf16[4,128,128]{2,1,0:T(8,128)(2,1)S(1)}, bf16[4,128,128]{2,1,0:T(8,128)(2,1)S(1)}, u32[]{:S(2)}, u32[]{:S(2)}) collective-permute-start(bf16[4,128,128]{2,1,0:T(8,128)(2,1)S(1)} %collective-permute-done.24.refs_11_), channel_id=1, source_target_pairs={{0,1},{1,0},{2,3},{3,2},{4,5},{5,4},{6,7},{7,6},{8,9},{9,8},{10,11... | collective-permute-start | bytes 393224 | tf_op jit(solution)/shard_map/ppermute | solution.py:89
  49.2 1.9 %collective-permute-start.21 = (bf16[4,128,128]{2,1,0:T(8,128)(2,1)S(1)}, bf16[4,128,128]{2,1,0:T(8,128)(2,1)S(1)}, u32[]{:S(2)}, u32[]{:S(2)}) collective-permute-start(bf16[4,128,128]{2,1,0:T(8,128)(2,1)S(1)} %collective-permute-done.20.refs_7_), channel_id=1, source_target_pairs={{0,1},{1,0},{2,3},{3,2},{4,5},{5,4},{6,7},{7,6},{8,9},{9,8},{10,11... | collective-permute-start | bytes 393224 | tf_op jit(solution)/shard_map/ppermute | solution.py:89
  49.2 1.9 %collective-permute-start.29 = (bf16[4,128,128]{2,1,0:T(8,128)(2,1)S(1)}, bf16[4,128,128]{2,1,0:T(8,128)(2,1)S(1)}, u32[]{:S(2)}, u32[]{:S(2)}) collective-permute-start(bf16[4,128,128]{2,1,0:T(8,128)(2,1)S(1)} %collective-permute-done.28.refs_15_), channel_id=1, source_target_pairs={{0,1},{1,0},{2,3},{3,2},{4,5},{5,4},{6,7},{7,6},{8,9},{9,8},{10,11... | collective-permute-start | bytes 393224 | tf_op jit(solution)/shard_map/ppermute | solution.py:89
  49.8 1.3 %collective-permute-start.34 = (f32[64,256]{1,0:T(8,128)S(1)}, f32[64,256]{1,0:T(8,128)S(1)}, u32[]{:S(2)}, u32[]{:S(2)}) collective-permute-start(f32[64,256]{1,0:T(8,128)S(1)} %add.15.refs_18_), channel_id=1, source_target_pairs={{0,1},{1,0},{2,3},{3,2},{4,5},{5,4},{6,7},{7,6},{8,9},{9,8},{10,11... | collective-permute-start | bytes 196616 | tf_op jit(solution)/shard_map/ppermute | solution.py:89

commit v5 on v4

--- a/solution.py
+++ b/solution.py
@@ -43,11 +43,12 @@
     run([pltpu.make_async_copy(i, o, sems.at[k]) for k, (i, o) in enumerate(pairs)])
     panels, slots = vals_out.shape[:2]
     for panel in range(panels):
-        for slot in range(slots):
-
-            @pl.when(slot >= counts_in[panel])
-            def _():
-                vals_out[panel, slot] = jnp.zeros(vals_out.shape[2:], vals_out.dtype)
+
+        def clear(slot, carry):
+            vals_out[panel, slot] = jnp.zeros(vals_out.shape[2:], vals_out.dtype)
+            return carry
+
+        lax.fori_loop(counts_in[panel], slots, clear, 0)
 
 
 def stage(cols, counts, vals, *plain):
@@ -93,48 +94,87 @@
     return lax.optimization_barrier((x, *others))[0]
 
 
-def gather_rows(x, own, size, staged=None):
+def pack_kernel(*refs):
+    out, start = refs[-1], 0
+    for r in refs[:-1]:
+        out[pl.ds(start, r.shape[0])] = r[...]
+        start += r.shape[0]
+
+
+def pack(arrays):
+    if len(arrays) == 1:
+        return arrays[0]
+    first = arrays[0]
+    total = sum(a.shape[0] for a in arrays)
+    return pl.pallas_call(
+        pack_kernel,
+        name="pack",
+        compiler_params=PARAMS,
+        out_shape=pltpu.VMEM((total, *first.shape[1:]), first.dtype),
+        in_specs=[VMEM] * len(arrays),
+        out_specs=VMEM,
+    )(*(in_vmem(a) for a in arrays))
+
+
+CORE_GROUPS = ((0, 2, 4, 8), (6, 10), (12, 14))
+SUM_BITS = (2, 8, 4)
+
+
+def row_sum(keep, send, size, bits):
+    total = keep + exchange(send, 1, size)
+    for bit in bits:
+        total = total + exchange(total, bit, size)
+    return total
+
+
+def gather_rows(x, own, size, staged, halves=None):
+    sums = None
     if size != 16:
-        return [(None, lax.all_gather(x, "row", axis=0, tiled=True))]
-    held = {0: x}
-    held[8] = exchange(x, 8, size)
-    held[4] = exchange(x, 4, size)
-    far = held[8] if staged is None else after(held[8], staged)
-    held[12] = exchange(far, 4, size)
+        if halves is not None:
+            bits = [1 << k for k in range(1, (size - 1).bit_length())]
+            total = row_sum(*halves, size, bits)
+            sums = total, exchange(total, 1, size)
+        return [((None,), lax.all_gather(x, "row", axis=0, tiled=True))], sums
+
+    def step(value, k):
+        return value if halves is None else after(value, totals[k])
+
+    def advance():
+        if halves is not None:
+            bit = SUM_BITS[len(totals) - 1]
+            totals.append(totals[-1] + exchange(totals[-1], bit, size))
+
+    held = {8: exchange(x, 8, size), 4: exchange(x, 4, size)}
+    totals = [] if halves is None else [halves[0] + exchange(halves[1], 1, size)]
+    held[12] = exchange(step(after(held[8], staged), 0), 4, size)
     held[2] = exchange(x, 2, size)
     held[6] = exchange(held[2], 4, size)
-    held[10] = exchange(held[8], 2, size)
-    held[14] = exchange(held[12], 2, size)
-    for mask in (0, 2, 4, 6, 8, 10, 12, 14):
-        held[mask ^ 1] = exchange(held[mask], 1, size)
+    advance()
+    held[10] = exchange(step(held[8], 1), 2, size)
+    advance()
+    held[14] = exchange(step(held[12], 2), 2, size)
+    advance()
+    if halves is not None:
+        sums = totals[-1], exchange(totals[-1], 1, size)
     held[0] = own
-    return sorted(held.items())
-
-
-def row_sum(keep, send, held, size):
-    held = dict(held)
-    total = keep + exchange(send, 1, size)
-    if size == 16:
-        total = total + exchange(total, 8, size)
-        total = total + exchange(after(total, held[8]), 4, size)
-        total = total + exchange(after(total, held[12]), 2, size)
-    else:
-        bit = size // 2
-        while bit > 1:
-            total = total + exchange(total, bit, size)
-            bit //= 2
-    return total, exchange(total, 1, size)
+    pieces = [((mask,), held[mask]) for mask in sorted(held)]
+    for group in CORE_GROUPS:
+        arrays = [held[mask] for mask in group]
+        if group is CORE_GROUPS[-1]:
+            arrays[0] = step(arrays[0], 3)
+        pieces.append((tuple(mask ^ 1 for mask in group), exchange(pack(arrays), 1, size)))
+    return pieces, sums
 
 
 def collect(me, masks, pieces, nodes):
     if nodes is None:
         return pieces[0]
-    rows = pieces[0].shape[0]
-    for mask, piece in zip(masks, pieces):
-        blocks = piece.shape[0]
-        start = (me ^ mask) * blocks
-        for i in range(blocks):
-            nodes[start + i] = piece[i]
+    for each, piece in zip(masks, pieces):
+        blocks = piece.shape[0] // len(each)
+        for k, mask in enumerate(each):
+            start = (me ^ mask) * blocks
+            for i in range(blocks):
+                nodes[start + i] = piece[k * blocks + i]
     return nodes
 
 
@@ -236,14 +276,14 @@
     )
     cols, vals = in_smem(cols), in_vmem(vals)
 
-    def gathered(x, own, staged=None):
-        held = gather_rows(x, own, size, staged)
+    def gathered(*arrays):
+        pieces, sums = gather_rows(*arrays)
         scratch = []
-        if len(held) > 1:
+        if len(pieces) > 1:
             scratch = [pltpu.VMEM((node_blocks, side, width), jnp.bfloat16)]
-        return held, tuple(m for m, _ in held), [in_vmem(a) for _, a in held], scratch
-
-    held, masks, pieces, scratch = gathered(features_in, own_rows, own_rows)
+        return sums, tuple(m for m, _ in pieces), [in_vmem(a) for _, a in pieces], scratch
+
+    _, masks, pieces, scratch = gathered(features_in, own_rows, size, own_rows)
     hidden, edge, keep, send = pl.pallas_call(
         lambda *refs: forward_kernel(masks, *refs),
         name="forward",
@@ -260,8 +300,7 @@
     )(cols, *pieces, vals, in_vmem(weight), in_vmem(out_grad))
 
     hidden = unstage(hidden)
-    held, masks, pieces, scratch = gathered(edge, edge, hidden)
-    own, other = row_sum(keep, send, held, size)
+    (own, other), masks, pieces, scratch = gathered(edge, edge, size, hidden, (keep, send))
     feat_grad, weight_grad = pl.pallas_call(
         lambda *refs: backward_kernel(masks, *refs),
         name="backward",

time: 52.8 us -> 52.4 us (level)
    ppermute x35 -> x25, waiting for transfers between devices: 17.9 us -> 17.5 us  [exchange(): return lax.ppermute(x, 'row', [(i, i ^ bit) for i in range(size)])]
    ppermute x35 -> x25, starting transfers between devices: 27.1 us -> 27.2 us  [exchange(): return lax.ppermute(x, 'row', [(i, i ^ bit) for i in range(size)])]
  transfers between devices with their start and end apart: 35 -> 25, of which waited for: 11 -> 16; matrix products, arithmetic and copies ran while one was open for 0% -> 0% of each run, Pallas kernels for 5% -> 5%
where the time goes in v5:
time: 52.4 us; the launch traced here: 52.2 us
  starting transfers between devices  27.2 us (52%)
  waiting for transfers between devices  17.5 us (33%)
  Pallas kernels  6.78 us (13%)
  between operations  0.78 us (1%)
    ppermute x25, starting transfers between devices, exchange(): return lax.ppermute(x, 'row', [(i, i ^ bit) for i in range(size)])  27.2 us
    ppermute x25, waiting for transfers between devices, exchange(): return lax.ppermute(x, 'row', [(i, i ^ bit) for i in range(size)])  17.5 us
    pallas_call x1, Pallas kernels, body(): pl.pallas_call(lambda *refs: forward_kernel(masks, *refs), name='forward'...  2.43 us
    pallas_call x1, Pallas kernels, stage(): pl.pallas_call(stage_kernel, name='stage', compiler_params=PARAMS, out_sh...  1.98 us
    pallas_call x1, Pallas kernels, body(): pl.pallas_call(lambda *refs: backward_kernel(masks, *refs), name='backwar...  1.52 us
  transfers between devices with their start and end apart: 25, of which 16 were waited for; matrix products, arithmetic and copies ran while one was open for 0% of the time, Pallas kernels for 5%

profile of v5, /device:TPU:0, one launch (start us, length us, event | category | flops | bytes accessed | tf_op | source)
XLA Modules:
  0.0 52.2 jit_solution(8018270944337527051)
XLA Ops:
  0.6 4.1 %collective-permute-start.3 = (bf16[4,128,128]{2,1,0:T(8,128)(2,1)}, bf16[4,128,128]{2,1,0:T(8,128)(2,1)S(1)}, u32[]{:S(2)}, u32[]{:S(2)}) collective-permute-start(bf16[4,128,128]{2,1,0:T(8,128)(2,1)} %bitcast.1), channel_id=1, source_target_pairs={{0,8},{1,9},{2,10},{3,11},{4,12},{5,13},{6,14},{7,15},{8,0},{9,1},... | collective-permute-start | bytes 393224 | tf_op jit(solution)/shard_map/ppermute | solution.py:90
  4.7 1.5 %collective-permute-start = (bf16[4,128,128]{2,1,0:T(8,128)(2,1)}, bf16[4,128,128]{2,1,0:T(8,128)(2,1)S(1)}, u32[]{:S(2)}, u32[]{:S(2)}) collective-permute-start(bf16[4,128,128]{2,1,0:T(8,128)(2,1)} %bitcast.2), channel_id=1, source_target_pairs={{0,2},{1,3},{2,0},{3,1},{4,6},{5,7},{6,4},{7,5},{8,10},{9,11},{10,... | collective-permute-start | bytes 393224 | tf_op jit(solution)/shard_map/ppermute | solution.py:90
  6.3 1.6 %collective-permute-start.1 = (bf16[4,128,128]{2,1,0:T(8,128)(2,1)}, bf16[4,128,128]{2,1,0:T(8,128)(2,1)S(1)}, u32[]{:S(2)}, u32[]{:S(2)}) collective-permute-start(bf16[4,128,128]{2,1,0:T(8,128)(2,1)} %bitcast.3), channel_id=1, source_target_pairs={{0,4},{1,5},{2,6},{3,7},{4,0},{5,1},{6,2},{7,3},{8,12},{9,13},{10,... | collective-permute-start | bytes 393224 | tf_op jit(solution)/shard_map/ppermute | solution.py:90
  7.8 2.0 %stage.1 = (s32[4,16]{1,0:T(4,128)S(4)}, bf16[4,16,128,128]{3,2,1,0:T(8,128)(2,1)S(1)}, bf16[512,256]{1,0:T(8,128)(2,1)S(1)}, bf16[128,256]{1,0:T(8,128)(2,1)S(1)}, bf16[4,128,128]{2,1,0:T(8,128)(2,1)S(1)}) custom-call(s32[4,16]{1,0:T(4,128)} %cols.1, s32[4]{0:T(128)} %counts.1, bf16[4,16,128,128]{3,2,1,0:T(8,128)(2,1)} %vals.1, bf16[512,256]{1,0:T(8,128)(2,1)} %refs_0_.1, ...), custom_call_target="tpu_custom_call" | custom-call | tf_op jit(solution)/shard_map/stage/pallas_call | solution.py:56
  9.8 1.5 %collective-permute-done.3.refs_3_.refs_5_ = bf16[4,128,128]{2,1,0:T(8,128)(2,1)S(1)} collective-permute-done((bf16[4,128,128]{2,1,0:T(8,128)(2,1)}, bf16[4,128,128]{2,1,0:T(8,128)(2,1)S(1)}, u32[]{:S(2)}, u32[]{:S(2)}) %collective-permute-start.3) | collective-permute-done | bytes 131104 | tf_op jit(solution)/shard_map/ppermute | solution.py:90
  11.4 0.8 %collective-permute-start.5 = (bf16[4,128,128]{2,1,0:T(8,128)(2,1)S(1)}, bf16[4,128,128]{2,1,0:T(8,128)(2,1)S(1)}, u32[]{:S(2)}, u32[]{:S(2)}) collective-permute-start(bf16[4,128,128]{2,1,0:T(8,128)(2,1)S(1)} %collective-permute-done.3.refs_3_.refs_5_), channel_id=1, source_target_pairs={{0,4},{1,5},{2,6},{3,7},{4,0},{5,1},{6,2},{7,3},{8,12},{9,13},{10,... | collective-permute-start | bytes 393224 | tf_op jit(solution)/shard_map/ppermute | solution.py:90
  12.1 0.0 collective-permute-done.refs_1_.refs_2_
  12.1 0.7 %collective-permute-done.1.refs_2_.refs_3_ = bf16[4,128,128]{2,1,0:T(8,128)(2,1)S(1)} collective-permute-done((bf16[4,128,128]{2,1,0:T(8,128)(2,1)}, bf16[4,128,128]{2,1,0:T(8,128)(2,1)S(1)}, u32[]{:S(2)}, u32[]{:S(2)}) %collective-permute-start.1) | collective-permute-done | bytes 131104 | tf_op jit(solution)/shard_map/ppermute | solution.py:90
  12.8 0.1 collective-permute-start.7
  12.9 0.7 %collective-permute-start.2 = (bf16[4,128,128]{2,1,0:T(8,128)(2,1)S(1)}, bf16[4,128,128]{2,1,0:T(8,128)(2,1)S(1)}, u32[]{:S(2)}, u32[]{:S(2)}) collective-permute-start(bf16[4,128,128]{2,1,0:T(8,128)(2,1)S(1)} %collective-permute-done.refs_1_.refs_2_), channel_id=1, source_target_pairs={{0,4},{1,5},{2,6},{3,7},{4,0},{5,1},{6,2},{7,3},{8,12},{9,13},{10,... | collective-permute-start | bytes 393224 | tf_op jit(solution)/shard_map/ppermute | solution.py:90
  13.6 1.6 %collective-permute-start.4 = (bf16[4,128,128]{2,1,0:T(8,128)(2,1)S(1)}, bf16[4,128,128]{2,1,0:T(8,128)(2,1)S(1)}, u32[]{:S(2)}, u32[]{:S(2)}) collective-permute-start(bf16[4,128,128]{2,1,0:T(8,128)(2,1)S(1)} %collective-permute-done.3.refs_3_.refs_5_), channel_id=1, source_target_pairs={{0,2},{1,3},{2,0},{3,1},{4,6},{5,7},{6,4},{7,5},{8,10},{9,11},{10,... | collective-permute-start | bytes 393224 | tf_op jit(solution)/shard_map/ppermute | solution.py:90
  15.1 1.5 %collective-permute-done.5.refs_0_.refs_7_ = bf16[4,128,128]{2,1,0:T(8,128)(2,1)S(1)} collective-permute-done((bf16[4,128,128]{2,1,0:T(8,128)(2,1)S(1)}, bf16[4,128,128]{2,1,0:T(8,128)(2,1)S(1)}, u32[]{:S(2)}, u32[]{:S(2)}) %collective-permute-start.5) | collective-permute-done | bytes 131104 | tf_op jit(solution)/shard_map/ppermute | solution.py:90
  16.6 2.3 %collective-permute-start.6 = (bf16[4,128,128]{2,1,0:T(8,128)(2,1)S(1)}, bf16[4,128,128]{2,1,0:T(8,128)(2,1)S(1)}, u32[]{:S(2)}, u32[]{:S(2)}) collective-permute-start(bf16[4,128,128]{2,1,0:T(8,128)(2,1)S(1)} %collective-permute-done.5.refs_0_.refs_7_), channel_id=1, source_target_pairs={{0,2},{1,3},{2,0},{3,1},{4,6},{5,7},{6,4},{7,5},{8,10},{9,11},{10,... | collective-permute-start | bytes 393224 | tf_op jit(solution)/shard_map/ppermute | solution.py:90
  19.0 0.2 collective-permute-done.2.refs_0_.refs_4_
  19.1 0.8 %collective-permute-done.4.refs_1_.refs_6_ = bf16[4,128,128]{2,1,0:T(8,128)(2,1)S(1)} collective-permute-done((bf16[4,128,128]{2,1,0:T(8,128)(2,1)S(1)}, bf16[4,128,128]{2,1,0:T(8,128)(2,1)S(1)}, u32[]{:S(2)}, u32[]{:S(2)}) %collective-permute-start.4) | collective-permute-done | bytes 131104 | tf_op jit(solution)/shard_map/ppermute | solution.py:90
  19.9 0.1 collective-permute-start.8
  20.0 1.9 %collective-permute-done.6.refs_1_.refs_8_ = bf16[4,128,128]{2,1,0:T(8,128)(2,1)S(1)} collective-permute-done((bf16[4,128,128]{2,1,0:T(8,128)(2,1)S(1)}, bf16[4,128,128]{2,1,0:T(8,128)(2,1)S(1)}, u32[]{:S(2)}, u32[]{:S(2)}) %collective-permute-start.6) | collective-permute-done | bytes 131104 | tf_op jit(solution)/shard_map/ppermute | solution.py:90
  22.0 0.1 collective-permute-start.9
  22.1 0.0 collective-permute-done.8.refs_10_
  22.1 0.0 collective-permute-done.7.refs_9_
  22.1 1.5 %collective-permute-done.9.refs_11_ = bf16[8,128,128]{2,1,0:T(8,128)(2,1)S(1)} collective-permute-done((bf16[8,128,128]{2,1,0:T(8,128)(2,1)S(1)}, bf16[8,128,128]{2,1,0:T(8,128)(2,1)S(1)}, u32[]{:S(2)}, u32[]{:S(2)}) %collective-permute-start.9) | collective-permute-done | bytes 262176 | tf_op jit(solution)/shard_map/ppermute | solution.py:90
  23.6 2.4 %forward.1 = (bf16[512,256]{1,0:T(8,128)(2,1)S(1)}, bf16[4,128,128]{2,1,0:T(8,128)(2,1)S(1)}, f32[64,256]{1,0:T(8,128)S(1)}, f32[64,256]{1,0:T(8,128)S(1)}) custom-call(s32[4,16]{1,0:T(4,128)S(4)} %get-tuple-element.20.refs_0_, bf16[4,128,128]{2,1,0:T(8,128)(2,1)S(1)} %get-tuple-element.21.refs_0_.refs_1_, ...), custom_call_target="tpu_custom_call" | custom-call | tf_op jit(solution)/shard_map/forward/pallas_call | solution.py:287
  26.0 2.7 %collective-permute-start.13 = (bf16[4,128,128]{2,1,0:T(8,128)(2,1)S(1)}, bf16[4,128,128]{2,1,0:T(8,128)(2,1)S(1)}, u32[]{:S(2)}, u32[]{:S(2)}) collective-permute-start(bf16[4,128,128]{2,1,0:T(8,128)(2,1)S(1)} %get-tuple-element.27.refs_0_.refs_1_), channel_id=1, source_target_pairs={{0,8},{1,9},{2,10},{3,11},{4,12},{5,13},{6,14},{7,15},{8,0},{9,1},... | collective-permute-start | bytes 393224 | tf_op jit(solution)/shard_map/ppermute | solution.py:90
  28.7 1.3 %collective-permute-start.10 = (bf16[4,128,128]{2,1,0:T(8,128)(2,1)S(1)}, bf16[4,128,128]{2,1,0:T(8,128)(2,1)S(1)}, u32[]{:S(2)}, u32[]{:S(2)}) collective-permute-start(bf16[4,128,128]{2,1,0:T(8,128)(2,1)S(1)} %get-tuple-element.27.refs_0_.refs_1_), channel_id=1, source_target_pairs={{0,2},{1,3},{2,0},{3,1},{4,6},{5,7},{6,4},{7,5},{8,10},{9,11},{10,... | collective-permute-start | bytes 393224 | tf_op jit(solution)/shard_map/ppermute | solution.py:90
  30.0 2.3 %collective-permute-start.11 = (bf16[4,128,128]{2,1,0:T(8,128)(2,1)S(1)}, bf16[4,128,128]{2,1,0:T(8,128)(2,1)S(1)}, u32[]{:S(2)}, u32[]{:S(2)}) collective-permute-start(bf16[4,128,128]{2,1,0:T(8,128)(2,1)S(1)} %get-tuple-element.27.refs_0_.refs_1_), channel_id=1, source_target_pairs={{0,4},{1,5},{2,6},{3,7},{4,0},{5,1},{6,2},{7,3},{8,12},{9,13},{10,... | collective-permute-start | bytes 393224 | tf_op jit(solution)/shard_map/ppermute | solution.py:90
  32.3 0.0 collective-permute-start.14
  32.3 0.7 %unstage.1 = bf16[512,256]{1,0:T(8,128)(2,1)} custom-call(bf16[512,256]{1,0:T(8,128)(2,1)S(1)} %get-tuple-element.26.x), custom_call_target="tpu_custom_call" | custom-call | tf_op jit(solution)/shard_map/unstage/pallas_call | solution.py:78
  33.0 0.5 %collective-permute-done.14 = f32[64,256]{1,0:T(8,128)S(1)} collective-permute-done((f32[64,256]{1,0:T(8,128)S(1)}, f32[64,256]{1,0:T(8,128)S(1)}, u32[]{:S(2)}, u32[]{:S(2)}) %collective-permute-start.14) | collective-permute-done | bytes 65568 | tf_op jit(solution)/shard_map/ppermute | solution.py:90
  33.6 0.7 %collective-permute-start.15 = (f32[64,256]{1,0:T(8,128)S(1)}, f32[64,256]{1,0:T(8,128)S(1)}, u32[]{:S(2)}, u32[]{:S(2)}) collective-permute-start(f32[64,256]{1,0:T(8,128)S(1)} %add.12), channel_id=1, source_target_pairs={{0,2},{1,3},{2,0},{3,1},{4,6},{5,7},{6,4},{7,5},{8,10},{9,11},{10,... | collective-permute-start | bytes 196616 | tf_op jit(solution)/shard_map/ppermute | solution.py:90
  34.3 1.2 %collective-permute-done.13.refs_3_.refs_5_ = bf16[4,128,128]{2,1,0:T(8,128)(2,1)S(1)} collective-permute-done((bf16[4,128,128]{2,1,0:T(8,128)(2,1)S(1)}, bf16[4,128,128]{2,1,0:T(8,128)(2,1)S(1)}, u32[]{:S(2)}, u32[]{:S(2)}) %collective-permute-start.13) | collective-permute-done | bytes 131104 | tf_op jit(solution)/shard_map/ppermute | solution.py:90
  35.5 0.7 %collective-permute-start.17 = (bf16[4,128,128]{2,1,0:T(8,128)(2,1)S(1)}, bf16[4,128,128]{2,1,0:T(8,128)(2,1)S(1)}, u32[]{:S(2)}, u32[]{:S(2)}) collective-permute-start(bf16[4,128,128]{2,1,0:T(8,128)(2,1)S(1)} %collective-permute-done.13.refs_3_.refs_5_), channel_id=1, source_target_pairs={{0,4},{1,5},{2,6},{3,7},{4,0},{5,1},{6,2},{7,3},{8,12},{9,13},{10,... | collective-permute-start | bytes 393224 | tf_op jit(solution)/shard_map/ppermute | solution.py:90
  36.1 0.0 collective-permute-done.10.refs_1_.refs_2_
  36.1 0.5 %collective-permute-done.11.refs_2_.refs_3_ = bf16[4,128,128]{2,1,0:T(8,128)(2,1)S(1)} collective-permute-done((bf16[4,128,128]{2,1,0:T(8,128)(2,1)S(1)}, bf16[4,128,128]{2,1,0:T(8,128)(2,1)S(1)}, u32[]{:S(2)}, u32[]{:S(2)}) %collective-permute-start.11) | collective-permute-done | bytes 131104 | tf_op jit(solution)/shard_map/ppermute | solution.py:90
  36.7 0.1 collective-permute-start.20
  36.8 1.2 %collective-permute-done.15 = f32[64,256]{1,0:T(8,128)S(1)} collective-permute-done((f32[64,256]{1,0:T(8,128)S(1)}, f32[64,256]{1,0:T(8,128)S(1)}, u32[]{:S(2)}, u32[]{:S(2)}) %collective-permute-start.15) | collective-permute-done | bytes 65568 | tf_op jit(solution)/shard_map/ppermute | solution.py:90
  37.9 1.8 %collective-permute-start.18 = (f32[64,256]{1,0:T(8,128)S(1)}, f32[64,256]{1,0:T(8,128)S(1)}, u32[]{:S(2)}, u32[]{:S(2)}) collective-permute-start(f32[64,256]{1,0:T(8,128)S(1)} %add.13), channel_id=1, source_target_pairs={{0,8},{1,9},{2,10},{3,11},{4,12},{5,13},{6,14},{7,15},{8,0},{9,1},... | collective-permute-start | bytes 196616 | tf_op jit(solution)/shard_map/ppermute | solution.py:90
  39.8 0.9 %collective-permute-start.12 = (bf16[4,128,128]{2,1,0:T(8,128)(2,1)S(1)}, bf16[4,128,128]{2,1,0:T(8,128)(2,1)S(1)}, u32[]{:S(2)}, u32[]{:S(2)}) collective-permute-start(bf16[4,128,128]{2,1,0:T(8,128)(2,1)S(1)} %collective-permute-done.10.refs_1_.refs_2_), channel_id=1, source_target_pairs={{0,4},{1,5},{2,6},{3,7},{4,0},{5,1},{6,2},{7,3},{8,12},{9,13},{10,... | collective-permute-start | bytes 393224 | tf_op jit(solution)/shard_map/ppermute | solution.py:90
  40.7 0.7 %collective-permute-start.16 = (bf16[4,128,128]{2,1,0:T(8,128)(2,1)S(1)}, bf16[4,128,128]{2,1,0:T(8,128)(2,1)S(1)}, u32[]{:S(2)}, u32[]{:S(2)}) collective-permute-start(bf16[4,128,128]{2,1,0:T(8,128)(2,1)S(1)} %collective-permute-done.13.refs_3_.refs_5_), channel_id=1, source_target_pairs={{0,2},{1,3},{2,0},{3,1},{4,6},{5,7},{6,4},{7,5},{8,10},{9,11},{10,... | collective-permute-start | bytes 393224 | tf_op jit(solution)/shard_map/ppermute | solution.py:90
  41.3 2.6 %collective-permute-done.18 = f32[64,256]{1,0:T(8,128)S(1)} collective-permute-done((f32[64,256]{1,0:T(8,128)S(1)}, f32[64,256]{1,0:T(8,128)S(1)}, u32[]{:S(2)}, u32[]{:S(2)}) %collective-permute-start.18) | collective-permute-done | bytes 65568 | tf_op jit(solution)/shard_map/ppermute | solution.py:90
  43.9 0.0 collective-permute-done.17.refs_0_.refs_7_
  44.0 0.5 collective-permute-start.19
  44.4 2.2 %collective-permute-start.22 = (f32[64,256]{1,0:T(8,128)S(1)}, f32[64,256]{1,0:T(8,128)S(1)}, u32[]{:S(2)}, u32[]{:S(2)}) collective-permute-start(f32[64,256]{1,0:T(8,128)S(1)} %add.14), channel_id=1, source_target_pairs={{0,4},{1,5},{2,6},{3,7},{4,0},{5,1},{6,2},{7,3},{8,12},{9,13},{10,... | collective-permute-start | bytes 196616 | tf_op jit(solution)/shard_map/ppermute | solution.py:90
  46.6 0.0 collective-permute-done.12.refs_0_.refs_4_
  46.6 0.4 collective-permute-done.16.refs_1_.refs_6_
  47.1 0.1 collective-permute-start.21
  47.1 1.7 %collective-permute-done.22 = f32[64,256]{1,0:T(8,128)S(1)} collective-permute-done((f32[64,256]{1,0:T(8,128)S(1)}, f32[64,256]{1,0:T(8,128)S(1)}, u32[]{:S(2)}, u32[]{:S(2)}) %collective-permute-start.22) | collective-permute-done | bytes 65568 | tf_op jit(solution)/shard_map/ppermute | solution.py:90
  48.9 0.1 collective-permute-done.19.refs_1_.refs_8_
  49.0 0.1 collective-permute-start.23
  49.1 0.5 collective-permute-start.24
  49.6 1.1 %collective-permute-done.24.refs_14_ = f32[64,256]{1,0:T(8,128)S(1)} collective-permute-done((f32[64,256]{1,0:T(8,128)S(1)}, f32[64,256]{1,0:T(8,128)S(1)}, u32[]{:S(2)}, u32[]{:S(2)}) %collective-permute-start.24) | collective-permute-done | bytes 65568 | tf_op jit(solution)/shard_map/ppermute | solution.py:90
  50.7 0.0 collective-permute-done.21.refs_10_
  50.7 0.0 collective-permute-done.20.refs_9_
  50.7 0.0 collective-permute-done.23.refs_11_
  50.7 1.5 %backward.1 = (bf16[512,128]{1,0:T(8,128)(2,1)}, f32[128,256]{1,0:T(8,128)}) custom-call(s32[4,16]{1,0:T(4,128)S(4)} %get-tuple-element.20.refs_0_, bf16[4,128,128]{2,1,0:T(8,128)(2,1)S(1)} %get-tuple-element.27.refs_0_.refs_1_, bf16[4,128,128]{2,1,0:T(8,128)(2,1)S(1)} %collective-permute-done.10.refs_1_.refs_2_, ...), custom_call_target="tpu_custom_call" | custom-call | tf_op jit(solution)/shard_map/backward/pallas_call | solution.py:304
  (10 shorter events, 0.2 us)
Async XLA Ops:
  0.6 10.7 %collective-permute-start.3 = (bf16[4,128,128]{2,1,0:T(8,128)(2,1)}, bf16[4,128,128]{2,1,0:T(8,128)(2,1)S(1)}, u32[]{:S(2)}, u32[]{:S(2)}) collective-permute-start(bf16[4,128,128]{2,1,0:T(8,128)(2,1)} %bitcast.1), channel_id=1, source_target_pairs={{0,8},{1,9},{2,10},{3,11},{4,12},{5,13},{6,14},{7,15},{8,0},{9,1},... | collective-permute-start | bytes 393224 | tf_op jit(solution)/shard_map/ppermute | solution.py:90
  4.7 7.4 %collective-permute-start = (bf16[4,128,128]{2,1,0:T(8,128)(2,1)}, bf16[4,128,128]{2,1,0:T(8,128)(2,1)S(1)}, u32[]{:S(2)}, u32[]{:S(2)}) collective-permute-start(bf16[4,128,128]{2,1,0:T(8,128)(2,1)} %bitcast.2), channel_id=1, source_target_pairs={{0,2},{1,3},{2,0},{3,1},{4,6},{5,7},{6,4},{7,5},{8,10},{9,11},{10,... | collective-permute-start | bytes 393224 | tf_op jit(solution)/shard_map/ppermute | solution.py:90
  6.3 6.5 %collective-permute-start.1 = (bf16[4,128,128]{2,1,0:T(8,128)(2,1)}, bf16[4,128,128]{2,1,0:T(8,128)(2,1)S(1)}, u32[]{:S(2)}, u32[]{:S(2)}) collective-permute-start(bf16[4,128,128]{2,1,0:T(8,128)(2,1)} %bitcast.3), channel_id=1, source_target_pairs={{0,4},{1,5},{2,6},{3,7},{4,0},{5,1},{6,2},{7,3},{8,12},{9,13},{10,... | collective-permute-start | bytes 393224 | tf_op jit(solution)/shard_map/ppermute | solution.py:90
  11.4 5.3 %collective-permute-start.5 = (bf16[4,128,128]{2,1,0:T(8,128)(2,1)S(1)}, bf16[4,128,128]{2,1,0:T(8,128)(2,1)S(1)}, u32[]{:S(2)}, u32[]{:S(2)}) collective-permute-start(bf16[4,128,128]{2,1,0:T(8,128)(2,1)S(1)} %collective-permute-done.3.refs_3_.refs_5_), channel_id=1, source_target_pairs={{0,4},{1,5},{2,6},{3,7},{4,0},{5,1},{6,2},{7,3},{8,12},{9,13},{10,... | collective-permute-start | bytes 393224 | tf_op jit(solution)/shard_map/ppermute | solution.py:90
  12.8 9.2 %collective-permute-start.7 = (bf16[16,128,128]{2,1,0:T(8,128)(2,1)S(1)}, bf16[16,128,128]{2,1,0:T(8,128)(2,1)S(1)}, u32[]{:S(2)}, u32[]{:S(2)}) collective-permute-start(bf16[16,128,128]{2,1,0:T(8,128)(2,1)S(1)} %pack.6), channel_id=1, source_target_pairs={{0,1},{1,0},{2,3},{3,2},{4,5},{5,4},{6,7},{7,6},{8,9},{9,8},{10,11... | collective-permute-start | bytes 1572872 | tf_op jit(solution)/shard_map/ppermute | solution.py:90
  12.9 6.2 %collective-permute-start.2 = (bf16[4,128,128]{2,1,0:T(8,128)(2,1)S(1)}, bf16[4,128,128]{2,1,0:T(8,128)(2,1)S(1)}, u32[]{:S(2)}, u32[]{:S(2)}) collective-permute-start(bf16[4,128,128]{2,1,0:T(8,128)(2,1)S(1)} %collective-permute-done.refs_1_.refs_2_), channel_id=1, source_target_pairs={{0,4},{1,5},{2,6},{3,7},{4,0},{5,1},{6,2},{7,3},{8,12},{9,13},{10,... | collective-permute-start | bytes 393224 | tf_op jit(solution)/shard_map/ppermute | solution.py:90
  13.6 6.3 %collective-permute-start.4 = (bf16[4,128,128]{2,1,0:T(8,128)(2,1)S(1)}, bf16[4,128,128]{2,1,0:T(8,128)(2,1)S(1)}, u32[]{:S(2)}, u32[]{:S(2)}) collective-permute-start(bf16[4,128,128]{2,1,0:T(8,128)(2,1)S(1)} %collective-permute-done.3.refs_3_.refs_5_), channel_id=1, source_target_pairs={{0,2},{1,3},{2,0},{3,1},{4,6},{5,7},{6,4},{7,5},{8,10},{9,11},{10,... | collective-permute-start | bytes 393224 | tf_op jit(solution)/shard_map/ppermute | solution.py:90
  16.6 5.3 %collective-permute-start.6 = (bf16[4,128,128]{2,1,0:T(8,128)(2,1)S(1)}, bf16[4,128,128]{2,1,0:T(8,128)(2,1)S(1)}, u32[]{:S(2)}, u32[]{:S(2)}) collective-permute-start(bf16[4,128,128]{2,1,0:T(8,128)(2,1)S(1)} %collective-permute-done.5.refs_0_.refs_7_), channel_id=1, source_target_pairs={{0,2},{1,3},{2,0},{3,1},{4,6},{5,7},{6,4},{7,5},{8,10},{9,11},{10,... | collective-permute-start | bytes 393224 | tf_op jit(solution)/shard_map/ppermute | solution.py:90
  19.9 2.1 %collective-permute-start.8 = (bf16[8,128,128]{2,1,0:T(8,128)(2,1)S(1)}, bf16[8,128,128]{2,1,0:T(8,128)(2,1)S(1)}, u32[]{:S(2)}, u32[]{:S(2)}) collective-permute-start(bf16[8,128,128]{2,1,0:T(8,128)(2,1)S(1)} %pack.7), channel_id=1, source_target_pairs={{0,1},{1,0},{2,3},{3,2},{4,5},{5,4},{6,7},{7,6},{8,9},{9,8},{10,11... | collective-permute-start | bytes 786440 | tf_op jit(solution)/shard_map/ppermute | solution.py:90
  22.0 1.6 %collective-permute-start.9 = (bf16[8,128,128]{2,1,0:T(8,128)(2,1)S(1)}, bf16[8,128,128]{2,1,0:T(8,128)(2,1)S(1)}, u32[]{:S(2)}, u32[]{:S(2)}) collective-permute-start(bf16[8,128,128]{2,1,0:T(8,128)(2,1)S(1)} %pack.8), channel_id=1, source_target_pairs={{0,1},{1,0},{2,3},{3,2},{4,5},{5,4},{6,7},{7,6},{8,9},{9,8},{10,11... | collective-permute-start | bytes 786440 | tf_op jit(solution)/shard_map/ppermute | solution.py:90
  26.0 9.4 %collective-permute-start.13 = (bf16[4,128,128]{2,1,0:T(8,128)(2,1)S(1)}, bf16[4,128,128]{2,1,0:T(8,128)(2,1)S(1)}, u32[]{:S(2)}, u32[]{:S(2)}) collective-permute-start(bf16[4,128,128]{2,1,0:T(8,128)(2,1)S(1)} %get-tuple-element.27.refs_0_.refs_1_), channel_id=1, source_target_pairs={{0,8},{1,9},{2,10},{3,11},{4,12},{5,13},{6,14},{7,15},{8,0},{9,1},... | collective-permute-start | bytes 393224 | tf_op jit(solution)/shard_map/ppermute | solution.py:90
  28.7 7.4 %collective-permute-start.10 = (bf16[4,128,128]{2,1,0:T(8,128)(2,1)S(1)}, bf16[4,128,128]{2,1,0:T(8,128)(2,1)S(1)}, u32[]{:S(2)}, u32[]{:S(2)}) collective-permute-start(bf16[4,128,128]{2,1,0:T(8,128)(2,1)S(1)} %get-tuple-element.27.refs_0_.refs_1_), channel_id=1, source_target_pairs={{0,2},{1,3},{2,0},{3,1},{4,6},{5,7},{6,4},{7,5},{8,10},{9,11},{10,... | collective-permute-start | bytes 393224 | tf_op jit(solution)/shard_map/ppermute | solution.py:90
  30.0 6.6 %collective-permute-start.11 = (bf16[4,128,128]{2,1,0:T(8,128)(2,1)S(1)}, bf16[4,128,128]{2,1,0:T(8,128)(2,1)S(1)}, u32[]{:S(2)}, u32[]{:S(2)}) collective-permute-start(bf16[4,128,128]{2,1,0:T(8,128)(2,1)S(1)} %get-tuple-element.27.refs_0_.refs_1_), channel_id=1, source_target_pairs={{0,4},{1,5},{2,6},{3,7},{4,0},{5,1},{6,2},{7,3},{8,12},{9,13},{10,... | collective-permute-start | bytes 393224 | tf_op jit(solution)/shard_map/ppermute | solution.py:90
  32.3 1.3 %collective-permute-start.14 = (f32[64,256]{1,0:T(8,128)S(1)}, f32[64,256]{1,0:T(8,128)S(1)}, u32[]{:S(2)}, u32[]{:S(2)}) collective-permute-start(f32[64,256]{1,0:T(8,128)S(1)} %get-tuple-element.29), channel_id=1, source_target_pairs={{0,1},{1,0},{2,3},{3,2},{4,5},{5,4},{6,7},{7,6},{8,9},{9,8},{10,11... | collective-permute-start | bytes 196616 | tf_op jit(solution)/shard_map/ppermute | solution.py:90
  33.6 4.3 %collective-permute-start.15 = (f32[64,256]{1,0:T(8,128)S(1)}, f32[64,256]{1,0:T(8,128)S(1)}, u32[]{:S(2)}, u32[]{:S(2)}) collective-permute-start(f32[64,256]{1,0:T(8,128)S(1)} %add.12), channel_id=1, source_target_pairs={{0,2},{1,3},{2,0},{3,1},{4,6},{5,7},{6,4},{7,5},{8,10},{9,11},{10,... | collective-permute-start | bytes 196616 | tf_op jit(solution)/shard_map/ppermute | solution.py:90
  35.5 8.5 %collective-permute-start.17 = (bf16[4,128,128]{2,1,0:T(8,128)(2,1)S(1)}, bf16[4,128,128]{2,1,0:T(8,128)(2,1)S(1)}, u32[]{:S(2)}, u32[]{:S(2)}) collective-permute-start(bf16[4,128,128]{2,1,0:T(8,128)(2,1)S(1)} %collective-permute-done.13.refs_3_.refs_5_), channel_id=1, source_target_pairs={{0,4},{1,5},{2,6},{3,7},{4,0},{5,1},{6,2},{7,3},{8,12},{9,13},{10,... | collective-permute-start | bytes 393224 | tf_op jit(solution)/shard_map/ppermute | solution.py:90
  36.7 14.0 %collective-permute-start.20 = (bf16[16,128,128]{2,1,0:T(8,128)(2,1)S(1)}, bf16[16,128,128]{2,1,0:T(8,128)(2,1)S(1)}, u32[]{:S(2)}, u32[]{:S(2)}) collective-permute-start(bf16[16,128,128]{2,1,0:T(8,128)(2,1)S(1)} %pack.9), channel_id=1, source_target_pairs={{0,1},{1,0},{2,3},{3,2},{4,5},{5,4},{6,7},{7,6},{8,9},{9,8},{10,11... | collective-permute-start | bytes 1572872 | tf_op jit(solution)/shard_map/ppermute | solution.py:90
  37.9 6.0 %collective-permute-start.18 = (f32[64,256]{1,0:T(8,128)S(1)}, f32[64,256]{1,0:T(8,128)S(1)}, u32[]{:S(2)}, u32[]{:S(2)}) collective-permute-start(f32[64,256]{1,0:T(8,128)S(1)} %add.13), channel_id=1, source_target_pairs={{0,8},{1,9},{2,10},{3,11},{4,12},{5,13},{6,14},{7,15},{8,0},{9,1},... | collective-permute-start | bytes 196616 | tf_op jit(solution)/shard_map/ppermute | solution.py:90
  39.8 6.9 %collective-permute-start.12 = (bf16[4,128,128]{2,1,0:T(8,128)(2,1)S(1)}, bf16[4,128,128]{2,1,0:T(8,128)(2,1)S(1)}, u32[]{:S(2)}, u32[]{:S(2)}) collective-permute-start(bf16[4,128,128]{2,1,0:T(8,128)(2,1)S(1)} %collective-permute-done.10.refs_1_.refs_2_), channel_id=1, source_target_pairs={{0,4},{1,5},{2,6},{3,7},{4,0},{5,1},{6,2},{7,3},{8,12},{9,13},{10,... | collective-permute-start | bytes 393224 | tf_op jit(solution)/shard_map/ppermute | solution.py:90
  40.7 6.4 %collective-permute-start.16 = (bf16[4,128,128]{2,1,0:T(8,128)(2,1)S(1)}, bf16[4,128,128]{2,1,0:T(8,128)(2,1)S(1)}, u32[]{:S(2)}, u32[]{:S(2)}) collective-permute-start(bf16[4,128,128]{2,1,0:T(8,128)(2,1)S(1)} %collective-permute-done.13.refs_3_.refs_5_), channel_id=1, source_target_pairs={{0,2},{1,3},{2,0},{3,1},{4,6},{5,7},{6,4},{7,5},{8,10},{9,11},{10,... | collective-permute-start | bytes 393224 | tf_op jit(solution)/shard_map/ppermute | solution.py:90
  44.0 5.0 %collective-permute-start.19 = (bf16[4,128,128]{2,1,0:T(8,128)(2,1)S(1)}, bf16[4,128,128]{2,1,0:T(8,128)(2,1)S(1)}, u32[]{:S(2)}, u32[]{:S(2)}) collective-permute-start(bf16[4,128,128]{2,1,0:T(8,128)(2,1)S(1)} %collective-permute-done.17.refs_0_.refs_7_), channel_id=1, source_target_pairs={{0,2},{1,3},{2,0},{3,1},{4,6},{5,7},{6,4},{7,5},{8,10},{9,11},{10,... | collective-permute-start | bytes 393224 | tf_op jit(solution)/shard_map/ppermute | solution.py:90
  44.4 4.4 %collective-permute-start.22 = (f32[64,256]{1,0:T(8,128)S(1)}, f32[64,256]{1,0:T(8,128)S(1)}, u32[]{:S(2)}, u32[]{:S(2)}) collective-permute-start(f32[64,256]{1,0:T(8,128)S(1)} %add.14), channel_id=1, source_target_pairs={{0,4},{1,5},{2,6},{3,7},{4,0},{5,1},{6,2},{7,3},{8,12},{9,13},{10,... | collective-permute-start | bytes 196616 | tf_op jit(solution)/shard_map/ppermute | solution.py:90
  47.1 3.7 %collective-permute-start.21 = (bf16[8,128,128]{2,1,0:T(8,128)(2,1)S(1)}, bf16[8,128,128]{2,1,0:T(8,128)(2,1)S(1)}, u32[]{:S(2)}, u32[]{:S(2)}) collective-permute-start(bf16[8,128,128]{2,1,0:T(8,128)(2,1)S(1)} %pack.10), channel_id=1, source_target_pairs={{0,1},{1,0},{2,3},{3,2},{4,5},{5,4},{6,7},{7,6},{8,9},{9,8},{10,11... | collective-permute-start | bytes 786440 | tf_op jit(solution)/shard_map/ppermute | solution.py:90
  49.0 1.7 %collective-permute-start.23 = (bf16[8,128,128]{2,1,0:T(8,128)(2,1)S(1)}, bf16[8,128,128]{2,1,0:T(8,128)(2,1)S(1)}, u32[]{:S(2)}, u32[]{:S(2)}) collective-permute-start(bf16[8,128,128]{2,1,0:T(8,128)(2,1)S(1)} %pack.11), channel_id=1, source_target_pairs={{0,1},{1,0},{2,3},{3,2},{4,5},{5,4},{6,7},{7,6},{8,9},{9,8},{10,11... | collective-permute-start | bytes 786440 | tf_op jit(solution)/shard_map/ppermute | solution.py:90
  49.1 1.6 %collective-permute-start.24 = (f32[64,256]{1,0:T(8,128)S(1)}, f32[64,256]{1,0:T(8,128)S(1)}, u32[]{:S(2)}, u32[]{:S(2)}) collective-permute-start(f32[64,256]{1,0:T(8,128)S(1)} %add.15.refs_13_), channel_id=1, source_target_pairs={{0,1},{1,0},{2,3},{3,2},{4,5},{5,4},{6,7},{7,6},{8,9},{9,8},{10,11... | collective-permute-start | bytes 196616 | tf_op jit(solution)/shard_map/ppermute | solution.py:90

commit v6 on v5

--- a/solution.py
+++ b/solution.py
@@ -213,6 +213,7 @@
     half = keep.shape[0]
     w = weight[...]
     ww = jnp.concatenate([w, w], 0)
+    left, right = [], []
     for panel in range(panels):
         rows = pl.ds(panel * side, side)
         agg = panel_product(cols, vals, nodes, panel)
@@ -226,12 +227,9 @@
         dz = out_grad[rows, :].astype(jnp.float32) * slope
         dz_h, dz_l = split(dz)
         edge[panel] = (dot(dz_h, w, ((1,), (1,))) + dot(dz_l, w, ((1,), (1,)))).astype(jnp.bfloat16)
-        part = dot(
-            jnp.concatenate([agg_h, agg_l, agg_h], 0),
-            jnp.concatenate([dz_h, dz_h, dz_l], 0),
-            ((0,), (0,)),
-        )
-        wsum[...] = part if panel == 0 else wsum[...] + part
+        left += [agg_h, agg_l, agg_h]
+        right += [dz_h, dz_h, dz_l]
+    wsum[...] = dot(jnp.concatenate(left, 0), jnp.concatenate(right, 0), ((0,), (0,)))
     core = me % 2
     keep[...] = wsum[pl.ds(pl.multiple_of(core * half, half), half), :]
     send[...] = wsum[pl.ds(pl.multiple_of((1 - core) * half, half), half), :]

time: 52.4 us -> 52.2 us (level)
  no operation moved by 1% of the time
where the time goes in v6:
time: 52.2 us; the launch traced here: 52 us
  starting transfers between devices  27.2 us (52%)
  waiting for transfers between devices  17.4 us (33%)
  Pallas kernels  6.58 us (13%)
  between operations  0.78 us (1%)
    ppermute x25, starting transfers between devices, exchange(): return lax.ppermute(x, 'row', [(i, i ^ bit) for i in range(size)])  27.2 us
    ppermute x25, waiting for transfers between devices, exchange(): return lax.ppermute(x, 'row', [(i, i ^ bit) for i in range(size)])  17.4 us
    pallas_call x1, Pallas kernels, body(): pl.pallas_call(lambda *refs: forward_kernel(masks, *refs), name='forward'...  2.23 us
    pallas_call x1, Pallas kernels, stage(): pl.pallas_call(stage_kernel, name='stage', compiler_params=PARAMS, out_sh...  1.99 us
    pallas_call x1, Pallas kernels, body(): pl.pallas_call(lambda *refs: backward_kernel(masks, *refs), name='backwar...  1.52 us
  transfers between devices with their start and end apart: 25, of which 16 were waited for; matrix products, arithmetic and copies ran while one was open for 0% of the time, Pallas kernels for 5%

profile of v6, /device:TPU:0, one launch (start us, length us, event | category | flops | bytes accessed | tf_op | source)
XLA Modules:
  0.0 52.0 jit_solution(5603582469691752262)
XLA Ops:
  0.6 4.1 %collective-permute-start.3 = (bf16[4,128,128]{2,1,0:T(8,128)(2,1)}, bf16[4,128,128]{2,1,0:T(8,128)(2,1)S(1)}, u32[]{:S(2)}, u32[]{:S(2)}) collective-permute-start(bf16[4,128,128]{2,1,0:T(8,128)(2,1)} %bitcast.1), channel_id=1, source_target_pairs={{0,8},{1,9},{2,10},{3,11},{4,12},{5,13},{6,14},{7,15},{8,0},{9,1},... | collective-permute-start | bytes 393224 | tf_op jit(solution)/shard_map/ppermute | solution.py:90
  4.7 1.5 %collective-permute-start = (bf16[4,128,128]{2,1,0:T(8,128)(2,1)}, bf16[4,128,128]{2,1,0:T(8,128)(2,1)S(1)}, u32[]{:S(2)}, u32[]{:S(2)}) collective-permute-start(bf16[4,128,128]{2,1,0:T(8,128)(2,1)} %bitcast.2), channel_id=1, source_target_pairs={{0,2},{1,3},{2,0},{3,1},{4,6},{5,7},{6,4},{7,5},{8,10},{9,11},{10,... | collective-permute-start | bytes 393224 | tf_op jit(solution)/shard_map/ppermute | solution.py:90
  6.3 1.6 %collective-permute-start.1 = (bf16[4,128,128]{2,1,0:T(8,128)(2,1)}, bf16[4,128,128]{2,1,0:T(8,128)(2,1)S(1)}, u32[]{:S(2)}, u32[]{:S(2)}) collective-permute-start(bf16[4,128,128]{2,1,0:T(8,128)(2,1)} %bitcast.3), channel_id=1, source_target_pairs={{0,4},{1,5},{2,6},{3,7},{4,0},{5,1},{6,2},{7,3},{8,12},{9,13},{10,... | collective-permute-start | bytes 393224 | tf_op jit(solution)/shard_map/ppermute | solution.py:90
  7.8 2.0 %stage.1 = (s32[4,16]{1,0:T(4,128)S(4)}, bf16[4,16,128,128]{3,2,1,0:T(8,128)(2,1)S(1)}, bf16[512,256]{1,0:T(8,128)(2,1)S(1)}, bf16[128,256]{1,0:T(8,128)(2,1)S(1)}, bf16[4,128,128]{2,1,0:T(8,128)(2,1)S(1)}) custom-call(s32[4,16]{1,0:T(4,128)} %cols.1, s32[4]{0:T(128)} %counts.1, bf16[4,16,128,128]{3,2,1,0:T(8,128)(2,1)} %vals.1, bf16[512,256]{1,0:T(8,128)(2,1)} %refs_0_.1, ...), custom_call_target="tpu_custom_call" | custom-call | tf_op jit(solution)/shard_map/stage/pallas_call | solution.py:56
  9.8 1.5 %collective-permute-done.3.refs_3_.refs_5_ = bf16[4,128,128]{2,1,0:T(8,128)(2,1)S(1)} collective-permute-done((bf16[4,128,128]{2,1,0:T(8,128)(2,1)}, bf16[4,128,128]{2,1,0:T(8,128)(2,1)S(1)}, u32[]{:S(2)}, u32[]{:S(2)}) %collective-permute-start.3) | collective-permute-done | bytes 131104 | tf_op jit(solution)/shard_map/ppermute | solution.py:90
  11.4 0.8 %collective-permute-start.5 = (bf16[4,128,128]{2,1,0:T(8,128)(2,1)S(1)}, bf16[4,128,128]{2,1,0:T(8,128)(2,1)S(1)}, u32[]{:S(2)}, u32[]{:S(2)}) collective-permute-start(bf16[4,128,128]{2,1,0:T(8,128)(2,1)S(1)} %collective-permute-done.3.refs_3_.refs_5_), channel_id=1, source_target_pairs={{0,4},{1,5},{2,6},{3,7},{4,0},{5,1},{6,2},{7,3},{8,12},{9,13},{10,... | collective-permute-start | bytes 393224 | tf_op jit(solution)/shard_map/ppermute | solution.py:90
  12.1 0.0 collective-permute-done.refs_1_.refs_2_
  12.1 0.7 %collective-permute-done.1.refs_2_.refs_3_ = bf16[4,128,128]{2,1,0:T(8,128)(2,1)S(1)} collective-permute-done((bf16[4,128,128]{2,1,0:T(8,128)(2,1)}, bf16[4,128,128]{2,1,0:T(8,128)(2,1)S(1)}, u32[]{:S(2)}, u32[]{:S(2)}) %collective-permute-start.1) | collective-permute-done | bytes 131104 | tf_op jit(solution)/shard_map/ppermute | solution.py:90
  12.8 0.1 collective-permute-start.7
  12.9 0.7 %collective-permute-start.2 = (bf16[4,128,128]{2,1,0:T(8,128)(2,1)S(1)}, bf16[4,128,128]{2,1,0:T(8,128)(2,1)S(1)}, u32[]{:S(2)}, u32[]{:S(2)}) collective-permute-start(bf16[4,128,128]{2,1,0:T(8,128)(2,1)S(1)} %collective-permute-done.refs_1_.refs_2_), channel_id=1, source_target_pairs={{0,4},{1,5},{2,6},{3,7},{4,0},{5,1},{6,2},{7,3},{8,12},{9,13},{10,... | collective-permute-start | bytes 393224 | tf_op jit(solution)/shard_map/ppermute | solution.py:90
  13.6 1.6 %collective-permute-start.4 = (bf16[4,128,128]{2,1,0:T(8,128)(2,1)S(1)}, bf16[4,128,128]{2,1,0:T(8,128)(2,1)S(1)}, u32[]{:S(2)}, u32[]{:S(2)}) collective-permute-start(bf16[4,128,128]{2,1,0:T(8,128)(2,1)S(1)} %collective-permute-done.3.refs_3_.refs_5_), channel_id=1, source_target_pairs={{0,2},{1,3},{2,0},{3,1},{4,6},{5,7},{6,4},{7,5},{8,10},{9,11},{10,... | collective-permute-start | bytes 393224 | tf_op jit(solution)/shard_map/ppermute | solution.py:90
  15.1 1.5 %collective-permute-done.5.refs_0_.refs_7_ = bf16[4,128,128]{2,1,0:T(8,128)(2,1)S(1)} collective-permute-done((bf16[4,128,128]{2,1,0:T(8,128)(2,1)S(1)}, bf16[4,128,128]{2,1,0:T(8,128)(2,1)S(1)}, u32[]{:S(2)}, u32[]{:S(2)}) %collective-permute-start.5) | collective-permute-done | bytes 131104 | tf_op jit(solution)/shard_map/ppermute | solution.py:90
  16.6 2.3 %collective-permute-start.6 = (bf16[4,128,128]{2,1,0:T(8,128)(2,1)S(1)}, bf16[4,128,128]{2,1,0:T(8,128)(2,1)S(1)}, u32[]{:S(2)}, u32[]{:S(2)}) collective-permute-start(bf16[4,128,128]{2,1,0:T(8,128)(2,1)S(1)} %collective-permute-done.5.refs_0_.refs_7_), channel_id=1, source_target_pairs={{0,2},{1,3},{2,0},{3,1},{4,6},{5,7},{6,4},{7,5},{8,10},{9,11},{10,... | collective-permute-start | bytes 393224 | tf_op jit(solution)/shard_map/ppermute | solution.py:90
  19.0 0.2 collective-permute-done.2.refs_0_.refs_4_
  19.1 0.8 %collective-permute-done.4.refs_1_.refs_6_ = bf16[4,128,128]{2,1,0:T(8,128)(2,1)S(1)} collective-permute-done((bf16[4,128,128]{2,1,0:T(8,128)(2,1)S(1)}, bf16[4,128,128]{2,1,0:T(8,128)(2,1)S(1)}, u32[]{:S(2)}, u32[]{:S(2)}) %collective-permute-start.4) | collective-permute-done | bytes 131104 | tf_op jit(solution)/shard_map/ppermute | solution.py:90
  19.9 0.1 collective-permute-start.8
  20.0 1.9 %collective-permute-done.6.refs_1_.refs_8_ = bf16[4,128,128]{2,1,0:T(8,128)(2,1)S(1)} collective-permute-done((bf16[4,128,128]{2,1,0:T(8,128)(2,1)S(1)}, bf16[4,128,128]{2,1,0:T(8,128)(2,1)S(1)}, u32[]{:S(2)}, u32[]{:S(2)}) %collective-permute-start.6) | collective-permute-done | bytes 131104 | tf_op jit(solution)/shard_map/ppermute | solution.py:90
  22.0 0.1 collective-permute-start.9
  22.1 0.0 collective-permute-done.8.refs_10_
  22.1 0.0 collective-permute-done.7.refs_9_
  22.1 1.5 %collective-permute-done.9.refs_11_ = bf16[8,128,128]{2,1,0:T(8,128)(2,1)S(1)} collective-permute-done((bf16[8,128,128]{2,1,0:T(8,128)(2,1)S(1)}, bf16[8,128,128]{2,1,0:T(8,128)(2,1)S(1)}, u32[]{:S(2)}, u32[]{:S(2)}) %collective-permute-start.9) | collective-permute-done | bytes 262176 | tf_op jit(solution)/shard_map/ppermute | solution.py:90
  23.6 2.2 %forward.1 = (bf16[512,256]{1,0:T(8,128)(2,1)S(1)}, bf16[4,128,128]{2,1,0:T(8,128)(2,1)S(1)}, f32[64,256]{1,0:T(8,128)S(1)}, f32[64,256]{1,0:T(8,128)S(1)}) custom-call(s32[4,16]{1,0:T(4,128)S(4)} %get-tuple-element.20.refs_0_, bf16[4,128,128]{2,1,0:T(8,128)(2,1)S(1)} %get-tuple-element.21.refs_0_.refs_1_, ...), custom_call_target="tpu_custom_call" | custom-call | tf_op jit(solution)/shard_map/forward/pallas_call | solution.py:285
  25.8 2.7 %collective-permute-start.13 = (bf16[4,128,128]{2,1,0:T(8,128)(2,1)S(1)}, bf16[4,128,128]{2,1,0:T(8,128)(2,1)S(1)}, u32[]{:S(2)}, u32[]{:S(2)}) collective-permute-start(bf16[4,128,128]{2,1,0:T(8,128)(2,1)S(1)} %get-tuple-element.27.refs_0_.refs_1_), channel_id=1, source_target_pairs={{0,8},{1,9},{2,10},{3,11},{4,12},{5,13},{6,14},{7,15},{8,0},{9,1},... | collective-permute-start | bytes 393224 | tf_op jit(solution)/shard_map/ppermute | solution.py:90
  28.5 1.3 %collective-permute-start.10 = (bf16[4,128,128]{2,1,0:T(8,128)(2,1)S(1)}, bf16[4,128,128]{2,1,0:T(8,128)(2,1)S(1)}, u32[]{:S(2)}, u32[]{:S(2)}) collective-permute-start(bf16[4,128,128]{2,1,0:T(8,128)(2,1)S(1)} %get-tuple-element.27.refs_0_.refs_1_), channel_id=1, source_target_pairs={{0,2},{1,3},{2,0},{3,1},{4,6},{5,7},{6,4},{7,5},{8,10},{9,11},{10,... | collective-permute-start | bytes 393224 | tf_op jit(solution)/shard_map/ppermute | solution.py:90
  29.8 2.3 %collective-permute-start.11 = (bf16[4,128,128]{2,1,0:T(8,128)(2,1)S(1)}, bf16[4,128,128]{2,1,0:T(8,128)(2,1)S(1)}, u32[]{:S(2)}, u32[]{:S(2)}) collective-permute-start(bf16[4,128,128]{2,1,0:T(8,128)(2,1)S(1)} %get-tuple-element.27.refs_0_.refs_1_), channel_id=1, source_target_pairs={{0,4},{1,5},{2,6},{3,7},{4,0},{5,1},{6,2},{7,3},{8,12},{9,13},{10,... | collective-permute-start | bytes 393224 | tf_op jit(solution)/shard_map/ppermute | solution.py:90
  32.1 0.0 collective-permute-start.14
  32.1 0.7 %unstage.1 = bf16[512,256]{1,0:T(8,128)(2,1)} custom-call(bf16[512,256]{1,0:T(8,128)(2,1)S(1)} %get-tuple-element.26.x), custom_call_target="tpu_custom_call" | custom-call | tf_op jit(solution)/shard_map/unstage/pallas_call | solution.py:78
  32.8 0.5 %collective-permute-done.14 = f32[64,256]{1,0:T(8,128)S(1)} collective-permute-done((f32[64,256]{1,0:T(8,128)S(1)}, f32[64,256]{1,0:T(8,128)S(1)}, u32[]{:S(2)}, u32[]{:S(2)}) %collective-permute-start.14) | collective-permute-done | bytes 65568 | tf_op jit(solution)/shard_map/ppermute | solution.py:90
  33.4 0.7 %collective-permute-start.15 = (f32[64,256]{1,0:T(8,128)S(1)}, f32[64,256]{1,0:T(8,128)S(1)}, u32[]{:S(2)}, u32[]{:S(2)}) collective-permute-start(f32[64,256]{1,0:T(8,128)S(1)} %add.12), channel_id=1, source_target_pairs={{0,2},{1,3},{2,0},{3,1},{4,6},{5,7},{6,4},{7,5},{8,10},{9,11},{10,... | collective-permute-start | bytes 196616 | tf_op jit(solution)/shard_map/ppermute | solution.py:90
  34.1 1.2 %collective-permute-done.13.refs_3_.refs_5_ = bf16[4,128,128]{2,1,0:T(8,128)(2,1)S(1)} collective-permute-done((bf16[4,128,128]{2,1,0:T(8,128)(2,1)S(1)}, bf16[4,128,128]{2,1,0:T(8,128)(2,1)S(1)}, u32[]{:S(2)}, u32[]{:S(2)}) %collective-permute-start.13) | collective-permute-done | bytes 131104 | tf_op jit(solution)/shard_map/ppermute | solution.py:90
  35.3 0.7 %collective-permute-start.17 = (bf16[4,128,128]{2,1,0:T(8,128)(2,1)S(1)}, bf16[4,128,128]{2,1,0:T(8,128)(2,1)S(1)}, u32[]{:S(2)}, u32[]{:S(2)}) collective-permute-start(bf16[4,128,128]{2,1,0:T(8,128)(2,1)S(1)} %collective-permute-done.13.refs_3_.refs_5_), channel_id=1, source_target_pairs={{0,4},{1,5},{2,6},{3,7},{4,0},{5,1},{6,2},{7,3},{8,12},{9,13},{10,... | collective-permute-start | bytes 393224 | tf_op jit(solution)/shard_map/ppermute | solution.py:90
  35.9 0.0 collective-permute-done.10.refs_1_.refs_2_
  35.9 0.5 %collective-permute-done.11.refs_2_.refs_3_ = bf16[4,128,128]{2,1,0:T(8,128)(2,1)S(1)} collective-permute-done((bf16[4,128,128]{2,1,0:T(8,128)(2,1)S(1)}, bf16[4,128,128]{2,1,0:T(8,128)(2,1)S(1)}, u32[]{:S(2)}, u32[]{:S(2)}) %collective-permute-start.11) | collective-permute-done | bytes 131104 | tf_op jit(solution)/shard_map/ppermute | solution.py:90
  36.5 0.1 collective-permute-start.20
  36.6 1.2 %collective-permute-done.15 = f32[64,256]{1,0:T(8,128)S(1)} collective-permute-done((f32[64,256]{1,0:T(8,128)S(1)}, f32[64,256]{1,0:T(8,128)S(1)}, u32[]{:S(2)}, u32[]{:S(2)}) %collective-permute-start.15) | collective-permute-done | bytes 65568 | tf_op jit(solution)/shard_map/ppermute | solution.py:90
  37.7 1.8 %collective-permute-start.18 = (f32[64,256]{1,0:T(8,128)S(1)}, f32[64,256]{1,0:T(8,128)S(1)}, u32[]{:S(2)}, u32[]{:S(2)}) collective-permute-start(f32[64,256]{1,0:T(8,128)S(1)} %add.13), channel_id=1, source_target_pairs={{0,8},{1,9},{2,10},{3,11},{4,12},{5,13},{6,14},{7,15},{8,0},{9,1},... | collective-permute-start | bytes 196616 | tf_op jit(solution)/shard_map/ppermute | solution.py:90
  39.6 0.9 %collective-permute-start.12 = (bf16[4,128,128]{2,1,0:T(8,128)(2,1)S(1)}, bf16[4,128,128]{2,1,0:T(8,128)(2,1)S(1)}, u32[]{:S(2)}, u32[]{:S(2)}) collective-permute-start(bf16[4,128,128]{2,1,0:T(8,128)(2,1)S(1)} %collective-permute-done.10.refs_1_.refs_2_), channel_id=1, source_target_pairs={{0,4},{1,5},{2,6},{3,7},{4,0},{5,1},{6,2},{7,3},{8,12},{9,13},{10,... | collective-permute-start | bytes 393224 | tf_op jit(solution)/shard_map/ppermute | solution.py:90
  40.5 0.7 %collective-permute-start.16 = (bf16[4,128,128]{2,1,0:T(8,128)(2,1)S(1)}, bf16[4,128,128]{2,1,0:T(8,128)(2,1)S(1)}, u32[]{:S(2)}, u32[]{:S(2)}) collective-permute-start(bf16[4,128,128]{2,1,0:T(8,128)(2,1)S(1)} %collective-permute-done.13.refs_3_.refs_5_), channel_id=1, source_target_pairs={{0,2},{1,3},{2,0},{3,1},{4,6},{5,7},{6,4},{7,5},{8,10},{9,11},{10,... | collective-permute-start | bytes 393224 | tf_op jit(solution)/shard_map/ppermute | solution.py:90
  41.1 2.6 %collective-permute-done.18 = f32[64,256]{1,0:T(8,128)S(1)} collective-permute-done((f32[64,256]{1,0:T(8,128)S(1)}, f32[64,256]{1,0:T(8,128)S(1)}, u32[]{:S(2)}, u32[]{:S(2)}) %collective-permute-start.18) | collective-permute-done | bytes 65568 | tf_op jit(solution)/shard_map/ppermute | solution.py:90
  43.7 0.0 collective-permute-done.17.refs_0_.refs_7_
  43.7 0.5 collective-permute-start.19
  44.2 2.2 %collective-permute-start.22 = (f32[64,256]{1,0:T(8,128)S(1)}, f32[64,256]{1,0:T(8,128)S(1)}, u32[]{:S(2)}, u32[]{:S(2)}) collective-permute-start(f32[64,256]{1,0:T(8,128)S(1)} %add.14), channel_id=1, source_target_pairs={{0,4},{1,5},{2,6},{3,7},{4,0},{5,1},{6,2},{7,3},{8,12},{9,13},{10,... | collective-permute-start | bytes 196616 | tf_op jit(solution)/shard_map/ppermute | solution.py:90
  46.4 0.0 collective-permute-done.12.refs_0_.refs_4_
  46.4 0.4 collective-permute-done.16.refs_1_.refs_6_
  46.8 0.1 collective-permute-start.21
  46.9 1.7 %collective-permute-done.22 = f32[64,256]{1,0:T(8,128)S(1)} collective-permute-done((f32[64,256]{1,0:T(8,128)S(1)}, f32[64,256]{1,0:T(8,128)S(1)}, u32[]{:S(2)}, u32[]{:S(2)}) %collective-permute-start.22) | collective-permute-done | bytes 65568 | tf_op jit(solution)/shard_map/ppermute | solution.py:90
  48.7 0.1 collective-permute-done.19.refs_1_.refs_8_
  48.8 0.1 collective-permute-start.23
  48.9 0.5 collective-permute-start.24
  49.4 1.1 %collective-permute-done.24.refs_14_ = f32[64,256]{1,0:T(8,128)S(1)} collective-permute-done((f32[64,256]{1,0:T(8,128)S(1)}, f32[64,256]{1,0:T(8,128)S(1)}, u32[]{:S(2)}, u32[]{:S(2)}) %collective-permute-start.24) | collective-permute-done | bytes 65568 | tf_op jit(solution)/shard_map/ppermute | solution.py:90
  50.5 0.0 collective-permute-done.21.refs_10_
  50.5 0.0 collective-permute-done.20.refs_9_
  50.5 0.0 collective-permute-done.23.refs_11_
  50.5 1.5 %backward.1 = (bf16[512,128]{1,0:T(8,128)(2,1)}, f32[128,256]{1,0:T(8,128)}) custom-call(s32[4,16]{1,0:T(4,128)S(4)} %get-tuple-element.20.refs_0_, bf16[4,128,128]{2,1,0:T(8,128)(2,1)S(1)} %get-tuple-element.27.refs_0_.refs_1_, bf16[4,128,128]{2,1,0:T(8,128)(2,1)S(1)} %collective-permute-done.10.refs_1_.refs_2_, ...), custom_call_target="tpu_custom_call" | custom-call | tf_op jit(solution)/shard_map/backward/pallas_call | solution.py:302
  (10 shorter events, 0.2 us)
Async XLA Ops:
  0.6 10.7 %collective-permute-start.3 = (bf16[4,128,128]{2,1,0:T(8,128)(2,1)}, bf16[4,128,128]{2,1,0:T(8,128)(2,1)S(1)}, u32[]{:S(2)}, u32[]{:S(2)}) collective-permute-start(bf16[4,128,128]{2,1,0:T(8,128)(2,1)} %bitcast.1), channel_id=1, source_target_pairs={{0,8},{1,9},{2,10},{3,11},{4,12},{5,13},{6,14},{7,15},{8,0},{9,1},... | collective-permute-start | bytes 393224 | tf_op jit(solution)/shard_map/ppermute | solution.py:90
  4.7 7.4 %collective-permute-start = (bf16[4,128,128]{2,1,0:T(8,128)(2,1)}, bf16[4,128,128]{2,1,0:T(8,128)(2,1)S(1)}, u32[]{:S(2)}, u32[]{:S(2)}) collective-permute-start(bf16[4,128,128]{2,1,0:T(8,128)(2,1)} %bitcast.2), channel_id=1, source_target_pairs={{0,2},{1,3},{2,0},{3,1},{4,6},{5,7},{6,4},{7,5},{8,10},{9,11},{10,... | collective-permute-start | bytes 393224 | tf_op jit(solution)/shard_map/ppermute | solution.py:90
  6.3 6.5 %collective-permute-start.1 = (bf16[4,128,128]{2,1,0:T(8,128)(2,1)}, bf16[4,128,128]{2,1,0:T(8,128)(2,1)S(1)}, u32[]{:S(2)}, u32[]{:S(2)}) collective-permute-start(bf16[4,128,128]{2,1,0:T(8,128)(2,1)} %bitcast.3), channel_id=1, source_target_pairs={{0,4},{1,5},{2,6},{3,7},{4,0},{5,1},{6,2},{7,3},{8,12},{9,13},{10,... | collective-permute-start | bytes 393224 | tf_op jit(solution)/shard_map/ppermute | solution.py:90
  11.4 5.3 %collective-permute-start.5 = (bf16[4,128,128]{2,1,0:T(8,128)(2,1)S(1)}, bf16[4,128,128]{2,1,0:T(8,128)(2,1)S(1)}, u32[]{:S(2)}, u32[]{:S(2)}) collective-permute-start(bf16[4,128,128]{2,1,0:T(8,128)(2,1)S(1)} %collective-permute-done.3.refs_3_.refs_5_), channel_id=1, source_target_pairs={{0,4},{1,5},{2,6},{3,7},{4,0},{5,1},{6,2},{7,3},{8,12},{9,13},{10,... | collective-permute-start | bytes 393224 | tf_op jit(solution)/shard_map/ppermute | solution.py:90
  12.8 9.2 %collective-permute-start.7 = (bf16[16,128,128]{2,1,0:T(8,128)(2,1)S(1)}, bf16[16,128,128]{2,1,0:T(8,128)(2,1)S(1)}, u32[]{:S(2)}, u32[]{:S(2)}) collective-permute-start(bf16[16,128,128]{2,1,0:T(8,128)(2,1)S(1)} %pack.6), channel_id=1, source_target_pairs={{0,1},{1,0},{2,3},{3,2},{4,5},{5,4},{6,7},{7,6},{8,9},{9,8},{10,11... | collective-permute-start | bytes 1572872 | tf_op jit(solution)/shard_map/ppermute | solution.py:90
  12.9 6.2 %collective-permute-start.2 = (bf16[4,128,128]{2,1,0:T(8,128)(2,1)S(1)}, bf16[4,128,128]{2,1,0:T(8,128)(2,1)S(1)}, u32[]{:S(2)}, u32[]{:S(2)}) collective-permute-start(bf16[4,128,128]{2,1,0:T(8,128)(2,1)S(1)} %collective-permute-done.refs_1_.refs_2_), channel_id=1, source_target_pairs={{0,4},{1,5},{2,6},{3,7},{4,0},{5,1},{6,2},{7,3},{8,12},{9,13},{10,... | collective-permute-start | bytes 393224 | tf_op jit(solution)/shard_map/ppermute | solution.py:90
  13.6 6.3 %collective-permute-start.4 = (bf16[4,128,128]{2,1,0:T(8,128)(2,1)S(1)}, bf16[4,128,128]{2,1,0:T(8,128)(2,1)S(1)}, u32[]{:S(2)}, u32[]{:S(2)}) collective-permute-start(bf16[4,128,128]{2,1,0:T(8,128)(2,1)S(1)} %collective-permute-done.3.refs_3_.refs_5_), channel_id=1, source_target_pairs={{0,2},{1,3},{2,0},{3,1},{4,6},{5,7},{6,4},{7,5},{8,10},{9,11},{10,... | collective-permute-start | bytes 393224 | tf_op jit(solution)/shard_map/ppermute | solution.py:90
  16.6 5.3 %collective-permute-start.6 = (bf16[4,128,128]{2,1,0:T(8,128)(2,1)S(1)}, bf16[4,128,128]{2,1,0:T(8,128)(2,1)S(1)}, u32[]{:S(2)}, u32[]{:S(2)}) collective-permute-start(bf16[4,128,128]{2,1,0:T(8,128)(2,1)S(1)} %collective-permute-done.5.refs_0_.refs_7_), channel_id=1, source_target_pairs={{0,2},{1,3},{2,0},{3,1},{4,6},{5,7},{6,4},{7,5},{8,10},{9,11},{10,... | collective-permute-start | bytes 393224 | tf_op jit(solution)/shard_map/ppermute | solution.py:90
  19.9 2.1 %collective-permute-start.8 = (bf16[8,128,128]{2,1,0:T(8,128)(2,1)S(1)}, bf16[8,128,128]{2,1,0:T(8,128)(2,1)S(1)}, u32[]{:S(2)}, u32[]{:S(2)}) collective-permute-start(bf16[8,128,128]{2,1,0:T(8,128)(2,1)S(1)} %pack.7), channel_id=1, source_target_pairs={{0,1},{1,0},{2,3},{3,2},{4,5},{5,4},{6,7},{7,6},{8,9},{9,8},{10,11... | collective-permute-start | bytes 786440 | tf_op jit(solution)/shard_map/ppermute | solution.py:90
  22.0 1.6 %collective-permute-start.9 = (bf16[8,128,128]{2,1,0:T(8,128)(2,1)S(1)}, bf16[8,128,128]{2,1,0:T(8,128)(2,1)S(1)}, u32[]{:S(2)}, u32[]{:S(2)}) collective-permute-start(bf16[8,128,128]{2,1,0:T(8,128)(2,1)S(1)} %pack.8), channel_id=1, source_target_pairs={{0,1},{1,0},{2,3},{3,2},{4,5},{5,4},{6,7},{7,6},{8,9},{9,8},{10,11... | collective-permute-start | bytes 786440 | tf_op jit(solution)/shard_map/ppermute | solution.py:90
  25.8 9.4 %collective-permute-start.13 = (bf16[4,128,128]{2,1,0:T(8,128)(2,1)S(1)}, bf16[4,128,128]{2,1,0:T(8,128)(2,1)S(1)}, u32[]{:S(2)}, u32[]{:S(2)}) collective-permute-start(bf16[4,128,128]{2,1,0:T(8,128)(2,1)S(1)} %get-tuple-element.27.refs_0_.refs_1_), channel_id=1, source_target_pairs={{0,8},{1,9},{2,10},{3,11},{4,12},{5,13},{6,14},{7,15},{8,0},{9,1},... | collective-permute-start | bytes 393224 | tf_op jit(solution)/shard_map/ppermute | solution.py:90
  28.5 7.4 %collective-permute-start.10 = (bf16[4,128,128]{2,1,0:T(8,128)(2,1)S(1)}, bf16[4,128,128]{2,1,0:T(8,128)(2,1)S(1)}, u32[]{:S(2)}, u32[]{:S(2)}) collective-permute-start(bf16[4,128,128]{2,1,0:T(8,128)(2,1)S(1)} %get-tuple-element.27.refs_0_.refs_1_), channel_id=1, source_target_pairs={{0,2},{1,3},{2,0},{3,1},{4,6},{5,7},{6,4},{7,5},{8,10},{9,11},{10,... | collective-permute-start | bytes 393224 | tf_op jit(solution)/shard_map/ppermute | solution.py:90
  29.8 6.6 %collective-permute-start.11 = (bf16[4,128,128]{2,1,0:T(8,128)(2,1)S(1)}, bf16[4,128,128]{2,1,0:T(8,128)(2,1)S(1)}, u32[]{:S(2)}, u32[]{:S(2)}) collective-permute-start(bf16[4,128,128]{2,1,0:T(8,128)(2,1)S(1)} %get-tuple-element.27.refs_0_.refs_1_), channel_id=1, source_target_pairs={{0,4},{1,5},{2,6},{3,7},{4,0},{5,1},{6,2},{7,3},{8,12},{9,13},{10,... | collective-permute-start | bytes 393224 | tf_op jit(solution)/shard_map/ppermute | solution.py:90
  32.1 1.3 %collective-permute-start.14 = (f32[64,256]{1,0:T(8,128)S(1)}, f32[64,256]{1,0:T(8,128)S(1)}, u32[]{:S(2)}, u32[]{:S(2)}) collective-permute-start(f32[64,256]{1,0:T(8,128)S(1)} %get-tuple-element.29), channel_id=1, source_target_pairs={{0,1},{1,0},{2,3},{3,2},{4,5},{5,4},{6,7},{7,6},{8,9},{9,8},{10,11... | collective-permute-start | bytes 196616 | tf_op jit(solution)/shard_map/ppermute | solution.py:90
  33.4 4.3 %collective-permute-start.15 = (f32[64,256]{1,0:T(8,128)S(1)}, f32[64,256]{1,0:T(8,128)S(1)}, u32[]{:S(2)}, u32[]{:S(2)}) collective-permute-start(f32[64,256]{1,0:T(8,128)S(1)} %add.12), channel_id=1, source_target_pairs={{0,2},{1,3},{2,0},{3,1},{4,6},{5,7},{6,4},{7,5},{8,10},{9,11},{10,... | collective-permute-start | bytes 196616 | tf_op jit(solution)/shard_map/ppermute | solution.py:90
  35.3 8.5 %collective-permute-start.17 = (bf16[4,128,128]{2,1,0:T(8,128)(2,1)S(1)}, bf16[4,128,128]{2,1,0:T(8,128)(2,1)S(1)}, u32[]{:S(2)}, u32[]{:S(2)}) collective-permute-start(bf16[4,128,128]{2,1,0:T(8,128)(2,1)S(1)} %collective-permute-done.13.refs_3_.refs_5_), channel_id=1, source_target_pairs={{0,4},{1,5},{2,6},{3,7},{4,0},{5,1},{6,2},{7,3},{8,12},{9,13},{10,... | collective-permute-start | bytes 393224 | tf_op jit(solution)/shard_map/ppermute | solution.py:90
  36.5 14.0 %collective-permute-start.20 = (bf16[16,128,128]{2,1,0:T(8,128)(2,1)S(1)}, bf16[16,128,128]{2,1,0:T(8,128)(2,1)S(1)}, u32[]{:S(2)}, u32[]{:S(2)}) collective-permute-start(bf16[16,128,128]{2,1,0:T(8,128)(2,1)S(1)} %pack.9), channel_id=1, source_target_pairs={{0,1},{1,0},{2,3},{3,2},{4,5},{5,4},{6,7},{7,6},{8,9},{9,8},{10,11... | collective-permute-start | bytes 1572872 | tf_op jit(solution)/shard_map/ppermute | solution.py:90
  37.7 6.0 %collective-permute-start.18 = (f32[64,256]{1,0:T(8,128)S(1)}, f32[64,256]{1,0:T(8,128)S(1)}, u32[]{:S(2)}, u32[]{:S(2)}) collective-permute-start(f32[64,256]{1,0:T(8,128)S(1)} %add.13), channel_id=1, source_target_pairs={{0,8},{1,9},{2,10},{3,11},{4,12},{5,13},{6,14},{7,15},{8,0},{9,1},... | collective-permute-start | bytes 196616 | tf_op jit(solution)/shard_map/ppermute | solution.py:90
  39.6 6.9 %collective-permute-start.12 = (bf16[4,128,128]{2,1,0:T(8,128)(2,1)S(1)}, bf16[4,128,128]{2,1,0:T(8,128)(2,1)S(1)}, u32[]{:S(2)}, u32[]{:S(2)}) collective-permute-start(bf16[4,128,128]{2,1,0:T(8,128)(2,1)S(1)} %collective-permute-done.10.refs_1_.refs_2_), channel_id=1, source_target_pairs={{0,4},{1,5},{2,6},{3,7},{4,0},{5,1},{6,2},{7,3},{8,12},{9,13},{10,... | collective-permute-start | bytes 393224 | tf_op jit(solution)/shard_map/ppermute | solution.py:90
  40.5 6.4 %collective-permute-start.16 = (bf16[4,128,128]{2,1,0:T(8,128)(2,1)S(1)}, bf16[4,128,128]{2,1,0:T(8,128)(2,1)S(1)}, u32[]{:S(2)}, u32[]{:S(2)}) collective-permute-start(bf16[4,128,128]{2,1,0:T(8,128)(2,1)S(1)} %collective-permute-done.13.refs_3_.refs_5_), channel_id=1, source_target_pairs={{0,2},{1,3},{2,0},{3,1},{4,6},{5,7},{6,4},{7,5},{8,10},{9,11},{10,... | collective-permute-start | bytes 393224 | tf_op jit(solution)/shard_map/ppermute | solution.py:90
  43.7 5.0 %collective-permute-start.19 = (bf16[4,128,128]{2,1,0:T(8,128)(2,1)S(1)}, bf16[4,128,128]{2,1,0:T(8,128)(2,1)S(1)}, u32[]{:S(2)}, u32[]{:S(2)}) collective-permute-start(bf16[4,128,128]{2,1,0:T(8,128)(2,1)S(1)} %collective-permute-done.17.refs_0_.refs_7_), channel_id=1, source_target_pairs={{0,2},{1,3},{2,0},{3,1},{4,6},{5,7},{6,4},{7,5},{8,10},{9,11},{10,... | collective-permute-start | bytes 393224 | tf_op jit(solution)/shard_map/ppermute | solution.py:90
  44.2 4.4 %collective-permute-start.22 = (f32[64,256]{1,0:T(8,128)S(1)}, f32[64,256]{1,0:T(8,128)S(1)}, u32[]{:S(2)}, u32[]{:S(2)}) collective-permute-start(f32[64,256]{1,0:T(8,128)S(1)} %add.14), channel_id=1, source_target_pairs={{0,4},{1,5},{2,6},{3,7},{4,0},{5,1},{6,2},{7,3},{8,12},{9,13},{10,... | collective-permute-start | bytes 196616 | tf_op jit(solution)/shard_map/ppermute | solution.py:90
  46.8 3.6 %collective-permute-start.21 = (bf16[8,128,128]{2,1,0:T(8,128)(2,1)S(1)}, bf16[8,128,128]{2,1,0:T(8,128)(2,1)S(1)}, u32[]{:S(2)}, u32[]{:S(2)}) collective-permute-start(bf16[8,128,128]{2,1,0:T(8,128)(2,1)S(1)} %pack.10), channel_id=1, source_target_pairs={{0,1},{1,0},{2,3},{3,2},{4,5},{5,4},{6,7},{7,6},{8,9},{9,8},{10,11... | collective-permute-start | bytes 786440 | tf_op jit(solution)/shard_map/ppermute | solution.py:90
  48.8 1.7 %collective-permute-start.23 = (bf16[8,128,128]{2,1,0:T(8,128)(2,1)S(1)}, bf16[8,128,128]{2,1,0:T(8,128)(2,1)S(1)}, u32[]{:S(2)}, u32[]{:S(2)}) collective-permute-start(bf16[8,128,128]{2,1,0:T(8,128)(2,1)S(1)} %pack.11), channel_id=1, source_target_pairs={{0,1},{1,0},{2,3},{3,2},{4,5},{5,4},{6,7},{7,6},{8,9},{9,8},{10,11... | collective-permute-start | bytes 786440 | tf_op jit(solution)/shard_map/ppermute | solution.py:90
  48.9 1.6 %collective-permute-start.24 = (f32[64,256]{1,0:T(8,128)S(1)}, f32[64,256]{1,0:T(8,128)S(1)}, u32[]{:S(2)}, u32[]{:S(2)}) collective-permute-start(f32[64,256]{1,0:T(8,128)S(1)} %add.15.refs_13_), channel_id=1, source_target_pairs={{0,1},{1,0},{2,3},{3,2},{4,5},{5,4},{6,7},{7,6},{8,9},{9,8},{10,11... | collective-permute-start | bytes 196616 | tf_op jit(solution)/shard_map/ppermute | solution.py:90
